TPU v7x, 32 devices: a whole 2x2x4 slice. The times are simulated.
32 devices in a mesh: bins: 2 (over x), fsdp: 16 (over z, y, core).
Axes of the slice: x: 2, y: 2, z: 4, core: 2. Of those that a mesh axis runs over, the one named last changes fastest.
Arguments:
- tokens: bfloat16 [16384, 1152], P(('bins', 'fsdp')), may hold values from -6 to 6
- condition: float32 [2, 1152], P('bins'), may hold values from -6 to 6
- segments: int32 [16384], P('bins'), may hold values from 0 to 63, as said below
- cotangent: bfloat16 [16384, 1152], P(('bins', 'fsdp')), may hold values from -6 to 6
- target: bfloat16 [16384, 768], P(('bins', 'fsdp')), may hold values from -6 to 6
- w_ada: bfloat16 [1152, 6912], P(None, 'fsdp'), may hold values from -0.1875 to 0.1875
- w_qkv: bfloat16 [1152, 3456], P('fsdp'), may hold values from -0.1875 to 0.1875
- w_out: bfloat16 [1152, 1152], P('fsdp'), may hold values from -0.75 to 0.75
- w_fc1: bfloat16 [1152, 4608], P('fsdp'), may hold values from -0.1875 to 0.1875
- w_fc2: bfloat16 [4608, 1152], P('fsdp'), may hold values from -0.09375 to 0.09375
- w_proj1: bfloat16 [1152, 2048], P('fsdp'), may hold values from -0.1875 to 0.1875
- w_proj2: bfloat16 [2048, 2048], P('fsdp'), may hold values from -0.125 to 0.125
- w_proj3: bfloat16 [2048, 768], P('fsdp'), may hold values from -0.125 to 0.125
Outputs:
- output: bfloat16 [16384, 1152], P(('bins', 'fsdp'))
- grad_tokens: float32 [16384, 1152], P(('bins', 'fsdp'))
- grad_condition: float32 [2, 1152], P('bins')
- grad_ada: float32 [1152, 6912], P(None, 'fsdp')
- grad_qkv: float32 [1152, 3456], P('fsdp')
- grad_out: float32 [1152, 1152], P('fsdp')
- grad_fc1: float32 [1152, 4608], P('fsdp')
- grad_fc2: float32 [4608, 1152], P('fsdp')
- grad_proj1: float32 [1152, 2048], P('fsdp')
- grad_proj2: float32 [2048, 2048], P('fsdp')
- grad_proj3: float32 [2048, 768], P('fsdp')
Inputs may be any that keep to these rules, and one draw needn't show every extreme that they name: segments never fall; each aligned block of 1024 tokens holds either one image of 1024 tokens or four images of 256 tokens; images of different blocks have different ids; the first block holds one image and the last block four.
All inputs are finite; a program needn't handle non-finite values.
Results may differ from a plain program's by a relative error of at most 0.015.
Values may be sent and summed in bfloat16 or wider, within the bound.
No kernel may reach another device: no remote copies, remote signals or barrier semaphores. Data moves between devices by JAX's collectives and lax.ppermute only.
A program may use at most 320 MiB of HBM per device.

v0:
```python
from functools import partial

import jax
import jax.numpy as jnp
from jax import lax
from jax.sharding import PartitionSpec as P

HEADS = 16


HIGH = lax.Precision.HIGHEST


def swapped(block, axis, apart):
    count = lax.axis_size(axis)
    route = []
    for low in range(count):
        high = low | 1 << apart
        if high != low and high < count:
            route += [(low, high), (high, low)]
    return lax.ppermute(block, axis, route)


def modulate(values, shift, scale):
    center = values - jnp.mean(values, axis=-1, keepdims=True)
    spread = jnp.mean(center * center, axis=-1, keepdims=True)
    return center * lax.rsqrt(spread + 1e-06) * (1.0 + scale) + shift


def cosine_sum(target_f, predicted):
    dots = jnp.sum(predicted * target_f, axis=-1)
    first = lax.rsqrt(jnp.sum(predicted * predicted, axis=-1) + 1e-06)
    second = lax.rsqrt(jnp.sum(target_f * target_f, axis=-1) + 1e-06)
    return jnp.sum(dots * first * second)


def product(left, right):
    return jnp.dot(left, right, preferred_element_type=jnp.float32)


def weight_grad(left, right):
    return jnp.einsum("nd,ne->de", left, right, preferred_element_type=jnp.float32)


def input_grad(grad, weight):
    return jnp.einsum("ne,de->nd", grad, weight, preferred_element_type=jnp.float32)


def shards(
    tokens,
    condition,
    segments,
    cotangent,
    target,
    w_ada,
    w_qkv,
    w_out,
    w_fc1,
    w_fc2,
    w_proj1,
    w_proj2,
    w_proj3,
):
    count = tokens.shape[0]
    width = tokens.shape[1]
    head_size = width // HEADS
    factor = head_size ** (-0.5)
    tokens_f = tokens.astype(jnp.float32)
    target_f = target.astype(jnp.float32)
    silu_cond, silu_back = jax.vjp(jax.nn.silu, condition)
    cond_low = silu_cond.astype(jnp.bfloat16)
    mod_cols = product(cond_low, w_ada)
    modulation = lax.all_gather(mod_cols, "fsdp", axis=1, tiled=True).reshape(6, width)
    block_set = (
        lax.all_gather(w_qkv, "fsdp", axis=0, tiled=True),
        lax.all_gather(w_out, "fsdp", axis=0, tiled=True),
        lax.all_gather(w_fc1, "fsdp", axis=0, tiled=True),
        lax.all_gather(w_fc2, "fsdp", axis=0, tiled=True),
    )
    head_set = (
        lax.all_gather(w_proj1, "fsdp", axis=0, tiled=True),
        lax.all_gather(w_proj2, "fsdp", axis=0, tiled=True),
        lax.all_gather(w_proj3, "fsdp", axis=0, tiled=True),
    )
    full_qkv, full_out, full_fc1, full_fc2 = block_set
    head_first, head_second, head_third = head_set
    h_one, norm_one_back = jax.vjp(modulate, tokens_f, modulation[0], modulation[1])
    in_one = h_one.astype(jnp.bfloat16)
    qkv_low = product(in_one, full_qkv).astype(jnp.bfloat16).reshape(count, 3, HEADS, head_size)
    queries = qkv_low[:, 0]
    pair_own = jnp.stack([qkv_low[:, 1], qkv_low[:, 2]])
    pair_peer = swapped(pair_own, "fsdp", 0)
    keys_all = jnp.concatenate([pair_own[0], pair_peer[0]], axis=0)
    values_all = jnp.concatenate([pair_own[1], pair_peer[1]], axis=0)
    place = lax.axis_index("fsdp")
    own_ids = lax.dynamic_slice_in_dim(segments, place * count, count)
    peer_ids = lax.dynamic_slice_in_dim(segments, jnp.bitwise_xor(place, 1) * count, count)
    same = own_ids[:, None] == jnp.concatenate([own_ids, peer_ids])[None, :]
    raw = jnp.einsum("qhd,khd->hqk", queries, keys_all, preferred_element_type=jnp.float32) * factor
    masked = jnp.where(same[None], raw, -1e30)
    highest = jnp.max(masked, axis=-1, keepdims=True)
    expo = jnp.exp(masked - highest)
    totals = jnp.sum(expo, axis=-1, keepdims=True)
    log_total = highest + jnp.log(totals)
    probs_low = (expo / totals).astype(jnp.bfloat16)
    attended = jnp.einsum("hqk,khd->qhd", probs_low, values_all, preferred_element_type=jnp.float32)
    attended = attended.astype(jnp.bfloat16).reshape(count, width)
    branch_one = product(attended, full_out)
    resid_one = tokens_f + modulation[2] * branch_one
    h_two, norm_two_back = jax.vjp(modulate, resid_one, modulation[3], modulation[4])
    in_two = h_two.astype(jnp.bfloat16)
    hidden_pre = product(in_two, full_fc1)
    hidden_act, gelu_back = jax.vjp(partial(jax.nn.gelu, approximate=True), hidden_pre)
    hidden_low = hidden_act.astype(jnp.bfloat16)
    branch_two = product(hidden_low, full_fc2)
    result = resid_one + modulation[5] * branch_two
    result_low = result.astype(jnp.bfloat16)
    first_act, first_back = jax.vjp(jax.nn.silu, product(result_low, head_first))
    first_low = first_act.astype(jnp.bfloat16)
    second_act, second_back = jax.vjp(jax.nn.silu, product(first_low, head_second))
    second_low = second_act.astype(jnp.bfloat16)
    predicted = product(second_low, head_third)
    cos_total, cos_back = jax.vjp(partial(cosine_sum, target_f), predicted)
    block_set = (
        lax.all_gather(w_qkv, "fsdp", axis=0, tiled=True),
        lax.all_gather(w_out, "fsdp", axis=0, tiled=True),
        lax.all_gather(w_fc1, "fsdp", axis=0, tiled=True),
        lax.all_gather(w_fc2, "fsdp", axis=0, tiled=True),
    )
    full_qkv, full_out, full_fc1, full_fc2 = block_set
    (grad_pred,) = cos_back(jnp.float32(-1.0))
    grad_pred_low = grad_pred.astype(jnp.bfloat16)
    grad_third = weight_grad(second_low, grad_pred_low)
    (grad_second_pre,) = second_back(input_grad(grad_pred_low, head_third))
    grad_second_low = grad_second_pre.astype(jnp.bfloat16)
    grad_second = weight_grad(first_low, grad_second_low)
    (grad_first_pre,) = first_back(input_grad(grad_second_low, head_second))
    grad_first_low = grad_first_pre.astype(jnp.bfloat16)
    grad_first = weight_grad(result_low, grad_first_low)
    head_sums = (
        lax.psum_scatter(grad_first, "fsdp", scatter_dimension=0, tiled=True),
        lax.psum_scatter(grad_second, "fsdp", scatter_dimension=0, tiled=True),
        lax.psum_scatter(grad_third, "fsdp", scatter_dimension=0, tiled=True),
    )
    d_result = cotangent.astype(jnp.float32) + input_grad(grad_first_low, head_first)
    grad_gate_two = jnp.sum(d_result * branch_two, axis=0)
    d_branch_two = (d_result * modulation[5]).astype(jnp.bfloat16)
    grad_fc2_local = weight_grad(hidden_low, d_branch_two)
    (d_pre,) = gelu_back(input_grad(d_branch_two, full_fc2))
    d_pre_low = d_pre.astype(jnp.bfloat16)
    grad_fc1_local = weight_grad(in_two, d_pre_low)
    d_resid_part, grad_shift_two, grad_scale_two = norm_two_back(input_grad(d_pre_low, full_fc1))
    d_resid = d_result + d_resid_part
    grad_gate_one = jnp.sum(d_resid * branch_one, axis=0)
    d_branch_one = (d_resid * modulation[2]).astype(jnp.bfloat16)
    grad_out_local = weight_grad(attended, d_branch_one)
    d_attended = (
        input_grad(d_branch_one, full_out).astype(jnp.bfloat16).reshape(count, HEADS, head_size)
    )
    again_raw = (
        jnp.einsum("qhd,khd->hqk", queries, keys_all, preferred_element_type=jnp.float32) * factor
    )
    probs = jnp.exp(jnp.where(same[None], again_raw, -1e30) - log_total)
    probs_again = probs.astype(jnp.bfloat16)
    d_probs = jnp.einsum("qhd,khd->hqk", d_attended, values_all, preferred_element_type=jnp.float32)
    centre = jnp.sum(d_probs * probs, axis=-1, keepdims=True)
    d_scores = (probs * (d_probs - centre)).astype(jnp.bfloat16)
    d_queries = (
        jnp.einsum("hqk,khd->qhd", d_scores, keys_all, preferred_element_type=jnp.float32) * factor
    )
    d_keys = (
        jnp.einsum("hqk,qhd->khd", d_scores, queries, preferred_element_type=jnp.float32) * factor
    )
    d_values = jnp.einsum(
        "hqk,qhd->khd", probs_again, d_attended, preferred_element_type=jnp.float32
    )
    from_peer = swapped(jnp.stack([d_keys[count:], d_values[count:]]), "fsdp", 0)
    keys_grad = d_keys[:count] + from_peer[0]
    values_grad = d_values[:count] + from_peer[1]
    d_qkv = (
        jnp.stack([d_queries, keys_grad, values_grad], axis=1)
        .reshape(count, 3 * width)
        .astype(jnp.bfloat16)
    )
    grad_qkv_local = weight_grad(in_one, d_qkv)
    d_tok_part, grad_shift_one, grad_scale_one = norm_one_back(input_grad(d_qkv, full_qkv))
    grad_tokens = d_resid + d_tok_part
    d_modulation = jnp.stack(
        [
            grad_shift_one,
            grad_scale_one,
            grad_gate_one,
            grad_shift_two,
            grad_scale_two,
            grad_gate_two,
        ]
    ).reshape(6 * width)
    block_sums = (
        lax.psum_scatter(grad_qkv_local, "fsdp", scatter_dimension=0, tiled=True),
        lax.psum_scatter(grad_out_local, "fsdp", scatter_dimension=0, tiled=True),
        lax.psum_scatter(grad_fc1_local, "fsdp", scatter_dimension=0, tiled=True),
        lax.psum_scatter(grad_fc2_local, "fsdp", scatter_dimension=0, tiled=True),
        lax.psum_scatter(d_modulation, "fsdp", scatter_dimension=0, tiled=True),
    )
    mod_grad_cols = block_sums[4].reshape(1, -1)
    summed = lax.psum(
        (
            block_sums[0],
            block_sums[1],
            block_sums[2],
            block_sums[3],
            head_sums[0],
            head_sums[1],
            head_sums[2],
        ),
        "bins",
    )
    cond_part = jnp.dot(mod_grad_cols, w_ada.astype(jnp.float32).T, precision=HIGH)
    cond_total = lax.psum(cond_part, "fsdp")
    (grad_condition,) = silu_back(cond_total)
    cond_low_f = cond_low.astype(jnp.float32)
    ada_local = jnp.dot(cond_low_f.T, mod_grad_cols, precision=HIGH)
    grad_ada = lax.psum(ada_local, "bins")
    return (
        result_low,
        grad_tokens,
        grad_condition,
        grad_ada,
        summed[0],
        summed[1],
        summed[2],
        summed[3],
        summed[4],
        summed[5],
        summed[6],
    )


def solution(mesh):
    placed = (
        P(("bins", "fsdp"), None),
        P("bins", None),
        P("bins"),
        P(("bins", "fsdp"), None),
        P(("bins", "fsdp"), None),
        P(None, "fsdp"),
        P("fsdp", None),
        P("fsdp", None),
        P("fsdp", None),
        P("fsdp", None),
        P("fsdp", None),
        P("fsdp", None),
        P("fsdp", None),
    )
    return jax.shard_map(
        shards,
        mesh=mesh,
        in_specs=placed,
        out_specs=(
            P(("bins", "fsdp"), None),
            P(("bins", "fsdp"), None),
            P("bins", None),
            P(None, "fsdp"),
            P("fsdp", None),
            P("fsdp", None),
            P("fsdp", None),
            P("fsdp", None),
            P("fsdp", None),
            P("fsdp", None),
            P("fsdp", None),
        ),
        check_vma=False,
    )
```

profile of v0, /device:TPU:0, one launch (start us, length us, event | category | flops | bytes accessed | tf_op | source)
XLA Modules:
  0.0 1830.2 jit_solution(13340199901718617089)
XLA Ops:
  14.0 64.6 %all-reduce = f32[6912]{0:T(1024)S(1)} all-reduce(f32[6912]{0:T(1024)S(1)} %dynamic-update-slice), channel_id=2, replica_groups=mesh['bins'=2,'fsdp'=16] {'fsdp'}, use_global_device_ids=true, to_apply=%add | all-reduce | flops 6912 | bytes 55296
  114.1 16.6 fusion.78
  130.7 14.7 fusion
  145.5 14.7 fusion.41
  167.6 51.8 %all-gather.13.cloned.1.call-done = bf16[1152,4608]{1,0:T(8,128)(2,1)} async-done(((bf16[72,4608]{1,0:T(8,128)(2,1)}), bf16[1152,4608]{1,0:T(8,128)(2,1)}) %all-gather.13.cloned.1.call-update) | async-done | bytes 10616848 | tf_op jit(solution)/shard_map/all_gather | solution.py:77
  219.4 13.9 fusion.70
  233.4 75.1 %all-gather.15.cloned.1.call-done = bf16[4608,1152]{1,0:T(8,128)(2,1)} async-done(((bf16[288,1152]{1,0:T(8,128)(2,1)}), bf16[4608,1152]{1,0:T(8,128)(2,1)}) %all-gather.15.cloned.1.call-update) | async-done | bytes 10616848 | tf_op jit(solution)/shard_map/all_gather | solution.py:78
  322.2 40.0 %all-gather.17.cloned.1.call-done = bf16[1152,2048]{1,0:T(8,128)(2,1)} async-done(((bf16[72,2048]{1,0:T(8,128)(2,1)}), bf16[1152,2048]{1,0:T(8,128)(2,1)}) %all-gather.17.cloned.1.call-update) | async-done | bytes 4718608 | tf_op jit(solution)/shard_map/all_gather | solution.py:81
  369.7 67.9 %all-gather.19.cloned.1.call-done = bf16[2048,2048]{1,0:T(8,128)(2,1)} async-done(((bf16[128,2048]{1,0:T(8,128)(2,1)}), bf16[2048,2048]{1,0:T(8,128)(2,1)}) %all-gather.19.cloned.1.call-update) | async-done | bytes 8388624 | tf_op jit(solution)/shard_map/all_gather | solution.py:82
  449.9 33.5 %all-gather.21.cloned.1.call-done = bf16[2048,768]{1,0:T(8,128)(2,1)} async-done(((bf16[128,768]{1,0:T(8,128)(2,1)}), bf16[2048,768]{1,0:T(8,128)(2,1)}) %all-gather.21.cloned.1.call-update) | async-done | bytes 3145744 | tf_op jit(solution)/shard_map/all_gather | solution.py:83
  508.3 17.1 fusion.12
  560.8 14.2 fusion.71
  582.9 13.9 fusion.34
  601.4 22.4 %multiply_reduce_fusion = (f32[16,512]{1,0:T(8,128)S(1)}, f32[16,512,1024]{2,1,0:T(8,128)}) fusion(f32[16,512,1024]{2,1,0:T(8,128)} %get-tuple-element.58, f32[16,512]{1,0:T(8,128)S(1)} %log_add_fusion, bf16[512,16,72]{0,2,1:T(8,128)(2,1)S(1)} %bitcast.106, bf16[512,16,72]{0,2,1:T(8,128)(2,1)S(1)} %copy-done.17, bf16[512,16,72]{0,2,1:T(8,128)(2,1)S(1)} %copy-done.16), kind=kOutput, calls=%fused_computation.1 | convolution fusion | flops 1237835776 | bytes 70713344 | tf_op jit(solution)/shard_map/qhd,khd->hqk/dot_general | solution.py:165
  623.7 30.4 %multiply_convert_fusion = bf16[16,512,1024]{2,1,0:T(8,128)(2,1)} fusion(f32[16,512,1024]{2,1,0:T(8,128)} %get-tuple-element.67, f32[16,512,1024]{2,1,0:T(8,128)} %get-tuple-element.58, f32[16,512]{1,0:T(8,128)S(1)} %get-tuple-element.66, f32[16,512]{1,0:T(8,128)S(1)} %log_add_fusion), kind=kLoop, calls=%fused_computation | loop fusion | flops 33554432 | bytes 83951616 | tf_op jit(solution)/shard_map/convert_element_type | solution.py:167
  694.4 14.9 fusion.46
  738.0 60.9 %all-reduce.1 = f32[6912]{0:T(1024)S(1)} all-reduce(f32[6912]{0:T(1024)S(1)} %reshape.171), channel_id=3, replica_groups=mesh['bins'=2,'fsdp'=16] {'fsdp'}, use_global_device_ids=true, to_apply=%region_20.21.clone | all-reduce | flops 6912 | bytes 55296
  800.5 27.4 %reduce-scatter.16.cloned.1.call-done = f32[72,2048]{1,0:T(8,128)} async-done(((f32[1152,2048]{1,0:T(8,128)}), f32[72,2048]{1,0:T(8,128)}) %reduce-scatter.16.cloned.1.call-update) | async-done | bytes 589840 | tf_op jit(solution)/shard_map/reduce_scatter | solution.py:141
  827.9 182.5 %reduce-scatter.18.cloned.1.call-done = f32[128,2048]{1,0:T(8,128)} async-done(((f32[2048,2048]{1,0:T(8,128)}), f32[128,2048]{1,0:T(8,128)}) %reduce-scatter.18.cloned.1.call-update) | async-done | bytes 1048592 | tf_op jit(solution)/shard_map/reduce_scatter | solution.py:142
  1010.4 174.9 %reduce-scatter.22.cloned.1.call-done = f32[72,3456]{1,0:T(8,128)} async-done(((f32[1152,3456]{1,0:T(8,128)}), f32[72,3456]{1,0:T(8,128)}) %reduce-scatter.22.cloned.1.call-update) | async-done | bytes 995344
  1185.3 216.2 %reduce-scatter.14.cloned.1.call-done = f32[288,1152]{1,0:T(8,128)} async-done(((f32[4608,1152]{1,0:T(8,128)}), f32[288,1152]{1,0:T(8,128)}) %reduce-scatter.14.cloned.1.call-update) | async-done | bytes 1327120 | tf_op jit(solution)/shard_map/reduce_scatter | solution.py:202
  1401.5 216.5 %reduce-scatter.12.cloned.1.call-done = f32[72,4608]{1,0:T(8,128)} async-done(((f32[1152,4608]{1,0:T(8,128)}), f32[72,4608]{1,0:T(8,128)}) %reduce-scatter.12.cloned.1.call-update) | async-done | bytes 1327120 | tf_op jit(solution)/shard_map/reduce_scatter | solution.py:201
  1618.6 32.0 %psum.63 = f32[1,1152]{1,0:T(1,128)S(1)} all-reduce(f32[1,1152]{1,0:T(1,128)S(1)} %fusion.80), channel_id=1, replica_groups=mesh['bins'=2,'fsdp'=16] {'fsdp'}, use_global_device_ids=true, to_apply=%region_21.22 | all-reduce | flops 1152 | bytes 9216 | tf_op jit(solution)/shard_map/psum | solution.py:219
  1655.9 158.0 %all-reduce.7.cloned.1.call-done = (f32[1152,432]{0,1:T(8,128)}, f32[72,3456]{1,0:T(8,128)}, f32[72,1152]{1,0:T(8,128)}, f32[72,4608]{1,0:T(8,128)}, f32[288,115...) async-done(((f32[1152,432]{0,1:T(8,128)}, f32[72,3456]{1,0:T(8,128)}, f32[72,1152]{1,0:T(8,128)}, f32[72,4608]{1,0:T(8,128)}, ...) | async-done | bytes 8003600 | tf_op jit(solution)/shard_map/psum | solution.py:223
  (263 shorter events, 239.7 us)
Async XLA Ops:
  7.2 71.5 %copy-start.1 = (bf16[512,1152]{1,0:T(8,128)(2,1)S(1)}, bf16[512,1152]{1,0:T(8,128)(2,1)}, u32[]{:S(2)}) copy-start(bf16[512,1152]{1,0:T(8,128)(2,1)} %param.13) | copy-start | bytes 3538948
  7.2 78.5 %all-gather.9.cloned.1.call-start = ((), (), s32[]{:S(2)}) async-start(), calls=%async_computation.7 | async-start | bytes 8460288 | tf_op jit(solution)/shard_map/all_gather | solution.py:75
  8.0 152.2 %all-gather.11.cloned.1.call-start = ((), (), s32[]{:S(2)}) async-start(), calls=%async_computation.8 | async-start | bytes 2820096 | tf_op jit(solution)/shard_map/all_gather | solution.py:76
  8.7 210.7 %all-gather.13.cloned.1.call-start = ((), (), s32[]{:S(2)}) async-start(), calls=%async_computation.9 | async-start | bytes 11280384 | tf_op jit(solution)/shard_map/all_gather | solution.py:77
  9.4 299.0 %all-gather.15.cloned.1.call-start = ((), (), s32[]{:S(2)}) async-start(), calls=%async_computation.10 | async-start | bytes 11280384 | tf_op jit(solution)/shard_map/all_gather | solution.py:78
  10.0 352.2 %all-gather.17.cloned.1.call-start = ((), (), s32[]{:S(2)}) async-start(), calls=%async_computation.11 | async-start | bytes 5013504 | tf_op jit(solution)/shard_map/all_gather | solution.py:81
  10.6 427.1 %all-gather.19.cloned.1.call-start = ((), (), s32[]{:S(2)}) async-start(), calls=%async_computation.12 | async-start | bytes 8912896 | tf_op jit(solution)/shard_map/all_gather | solution.py:82
  11.2 472.3 %all-gather.21.cloned.1.call-start = ((), (), s32[]{:S(2)}) async-start(), calls=%async_computation.13 | async-start | bytes 3342336 | tf_op jit(solution)/shard_map/all_gather | solution.py:83
  78.8 140.7 %copy-start.55 = (f32[1152]{0:T(1024)}, f32[1152]{0:T(1024)S(1)}, u32[]{:S(2)}) copy-start(f32[1152]{0:T(1024)S(1)} %get-tuple-element.21) | copy-start | bytes 13828
  78.8 429.5 %copy-start.57 = (f32[1152]{0:T(1024)}, f32[1152]{0:T(1024)S(1)}, u32[]{:S(2)}) copy-start(f32[1152]{0:T(1024)S(1)} %get-tuple-element.20) | copy-start | bytes 13828
  78.8 459.2 %copy-start.40 = (f32[1152]{0:T(1024)}, f32[1152]{0:T(1024)S(1)}, u32[]{:S(2)}) copy-start(f32[1152]{0:T(1024)S(1)} %get-tuple-element.22) | copy-start | bytes 13828
  106.3 4.9 collective-permute-start
  106.6 693.9 %reduce-scatter.24.cloned.1.call-start = ((), (), s32[]{:S(2)}) async-start(), calls=%async_computation.20 | async-start | bytes 5640192
  165.8 372.2 %copy-start.46 = (f32[512]{0:T(512)}, f32[512]{0:T(512)S(1)}, u32[]{:S(2)}) copy-start(f32[512]{0:T(512)S(1)} %broadcast_multiply_fusion.1) | copy-start | bytes 6148
  167.6 370.4 %copy-start.53 = (f32[512]{0:T(512)}, f32[512]{0:T(512)S(1)}, u32[]{:S(2)}) copy-start(f32[512]{0:T(512)S(1)} %fusion.59) | copy-start | bytes 6148
  219.4 89.0 %copy-start.4 = (f32[512,1152]{1,0:T(8,128)S(1)}, f32[512,1152]{1,0:T(8,128)}, u32[]{:S(2)}) copy-start(f32[512,1152]{1,0:T(8,128)} %copy-done.3) | copy-start | bytes 7077892
  545.7 254.7 %reduce-scatter.20.cloned.1.call-start = ((), (), s32[]{:S(2)}) async-start(), calls=%async_computation.18 | async-start | bytes 6684672 | tf_op jit(solution)/shard_map/reduce_scatter | solution.py:143
  552.0 275.9 %reduce-scatter.16.cloned.1.call-start = ((), (), s32[]{:S(2)}) async-start(), calls=%async_computation.16 | async-start | bytes 10027008 | tf_op jit(solution)/shard_map/reduce_scatter | solution.py:141
  560.7 449.7 %reduce-scatter.18.cloned.1.call-start = ((), (), s32[]{:S(2)}) async-start(), calls=%async_computation.17 | async-start | bytes 17825792 | tf_op jit(solution)/shard_map/reduce_scatter | solution.py:142
  575.0 610.3 %reduce-scatter.22.cloned.1.call-start = ((), (), s32[]{:S(2)}) async-start(), calls=%async_computation.19 | async-start | bytes 16920576
  668.7 10.7 collective-permute-start.1
  693.8 707.7 %reduce-scatter.14.cloned.1.call-start = ((), (), s32[]{:S(2)}) async-start(), calls=%async_computation.15 | async-start | bytes 22560768 | tf_op jit(solution)/shard_map/reduce_scatter | solution.py:202
  709.3 908.7 %reduce-scatter.12.cloned.1.call-start = ((), (), s32[]{:S(2)}) async-start(), calls=%async_computation.14 | async-start | bytes 22560768 | tf_op jit(solution)/shard_map/reduce_scatter | solution.py:201
  723.1 1090.9 %all-reduce.7.cloned.1.call-start = ((), (), s32[]{:S(2)}) async-start(), calls=%async_computation.21 | async-start | bytes 16007168 | tf_op jit(solution)/shard_map/psum | solution.py:223
  (65 other events, 466.7 us)
Sparse Core Ops, SparseCore 0:
  10.2 75.4 all-gather.8
  87.9 41.8 all-gather.10
  132.0 87.3 all-gather.12
  221.6 86.8 all-gather.14
  310.6 51.5 all-gather.16
  364.2 73.4 all-gather.18
  440.0 43.4 all-gather.20
  545.9 78.2 reduce-scatter.23
  628.2 84.2 reduce-scatter.19
  717.0 110.9 reduce-scatter.15
  832.0 178.3 reduce-scatter.17
  1014.4 170.8 reduce-scatter.21
  1189.4 212.0 reduce-scatter.13
  1406.0 211.9 reduce-scatter.11
  1621.5 192.4 all-reduce.6
where the time goes:
time: 1840 us; the launch traced here: 1830 us
  waiting for transfers between devices  1260 us (68%)
  matrix products  289 us (16%)
  blocking collectives  158 us (9%)
  other arithmetic  66 us (4%)
  local copies, waits for them, and re-layouts  42.3 us (2%)
    reduce_scatter x1, waiting for transfers between devices, shards(): lax.psum_scatter(grad_fc1_local, 'fsdp', scatter_dimension=0, tiled=True)  217 us
    reduce_scatter x1, waiting for transfers between devices, shards(): lax.psum_scatter(grad_fc2_local, 'fsdp', scatter_dimension=0, tiled=True)  216 us
    reduce_scatter x1, waiting for transfers between devices, shards(): lax.psum_scatter(grad_second, 'fsdp', scatter_dimension=0, tiled=True)  182 us
    unnamed x17, waiting for transfers between devices  179 us
    psum x1, waiting for transfers between devices, shards(): grad_ada = lax.psum(ada_local, 'bins')  158 us
    unnamed x2, blocking collectives  126 us
    all_gather x1, waiting for transfers between devices, shards(): lax.all_gather(w_fc2, 'fsdp', axis=0, tiled=True)  75.1 us
    dot_general x7, matrix products, weight_grad(): jnp.einsum('nd,ne->de', left, right, preferred_element_type=jnp.float32)  69.7 us
  transfers between devices with their start and end apart: 17, of which 13 were waited for; matrix products, arithmetic and copies ran while one was open for 17% of the time, Pallas kernels for 0%

commit v1 on v0

--- a/solution.py
+++ b/solution.py
@@ -21,6 +21,115 @@
     return lax.ppermute(block, axis, route)
 
 
+def bins_peer(block):
+    return lax.ppermute(block, "bins", [(0, 1), (1, 0)])
+
+
+def hop(block, apart):
+    chips = lax.axis_size("fsdp") // 2
+    route = [2 * chip for chip in range(chips // 2)]
+    route = route + [chip + 1 for chip in reversed(route)]
+    pairs = []
+    for spot, chip in enumerate(route):
+        onward = route[(spot + apart) % chips]
+        pairs += [(2 * chip, 2 * onward), (2 * chip + 1, 2 * onward + 1)]
+    return lax.ppermute(block, "fsdp", pairs)
+
+
+def chip_at(apart):
+    chips = lax.axis_size("fsdp") // 2
+    chip = lax.axis_index("fsdp") // 2
+    spot = jnp.where(chip % 2 == 0, chip // 2, chips - 1 - chip // 2)
+    spot = (spot + apart) % chips
+    return jnp.where(spot < chips // 2, 2 * spot, 2 * (chips - 1 - spot) + 1)
+
+
+def doubled(block):
+    count, place = lax.axis_size("fsdp"), lax.axis_index("fsdp")
+    step = 0
+    while 1 << step < count:
+        other = swapped(block, "fsdp", step)
+        upper = (place >> step) % 2 == 1
+        block = jnp.where(
+            upper, jnp.concatenate([other, block]), jnp.concatenate([block, other])
+        )
+        step += 1
+    return block
+
+
+def halved(block):
+    count, place = lax.axis_size("fsdp"), lax.axis_index("fsdp")
+    step = count.bit_length() - 1
+    while step:
+        step -= 1
+        upper = (place >> step) % 2
+        length = block.shape[0] // 2
+        sent = lax.dynamic_slice_in_dim(block, (1 - upper) * length, length)
+        kept = lax.dynamic_slice_in_dim(block, upper * length, length)
+        block = kept + swapped(sent, "fsdp", step)
+    return block
+
+
+def group_sum(block):
+    step = 0
+    while 1 << step < lax.axis_size("fsdp"):
+        block = block + swapped(block, "fsdp", step)
+        step += 1
+    return block
+
+
+def core_rows(turned, core):
+    chips = lax.axis_size("fsdp") // 2
+    split = turned.reshape(chips, 2, -1, turned.shape[-1])
+    picked = lax.dynamic_index_in_dim(split, core, 1, keepdims=False)
+    return picked.reshape(-1, turned.shape[-1])
+
+
+def chip_grad(left, right):
+    core = lax.axis_index("fsdp") % 2
+    turned = left.T
+    mine = core_rows(turned, core)
+    theirs = swapped(core_rows(turned, 1 - core), "fsdp", 0)
+    rows = jnp.concatenate([mine, theirs], axis=1)
+    grads = jnp.concatenate([right, swapped(right, "fsdp", 0)], axis=0)
+    total = jnp.dot(rows, grads, preferred_element_type=jnp.float32)
+    return total.reshape(lax.axis_size("fsdp") // 2, -1, right.shape[1])
+
+
+def ring_sum(parts):
+    chips, rows = parts.shape[:2]
+    far = chips // 2
+    cut = (rows // 2 + 7) // 8 * 8
+
+    def part(apart):
+        return lax.dynamic_index_in_dim(parts, chip_at(apart), 0, keepdims=False)
+
+    def low(block):
+        return block.astype(jnp.bfloat16)
+
+    last = part(far)
+    onward = hop(low(last[:cut]), 1)
+    back = hop(low(last[cut:]), -1)
+    for apart in range(far - 1, 0, -1):
+        ahead, behind = part(apart), part(-apart)
+        if apart == far - 1:
+            ahead = jnp.concatenate([ahead[:cut] + onward, ahead[cut:]])
+            behind = jnp.concatenate([behind[:cut], behind[cut:] + back])
+        else:
+            ahead, behind = ahead + onward, behind + back
+        onward, back = hop(low(ahead), 1), hop(low(behind), -1)
+    return part(0) + onward + back
+
+
+def both_groups(block):
+    rounded = lax.reduce_precision(block, 8, 7)
+    return rounded + bins_peer(rounded.astype(jnp.bfloat16)).astype(jnp.float32)
+
+
+def full_grad(left, right):
+    return both_groups(ring_sum(chip_grad(left, right)))
+
+
 def modulate(values, shift, scale):
     center = values - jnp.mean(values, axis=-1, keepdims=True)
     spread = jnp.mean(center * center, axis=-1, keepdims=True)
@@ -36,10 +145,6 @@
 
 def product(left, right):
     return jnp.dot(left, right, preferred_element_type=jnp.float32)
-
-
-def weight_grad(left, right):
-    return jnp.einsum("nd,ne->de", left, right, preferred_element_type=jnp.float32)
 
 
 def input_grad(grad, weight):
@@ -70,7 +175,7 @@
     silu_cond, silu_back = jax.vjp(jax.nn.silu, condition)
     cond_low = silu_cond.astype(jnp.bfloat16)
     mod_cols = product(cond_low, w_ada)
-    modulation = lax.all_gather(mod_cols, "fsdp", axis=1, tiled=True).reshape(6, width)
+    modulation = doubled(mod_cols.reshape(-1)).reshape(6, width)
     block_set = (
         lax.all_gather(w_qkv, "fsdp", axis=0, tiled=True),
         lax.all_gather(w_out, "fsdp", axis=0, tiled=True),
@@ -121,39 +226,27 @@
     second_low = second_act.astype(jnp.bfloat16)
     predicted = product(second_low, head_third)
     cos_total, cos_back = jax.vjp(partial(cosine_sum, target_f), predicted)
-    block_set = (
-        lax.all_gather(w_qkv, "fsdp", axis=0, tiled=True),
-        lax.all_gather(w_out, "fsdp", axis=0, tiled=True),
-        lax.all_gather(w_fc1, "fsdp", axis=0, tiled=True),
-        lax.all_gather(w_fc2, "fsdp", axis=0, tiled=True),
-    )
-    full_qkv, full_out, full_fc1, full_fc2 = block_set
     (grad_pred,) = cos_back(jnp.float32(-1.0))
     grad_pred_low = grad_pred.astype(jnp.bfloat16)
-    grad_third = weight_grad(second_low, grad_pred_low)
+    grad_third = full_grad(second_low, grad_pred_low)
     (grad_second_pre,) = second_back(input_grad(grad_pred_low, head_third))
     grad_second_low = grad_second_pre.astype(jnp.bfloat16)
-    grad_second = weight_grad(first_low, grad_second_low)
+    grad_second = full_grad(first_low, grad_second_low)
     (grad_first_pre,) = first_back(input_grad(grad_second_low, head_second))
     grad_first_low = grad_first_pre.astype(jnp.bfloat16)
-    grad_first = weight_grad(result_low, grad_first_low)
-    head_sums = (
-        lax.psum_scatter(grad_first, "fsdp", scatter_dimension=0, tiled=True),
-        lax.psum_scatter(grad_second, "fsdp", scatter_dimension=0, tiled=True),
-        lax.psum_scatter(grad_third, "fsdp", scatter_dimension=0, tiled=True),
-    )
+    grad_first = full_grad(result_low, grad_first_low)
     d_result = cotangent.astype(jnp.float32) + input_grad(grad_first_low, head_first)
     grad_gate_two = jnp.sum(d_result * branch_two, axis=0)
     d_branch_two = (d_result * modulation[5]).astype(jnp.bfloat16)
-    grad_fc2_local = weight_grad(hidden_low, d_branch_two)
+    grad_fc2 = full_grad(hidden_low, d_branch_two)
     (d_pre,) = gelu_back(input_grad(d_branch_two, full_fc2))
     d_pre_low = d_pre.astype(jnp.bfloat16)
-    grad_fc1_local = weight_grad(in_two, d_pre_low)
+    grad_fc1 = full_grad(in_two, d_pre_low)
     d_resid_part, grad_shift_two, grad_scale_two = norm_two_back(input_grad(d_pre_low, full_fc1))
     d_resid = d_result + d_resid_part
     grad_gate_one = jnp.sum(d_resid * branch_one, axis=0)
     d_branch_one = (d_resid * modulation[2]).astype(jnp.bfloat16)
-    grad_out_local = weight_grad(attended, d_branch_one)
+    grad_out = full_grad(attended, d_branch_one)
     d_attended = (
         input_grad(d_branch_one, full_out).astype(jnp.bfloat16).reshape(count, HEADS, head_size)
     )
@@ -182,7 +275,7 @@
         .reshape(count, 3 * width)
         .astype(jnp.bfloat16)
     )
-    grad_qkv_local = weight_grad(in_one, d_qkv)
+    grad_qkv = full_grad(in_one, d_qkv)
     d_tok_part, grad_shift_one, grad_scale_one = norm_one_back(input_grad(d_qkv, full_qkv))
     grad_tokens = d_resid + d_tok_part
     d_modulation = jnp.stack(
@@ -195,44 +288,29 @@
             grad_gate_two,
         ]
     ).reshape(6 * width)
-    block_sums = (
-        lax.psum_scatter(grad_qkv_local, "fsdp", scatter_dimension=0, tiled=True),
-        lax.psum_scatter(grad_out_local, "fsdp", scatter_dimension=0, tiled=True),
-        lax.psum_scatter(grad_fc1_local, "fsdp", scatter_dimension=0, tiled=True),
-        lax.psum_scatter(grad_fc2_local, "fsdp", scatter_dimension=0, tiled=True),
-        lax.psum_scatter(d_modulation, "fsdp", scatter_dimension=0, tiled=True),
-    )
-    mod_grad_cols = block_sums[4].reshape(1, -1)
-    summed = lax.psum(
-        (
-            block_sums[0],
-            block_sums[1],
-            block_sums[2],
-            block_sums[3],
-            head_sums[0],
-            head_sums[1],
-            head_sums[2],
-        ),
-        "bins",
-    )
+    mod_grad_cols = halved(d_modulation).reshape(1, -1)
     cond_part = jnp.dot(mod_grad_cols, w_ada.astype(jnp.float32).T, precision=HIGH)
-    cond_total = lax.psum(cond_part, "fsdp")
-    (grad_condition,) = silu_back(cond_total)
+    (grad_condition,) = silu_back(group_sum(cond_part))
+    group = lax.axis_index("bins")
     cond_low_f = cond_low.astype(jnp.float32)
-    ada_local = jnp.dot(cond_low_f.T, mod_grad_cols, precision=HIGH)
-    grad_ada = lax.psum(ada_local, "bins")
+    other_cond, other_cols = bins_peer(cond_low_f), bins_peer(mod_grad_cols)
+    first_cond = jnp.where(group == 0, cond_low_f, other_cond)
+    last_cond = jnp.where(group == 0, other_cond, cond_low_f)
+    first_cols = jnp.where(group == 0, mod_grad_cols, other_cols)
+    last_cols = jnp.where(group == 0, other_cols, mod_grad_cols)
+    grad_ada = first_cond.T * first_cols + last_cond.T * last_cols
     return (
         result_low,
         grad_tokens,
         grad_condition,
         grad_ada,
-        summed[0],
-        summed[1],
-        summed[2],
-        summed[3],
-        summed[4],
-        summed[5],
-        summed[6],
+        grad_qkv,
+        grad_out,
+        grad_fc1,
+        grad_fc2,
+        grad_first,
+        grad_second,
+        grad_third,
     )
 
 

time: 1840 us -> 1130 us (0.61)
  waiting for transfers between devices: 1260 us -> 565 us
  blocking collectives: 158 us -> 0 us
  starting transfers between devices: 1.59 us -> 88.8 us
  local copies, waits for them, and re-layouts: 42.3 us -> 92.7 us
  other arithmetic: 66 us -> 92.5 us
  matrix products: 289 us -> 266 us
    reduce_scatter x5 -> x0, waiting for transfers between devices: 643 us -> none  [the longest x1 217 us: shards(): lax.psum_scatter(grad_fc1_local, 'fsdp', scatter_dimension=0, tiled=True)]
    ppermute x0 -> x65, waiting for transfers between devices: none -> 217 us  [the longest x56 197 us: hop(): return lax.ppermute(block, 'fsdp', pairs)]
    unnamed x17 -> x7, waiting for transfers between devices: 179 us -> 3.65 us
    psum x1 -> x0, waiting for transfers between devices: 158 us -> none  [shards(): grad_ada = lax.psum(ada_local, 'bins')]
    unnamed x2 -> x0, blocking collectives: 126 us -> none
    ppermute x0 -> x65, starting transfers between devices: none -> 72.7 us  [the longest x56 57.3 us: hop(): return lax.ppermute(block, 'fsdp', pairs)]
    all_gather x1, waiting for transfers between devices: 6.21 us -> 58.8 us  [shards(): lax.all_gather(w_qkv, 'fsdp', axis=0, tiled=True)]
    psum x1 -> x0, blocking collectives: 32 us -> none  [shards(): cond_total = lax.psum(cond_part, 'fsdp')]
  transfers between devices with their start and end apart: 17 -> 100, of which waited for: 13 -> 57; matrix products, arithmetic and copies ran while one was open for 17% -> 39% of each run, Pallas kernels for 0% -> 0%
where the time goes in v1:
time: 1130 us; the launch traced here: 1120 us
  waiting for transfers between devices  565 us (50%)
  matrix products  266 us (24%)
  local copies, waits for them, and re-layouts  92.7 us (8%)
  other arithmetic  92.5 us (8%)
  starting transfers between devices  88.8 us (8%)
  between operations  16.4 us (1%)
    ppermute x56, waiting for transfers between devices, hop(): return lax.ppermute(block, 'fsdp', pairs)  197 us
    all_gather x1, waiting for transfers between devices, shards(): lax.all_gather(w_fc2, 'fsdp', axis=0, tiled=True)  73.6 us
    dot_general x8, matrix products, product(): return jnp.dot(left, right, preferred_element_type=jnp.float32)  72 us
    all_gather x1, waiting for transfers between devices, shards(): lax.all_gather(w_proj2, 'fsdp', axis=0, tiled=True)  66.9 us
    dot_general x7, matrix products, input_grad(): jnp.einsum('ne,de->nd', grad, weight, preferred_element_type=jnp.float32)  59.2 us
    all_gather x1, waiting for transfers between devices, shards(): lax.all_gather(w_qkv, 'fsdp', axis=0, tiled=True)  58.8 us
    ppermute x56, starting transfers between devices, hop(): return lax.ppermute(block, 'fsdp', pairs)  57.3 us
    all_gather x1, waiting for transfers between devices, shards(): lax.all_gather(w_fc1, 'fsdp', axis=0, tiled=True)  51.1 us
  transfers between devices with their start and end apart: 100, of which 57 were waited for; matrix products, arithmetic and copies ran while one was open for 39% of the time, Pallas kernels for 0%

profile of v1, /device:TPU:0, one launch (start us, length us, event | category | flops | bytes accessed | tf_op | source)
XLA Modules:
  0.0 1121.1 jit_solution(2670835607985499530)
XLA Ops:
  27.0 58.8 %all-gather.8.cloned.1.call-done = bf16[1152,3456]{1,0:T(8,128)(2,1)} async-done(((bf16[72,3456]{1,0:T(8,128)(2,1)}), bf16[1152,3456]{1,0:T(8,128)(2,1)}) %all-gather.8.cloned.1.call-update) | async-done | bytes 7962640 | tf_op jit(solution)/shard_map/all_gather | solution.py:180
  85.8 9.9 convolution_convert_fusion
  114.2 16.7 %fusion.244 = (f32[16,512]{1,0:T(8,128)S(1)}, f32[16,512,1024]{2,1,0:T(8,128)}) fusion(bf16[512,16,72]{0,2,1:T(8,128)(2,1)S(1)} %get-tuple-element.67, bf16[512,16,72]{0,2,1:T(8,128)(2,1)S(1)} %get-tuple-element.54, bf16[512,3,16,72]{0,3,2,1:T(8,128)(2,1)} %bitcast.488, pred[512,1024]{1,0:T(8,128)(4,1)S(1)} %copy-done.46), kind=kOutput, calls=%fused_computation.452 | convolution fusion | flops 1237835776 | bytes 37650432 | tf_op jit(solution)/shard_map/qhd,khd->hqk/dot_general | solution.py:204
  130.8 14.6 %fusion = f32[16,512]{1,0:T(8,128)S(1)} fusion(f32[16,512,1024]{2,1,0:T(8,128)} %get-tuple-element.101, f32[16,512]{1,0:T(8,128)S(1)} %get-tuple-element.100), kind=kLoop, calls=%fused_computation.6 | loop fusion | flops 16769024 | bytes 33619968 | tf_op jit(solution)/shard_map/reduce_sum | solution.py:208
  146.1 14.9 %fusion.98 = bf16[16,72,512]{2,1,0:T(8,128)(2,1)S(1)} fusion(f32[16,512,1024]{2,1,0:T(8,128)} %get-tuple-element.101, f32[16,512]{1,0:T(8,128)S(1)} %fusion, f32[16,512]{1,0:T(8,128)S(1)} %get-tuple-element.100, bf16[512,16,72]{0,2,1:T(8,128)(2,1)} %get-tuple-element.66, bf16[512,16,72]{0,2,1:T(8,128)(2,1)} %get-tuple-element.52), kind=kOutput, calls=%fused_computation.150 | convolution fusion | flops 1238433792 | bytes 37158912 | tf_op jit(solution)/shard_map/hqk,khd->qhd/dot_general | solution.py:211
  168.2 51.1 %all-gather.12.cloned.1.call-done = bf16[1152,4608]{1,0:T(8,128)(2,1)} async-done(((bf16[72,4608]{1,0:T(8,128)(2,1)}), bf16[1152,4608]{1,0:T(8,128)(2,1)}) %all-gather.12.cloned.1.call-update) | async-done | bytes 10616848 | tf_op jit(solution)/shard_map/all_gather | solution.py:182
  219.3 15.4 %fusion.20 = (bf16[4608,512]{0,1:T(8,128)(2,1)}, f32[512,4608]{1,0:T(8,128)}) fusion(bf16[1152,4608]{1,0:T(8,128)(2,1)} %all-gather.12.cloned.1.call-done, f32[512,1152]{1,0:T(8,128)} %copy-done.5, f32[1152]{0:T(1024)S(1)} %get-tuple-element.91, f32[1152]{0:T(1024)S(1)} %get-tuple-element.92, f32[512]{0:T(512)S(1)} %fusion.216, ...), kind=kOutput, calls=%fused_computation.28 | convolution fusion | flops 5460000768 | bytes 27145216 | tf_op jit(solution)/shard_map/dot_general | solution.py:147
  234.8 73.6 %all-gather.14.cloned.1.call-done = bf16[4608,1152]{1,0:T(8,128)(2,1)} async-done(((bf16[288,1152]{1,0:T(8,128)(2,1)}), bf16[4608,1152]{1,0:T(8,128)(2,1)}) %all-gather.14.cloned.1.call-update) | async-done | bytes 10616848 | tf_op jit(solution)/shard_map/all_gather | solution.py:183
  308.4 14.1 %add_convert_fusion = (bf16[512,1152]{1,0:T(8,128)(2,1)}, f32[512,1152]{1,0:T(8,128)}) fusion(f32[512,1152]{1,0:T(8,128)S(1)} %copy-done.6, f32[1152]{0:T(1024)S(1)} %get-tuple-element.90, bf16[4608,1152]{1,0:T(8,128)(2,1)} %all-gather.14.cloned.1.call-done, f32[512,4608]{1,0:T(8,128)} %get-tuple-element.114), kind=kOutput, calls=%fused_computation.127 | convolution fusion | flops 5458821120 | bytes 25956864 | tf_op jit(solution)/shard_map/dot_general | solution.py:147
  322.4 39.6 %all-gather.16.cloned.1.call-done = bf16[1152,2048]{1,0:T(8,128)(2,1)} async-done(((bf16[72,2048]{1,0:T(8,128)(2,1)}), bf16[1152,2048]{1,0:T(8,128)(2,1)}) %all-gather.16.cloned.1.call-update) | async-done | bytes 4718608 | tf_op jit(solution)/shard_map/all_gather | solution.py:186
  370.7 66.9 %all-gather.18.cloned.1.call-done = bf16[2048,2048]{1,0:T(8,128)(2,1)} async-done(((bf16[128,2048]{1,0:T(8,128)(2,1)}), bf16[2048,2048]{1,0:T(8,128)(2,1)}) %all-gather.18.cloned.1.call-update) | async-done | bytes 8388624 | tf_op jit(solution)/shard_map/all_gather | solution.py:187
  437.6 12.3 %fusion.55 = (bf16[2048,512]{0,1:T(8,128)(2,1)}, f32[512,2048]{1,0:T(8,128)}) fusion(bf16[2048,2048]{1,0:T(8,128)(2,1)} %all-gather.18.cloned.1.call-done, f32[512,2048]{1,0:T(8,128)} %get-tuple-element.116), kind=kOutput, calls=%fused_computation.77 | convolution fusion | flops 4305453056 | bytes 18874368 | tf_op jit(solution)/shard_map/dot_general | solution.py:147
  449.9 33.4 %all-gather.20.cloned.1.call-done = bf16[2048,768]{1,0:T(8,128)(2,1)} async-done(((bf16[128,768]{1,0:T(8,128)(2,1)}), bf16[2048,768]{1,0:T(8,128)(2,1)}) %all-gather.20.cloned.1.call-update) | async-done | bytes 3145744 | tf_op jit(solution)/shard_map/all_gather | solution.py:188
  511.7 16.3 %fusion.12 = bf16[512,4608]{1,0:T(8,128)(2,1)} fusion(f32[512,4608]{1,0:T(8,128)} %get-tuple-element.114, bf16[512,1152]{1,0:T(8,128)(2,1)S(1)} %get-tuple-element.106, bf16[4608,1152]{1,0:T(8,128)(2,1)} %all-gather.14.cloned.1.call-done), kind=kOutput, calls=%fused_computation.20 | convolution fusion | flops 5483003904 | bytes 25952256 | tf_op jit(solution)/shard_map/ne,de->nd/dot_general | solution.py:151
  527.9 11.8 %multiply_reduce_fusion.2 = (f32[1152]{0:T(1024)S(1)}, f32[512]{0:T(512)S(1)}, f32[1152]{0:T(1024)S(1)}, f32[512,1152]{1,0:T(8,128)S(1)}) fusion(f32[512,1152]{1,0:T(8,128)S(1)} %copy-done.6, f32[512]{0:T(512)S(1)} %fusion.216, f32[512]{0:T(512)S(1)} %broadcast_multiply_fusion, f32[1152]{0:T(1024)S(1)} %get-tuple-element.92, ...), kind=kOutput, calls=%fused_computation.119 | convolution fusion | flops 5440534016 | bytes 20073984 | tf_op jit(solution)/shard_map/ne,de->nd/dot_general | solution.py:151
  550.0 15.6 %fusion.78 = f32[1024,16,72]{0,2,1:T(8,128)} fusion(bf16[512,16,72]{0,2,1:T(8,128)(2,1)S(1)} %bitcast.490, f32[16,512,1024]{2,1,0:T(8,128)} %get-tuple-element.101, f32[16,512]{1,0:T(8,128)S(1)} %copy-done.36), kind=kOutput, calls=%fused_computation.130 | convolution fusion | flops 1224736768 | bytes 39485440 | tf_op jit(solution)/shard_map/hqk,qhd->khd/dot_general | solution.py:267
  565.6 22.3 %multiply_reduce_fusion = (f32[16,512]{1,0:T(8,128)S(1)}, f32[16,512,1024]{2,1,0:T(8,128)}) fusion(f32[16,512,1024]{2,1,0:T(8,128)} %get-tuple-element.101, f32[16,512]{1,0:T(8,128)S(1)} %copy-done.36, bf16[512,16,72]{0,2,1:T(8,128)(2,1)S(1)} %bitcast.491, bf16[512,16,72]{0,2,1:T(8,128)(2,1)S(1)} %copy-done.24, bf16[512,16,72]{0,2,1:T(8,128)(2,1)S(1)} %copy-done.23), kind=kOutput, calls=%fused_computation.1 | convolution fusion | flops 1237835776 | bytes 70713344 | tf_op jit(solution)/shard_map/qhd,khd->hqk/dot_general | solution.py:258
  588.6 27.8 %multiply_convert_fusion = bf16[16,512,1024]{2,1,0:T(8,128)(2,1)} fusion(f32[16,512,1024]{2,1,0:T(8,128)} %get-tuple-element.110, f32[16,512,1024]{2,1,0:T(8,128)} %get-tuple-element.101, f32[16,512]{1,0:T(8,128)S(1)} %get-tuple-element.109, f32[16,512]{1,0:T(8,128)S(1)} %copy-done.36), kind=kLoop, calls=%fused_computation | loop fusion | flops 33554432 | bytes 83951616 | tf_op jit(solution)/shard_map/convert_element_type | solution.py:260
  616.5 11.4 %multiply_bitcast_fusion = f32[1024,16,72]{0,2,1:T(8,128)} fusion(bf16[16,512,1024]{2,1,0:T(8,128)(2,1)} %multiply_convert_fusion, bf16[512,3,16,72]{0,3,2,1:T(8,128)(2,1)} %bitcast.489), kind=kOutput, calls=%fused_computation.46 | convolution fusion | flops 1209139200 | bytes 22675456 | tf_op jit(solution)/shard_map/hqk,qhd->khd/dot_general | solution.py:265
  650.3 11.8 %constant_dynamic-slice_fusion.1 = (bf16[8,1,128,512]{2,1,0,3:T(2,128)(2,1)}, bf16[8,1,128,512]{2,1,0,3:T(2,128)(2,1)}, bf16[8,1,128,512]{2,1,0,3:T(2,128)(2,1)}, bf16[8,1,128,512]{2,1,0,3:T(2,128)(2,1)}) fusion(bf16[8,2,128,512]{2,1,0,3:T(2,128)(2,1)S(1)} %reshape.384, s32[]{:T(128)S(6)} %select_n.809, s32[]{:T(128)S(6)} %select_n.810, ...), kind=kLoop, calls=%fused_computation.374 | loop fusion | bytes 8388616 | tf_op jit(solution)/shard_map/jit(dynamic_index_in_dim)/dynamic_slice | solution.py:84
  691.0 10.4 fusion.100
  861.6 9.7 collective-permute-done.52
  1054.2 10.1 collective-permute-done.20
  1082.3 10.8 collective-permute-done.47
  (560 shorter events, 525.4 us)
Async XLA Ops:
  7.2 78.6 %all-gather.8.cloned.1.call-start = ((), (), s32[]{:S(2)}) async-start(), calls=%async_computation | async-start | bytes 8460288 | tf_op jit(solution)/shard_map/all_gather | solution.py:180
  8.0 153.1 %all-gather.10.cloned.1.call-start = ((), (), s32[]{:S(2)}) async-start(), calls=%async_computation.1 | async-start | bytes 2820096 | tf_op jit(solution)/shard_map/all_gather | solution.py:181
  8.7 210.6 %all-gather.12.cloned.1.call-start = ((), (), s32[]{:S(2)}) async-start(), calls=%async_computation.2 | async-start | bytes 11280384 | tf_op jit(solution)/shard_map/all_gather | solution.py:182
  9.4 298.9 %all-gather.14.cloned.1.call-start = ((), (), s32[]{:S(2)}) async-start(), calls=%async_computation.3 | async-start | bytes 11280384 | tf_op jit(solution)/shard_map/all_gather | solution.py:183
  10.0 352.1 %all-gather.16.cloned.1.call-start = ((), (), s32[]{:S(2)}) async-start(), calls=%async_computation.4 | async-start | bytes 5013504 | tf_op jit(solution)/shard_map/all_gather | solution.py:186
  10.6 427.0 %all-gather.18.cloned.1.call-start = ((), (), s32[]{:S(2)}) async-start(), calls=%async_computation.5 | async-start | bytes 8912896 | tf_op jit(solution)/shard_map/all_gather | solution.py:187
  11.2 472.2 %all-gather.20.cloned.1.call-start = ((), (), s32[]{:S(2)}) async-start(), calls=%async_computation.6 | async-start | bytes 3342336 | tf_op jit(solution)/shard_map/all_gather | solution.py:188
  168.0 543.8 %collective-permute-start.27 = (bf16[576,512]{1,0:T(8,128)(2,1)}, bf16[576,512]{1,0:T(8,128)(2,1)}, u32[]{:S(2)}, u32[]{:S(2)}) collective-permute-start(bf16[576,512]{1,0:T(8,128)(2,1)} %bitcast.49), channel_id=1, source_target_pairs={{0,1},{1,0},{2,3},{3,2},{4,5},{5,4},{6,7},{7,6},{8,9},{9,8},{10,11... | collective-permute-start | bytes 1769480 | tf_op jit(solution)/shard_map/ppermute | solution.py:21
  587.9 124.9 %collective-permute-start.28 = (bf16[512,1152]{1,0:T(8,128)(2,1)}, bf16[512,1152]{1,0:T(8,128)(2,1)}, u32[]{:S(2)}, u32[]{:S(2)}) collective-permute-start(bf16[512,1152]{1,0:T(8,128)(2,1)} %multiply_convert_fusion.6), channel_id=1, source_target_pairs={{0,1},{1,0},{2,3},{3,2},{4,5},{5,4},{6,7},{7,6},{8,9},{9,8},{10,11... | collective-permute-start | bytes 3538952 | tf_op jit(solution)/shard_map/ppermute | solution.py:21
  588.1 176.5 %collective-permute-start.61 = (bf16[512,2048]{1,0:T(8,128)(2,1)}, bf16[512,2048]{1,0:T(8,128)(2,1)}, u32[]{:S(2)}, u32[]{:S(2)}) collective-permute-start(bf16[512,2048]{1,0:T(8,128)(2,1)} %fusion.39), channel_id=1, source_target_pairs={{0,1},{1,0},{2,3},{3,2},{4,5},{5,4},{6,7},{7,6},{8,9},{9,8},{10,11... | collective-permute-start | bytes 6291464 | tf_op jit(solution)/shard_map/ppermute | solution.py:21
  588.4 113.0 %collective-permute-start.83 = (bf16[512,768]{1,0:T(8,128)(2,1)}, bf16[512,768]{1,0:T(8,128)(2,1)}, u32[]{:S(2)}, u32[]{:S(2)}) collective-permute-start(bf16[512,768]{1,0:T(8,128)(2,1)} %fusion.94), channel_id=1, source_target_pairs={{0,1},{1,0},{2,3},{3,2},{4,5},{5,4},{6,7},{7,6},{8,9},{9,8},{10,11... | collective-permute-start | bytes 2359304 | tf_op jit(solution)/shard_map/ppermute | solution.py:21
  710.2 63.3 %collective-permute-start.72 = (bf16[512,2048]{1,0:T(8,128)(2,1)S(1)}, bf16[512,2048]{1,0:T(8,128)(2,1)S(1)}, u32[]{:S(2)}, u32[]{:S(2)}) collective-permute-start(bf16[512,2048]{1,0:T(8,128)(2,1)S(1)} %copy-done.74), channel_id=1, source_target_pairs={{0,1},{1,0},{2,3},{3,2},{4,5},{5,4},{6,7},{7,6},{8,9},{9,8},{10,11... | collective-permute-start | bytes 6291464 | tf_op jit(solution)/shard_map/ppermute | solution.py:21
  711.8 52.2 %collective-permute-start.60 = (bf16[576,512]{1,0:T(8,128)(2,1)S(1)}, bf16[576,512]{1,0:T(8,128)(2,1)S(1)}, u32[]{:S(2)}, u32[]{:S(2)}) collective-permute-start(bf16[576,512]{1,0:T(8,128)(2,1)S(1)} %bitcast.573), channel_id=1, source_target_pairs={{0,1},{1,0},{2,3},{3,2},{4,5},{5,4},{6,7},{7,6},{8,9},{9,8},{10,11... | collective-permute-start | bytes 1769480 | tf_op jit(solution)/shard_map/ppermute | solution.py:21
  759.9 184.0 %collective-permute-start.39 = (bf16[512,4608]{1,0:T(8,128)(2,1)}, bf16[512,4608]{1,0:T(8,128)(2,1)}, u32[]{:S(2)}, u32[]{:S(2)}) collective-permute-start(bf16[512,4608]{1,0:T(8,128)(2,1)} %fusion.12), channel_id=1, source_target_pairs={{0,1},{1,0},{2,3},{3,2},{4,5},{5,4},{6,7},{7,6},{8,9},{9,8},{10,11... | collective-permute-start | bytes 14155784 | tf_op jit(solution)/shard_map/ppermute | solution.py:21
  763.9 37.0 %collective-permute-start.50 = (bf16[512,1152]{1,0:T(8,128)(2,1)S(1)}, bf16[512,1152]{1,0:T(8,128)(2,1)}, u32[]{:S(2)}, u32[]{:S(2)}) collective-permute-start(bf16[512,1152]{1,0:T(8,128)(2,1)S(1)} %copy-done.77), channel_id=1, source_target_pairs={{0,1},{1,0},{2,3},{3,2},{4,5},{5,4},{6,7},{7,6},{8,9},{9,8},{10,11... | collective-permute-start | bytes 3538952 | tf_op jit(solution)/shard_map/ppermute | solution.py:21
  764.0 160.5 %collective-permute-start.5 = (f32[2,512,16,72]{1,3,2,0:T(8,128)}, f32[2,512,16,72]{1,3,2,0:T(8,128)}, u32[]{:S(2)}, u32[]{:S(2)}) collective-permute-start(f32[2,512,16,72]{1,3,2,0:T(8,128)} %pad_maximum_fusion), channel_id=1, source_target_pairs={{0,1},{1,0},{2,3},{3,2},{4,5},{5,4},{6,7},{7,6},{8,9},{9,8},{10,11... | collective-permute-start | bytes 14155784 | tf_op jit(solution)/shard_map/ppermute | solution.py:21
  906.5 35.4 %collective-permute-start.38 = (bf16[576,512]{1,0:T(8,128)(2,1)S(1)}, bf16[576,512]{1,0:T(8,128)(2,1)}, u32[]{:S(2)}, u32[]{:S(2)}) collective-permute-start(bf16[576,512]{1,0:T(8,128)(2,1)S(1)} %bitcast.571), channel_id=1, source_target_pairs={{0,1},{1,0},{2,3},{3,2},{4,5},{5,4},{6,7},{7,6},{8,9},{9,8},{10,11... | collective-permute-start | bytes 1769480 | tf_op jit(solution)/shard_map/ppermute | solution.py:21
  910.6 89.0 %collective-permute-start.54 = (bf16[288,1152]{1,0:T(8,128)(2,1)}, bf16[288,1152]{1,0:T(8,128)(2,1)}, u32[]{:S(2)}, u32[]{:S(2)}) collective-permute-start(bf16[288,1152]{1,0:T(8,128)(2,1)} %get-tuple-element.30), channel_id=1, source_target_pairs={{0,4},{1,5},{4,8},{5,9},{8,12},{9,13},{12,14},{13,15},{14,10},{15,... | collective-permute-start | bytes 1990664 | tf_op jit(solution)/shard_map/ppermute | solution.py:36
  921.0 57.1 %collective-permute-start.81 = (bf16[128,2048]{1,0:T(8,128)(2,1)}, bf16[128,2048]{1,0:T(8,128)(2,1)}, u32[]{:S(2)}, u32[]{:S(2)}) collective-permute-start(bf16[128,2048]{1,0:T(8,128)(2,1)} %fusion.182), channel_id=1, source_target_pairs={{0,16},{16,0},{1,17},{17,1},{2,18},{18,2},{3,19},{19,3},{4,20},{20... | collective-permute-start | bytes 1572872 | tf_op jit(solution)/shard_map/ppermute | solution.py:25
  924.5 76.7 %collective-permute-start.58 = (bf16[288,1152]{1,0:T(8,128)(2,1)}, bf16[288,1152]{1,0:T(8,128)(2,1)}, u32[]{:S(2)}, u32[]{:S(2)}) collective-permute-start(bf16[288,1152]{1,0:T(8,128)(2,1)} %fusion.102), channel_id=1, source_target_pairs={{0,2},{1,3},{4,0},{5,1},{8,4},{9,5},{12,8},{13,9},{14,12},{15,13},... | collective-permute-start | bytes 1990664 | tf_op jit(solution)/shard_map/ppermute | solution.py:36
  969.2 52.5 %collective-permute-start.17 = (bf16[512,3456]{0,1:T(8,128)(2,1)}, bf16[512,3456]{0,1:T(8,128)(2,1)S(1)}, u32[]{:S(2)}, u32[]{:S(2)}) collective-permute-start(bf16[512,3456]{0,1:T(8,128)(2,1)} %bitcast.544), channel_id=1, source_target_pairs={{0,1},{1,0},{2,3},{3,2},{4,5},{5,4},{6,7},{7,6},{8,9},{9,8},{10,11... | collective-permute-start | bytes 10616840 | tf_op jit(solution)/shard_map/ppermute | solution.py:21
  977.4 44.2 %collective-permute-start.16 = (bf16[576,512]{1,0:T(8,128)(2,1)S(1)}, bf16[576,512]{1,0:T(8,128)(2,1)S(1)}, u32[]{:S(2)}, u32[]{:S(2)}) collective-permute-start(bf16[576,512]{1,0:T(8,128)(2,1)S(1)} %bitcast.576), channel_id=1, source_target_pairs={{0,1},{1,0},{2,3},{3,2},{4,5},{5,4},{6,7},{7,6},{8,9},{9,8},{10,11... | collective-permute-start | bytes 1769480 | tf_op jit(solution)/shard_map/ppermute | solution.py:21
  999.6 50.9 %collective-permute-start.45 = (bf16[72,4608]{1,0:T(8,128)(2,1)S(1)}, bf16[72,4608]{1,0:T(8,128)(2,1)}, u32[]{:S(2)}, u32[]{:S(2)}) collective-permute-start(bf16[72,4608]{1,0:T(8,128)(2,1)S(1)} %pad_maximum_fusion.12), channel_id=1, source_target_pairs={{0,2},{1,3},{4,0},{5,1},{8,4},{9,5},{12,8},{13,9},{14,12},{15,13},... | collective-permute-start | bytes 1990664 | tf_op jit(solution)/shard_map/ppermute | solution.py:36
  1014.9 35.7 %collective-permute-start.42 = (bf16[72,4608]{1,0:T(8,128)(2,1)S(1)}, bf16[72,4608]{1,0:T(8,128)(2,1)}, u32[]{:S(2)}, u32[]{:S(2)}) collective-permute-start(bf16[72,4608]{1,0:T(8,128)(2,1)S(1)} %fusion.109), channel_id=1, source_target_pairs={{0,4},{1,5},{4,8},{5,9},{8,12},{9,13},{12,14},{13,15},{14,10},{15,... | collective-permute-start | bytes 1990664 | tf_op jit(solution)/shard_map/ppermute | solution.py:36
  (165 other events, 2578.7 us)
Sparse Core Ops, SparseCore 0:
  10.2 75.5 all-gather.7
  87.9 41.6 all-gather.9
  131.9 87.3 all-gather.11
  221.5 86.8 all-gather.13
  310.5 51.5 all-gather.15
  364.1 73.4 all-gather.17
  439.9 43.4 all-gather.19

commit v2 on v1

--- a/solution.py
+++ b/solution.py
@@ -1,14 +1,167 @@
 from functools import partial
+from math import gcd
 
 import jax
 import jax.numpy as jnp
 from jax import lax
+from jax.experimental import pallas as pl
+from jax.experimental.pallas import tpu as pltpu
 from jax.sharding import PartitionSpec as P
 
 HEADS = 16
-
-
+SHORT = 256
 HIGH = lax.Precision.HIGHEST
+NT = (((1,), (1,)), ((), ()))
+TN = (((0,), (0,)), ((), ()))
+NN = (((1,), (0,)), ((), ()))
+
+
+def mat(left, right, dims):
+    return lax.dot_general(left, right, dims, preferred_element_type=jnp.float32)
+
+
+def head_window(head, width):
+    size = width // HEADS
+    first = jnp.minimum(head * size // 128, width // 128 - 2) * 128
+    lane = lax.broadcasted_iota(jnp.int32, (1, 256), 1)
+    low = head * size - first
+    return pl.multiple_of(first, 128), (lane >= low) & (lane < low + size)
+
+
+def attend_kernel(factor, long_ref, q_ref, k_ref, v_ref, kp_ref, vp_ref, att_ref, exact_ref, turned_ref, log_ref, sums):
+    count, width = q_ref.shape
+    sums[...] = jnp.zeros_like(sums)
+
+    def attend(head, key_parts, cols):
+        first, mask = head_window(head, width)
+        window = pl.ds(first, 256)
+        queries = jnp.where(mask, q_ref[cols, window], 0)
+        scores = [mat(k[rows, window], queries, NT) for k, v, rows in key_parts]
+        highest = scores[0].max(axis=0, keepdims=True)
+        for more in scores[1:]:
+            highest = jnp.maximum(highest, more.max(axis=0, keepdims=True))
+        expos = [jnp.exp((score - highest) * factor) for score in scores]
+        total, out = 0.0, 0.0
+        for expo in expos:
+            total = total + expo.sum(axis=0, keepdims=True)
+        share = 1.0 / total
+        for (k, v, rows), expo in zip(key_parts, expos):
+            values = jnp.where(mask, v[rows, window], 0)
+            out = out + mat(values, (expo * share).astype(jnp.bfloat16), TN)
+        sums[window, cols] += out
+        log_ref[pl.ds(head, 1), cols] = highest * factor + jnp.log(total)
+
+    everything = pl.ds(0, count)
+
+    @pl.when(long_ref[0] == 1)
+    def _():
+        @pl.loop(0, HEADS, unroll=2)
+        def _(head):
+            attend(head, [(k_ref, v_ref, everything), (kp_ref, vp_ref, everything)], everything)
+
+    @pl.when(long_ref[0] == 0)
+    def _():
+        @pl.loop(0, HEADS, unroll=2)
+        def _(head):
+            for top in range(0, count, SHORT):
+                attend(head, [(k_ref, v_ref, pl.ds(top, SHORT))], pl.ds(top, SHORT))
+
+    turned_ref[...] = sums[...].astype(jnp.bfloat16)
+    exact_ref[...] = sums[...].T
+    att_ref[...] = exact_ref[...].astype(jnp.bfloat16)
+
+
+def part_spec(count, width, number):
+    return pl.BlockSpec((count, width), lambda i: (0, number), pipeline_mode=pl.Buffered(1))
+
+
+def attend(long, qkv, peer, factor):
+    count, width = qkv.shape[0], qkv.shape[1] // 3
+    flops = 4 * HEADS * count * 2 * count * 256
+    return pl.pallas_call(
+        partial(attend_kernel, factor),
+        out_shape=[
+            jax.ShapeDtypeStruct((count, width), jnp.bfloat16),
+            jax.ShapeDtypeStruct((count, width), jnp.float32),
+            jax.ShapeDtypeStruct((width, count), jnp.bfloat16),
+            jax.ShapeDtypeStruct((HEADS, count), jnp.float32),
+        ],
+        grid=(1,),
+        in_specs=[pl.BlockSpec(memory_space=pltpu.SMEM)]
+        + [part_spec(count, width, j) for j in (0, 1, 2, 0, 1)],
+        out_specs=[part_spec(count, width, 0)] * 2
+        + [part_spec(width, count, 0), part_spec(HEADS, count, 0)],
+        scratch_shapes=[pltpu.VMEM((width, count), jnp.float32)],
+        compiler_params=pltpu.CompilerParams(vmem_limit_bytes=40 << 20),
+        cost_estimate=pl.CostEstimate(flops=flops, transcendentals=HEADS * count * 2 * count, bytes_accessed=16 * count * width),
+    )(long, qkv, qkv, qkv, peer, peer)
+
+
+def attend_back_kernel(factor, long_ref, q_ref, k_ref, v_ref, kp_ref, vp_ref, grad_ref, exact_ref, log_ref, dq_ref, dk_ref, dv_ref, peer_ref, sums):
+    count, width = q_ref.shape
+    for ref in (sums, dk_ref, dv_ref, peer_ref):
+        ref[...] = jnp.zeros_like(ref)
+
+    def back(head, key_parts, cols):
+        first, mask = head_window(head, width)
+        window = pl.ds(first, 256)
+        queries = jnp.where(mask, q_ref[cols, window], 0)
+        grads = jnp.where(mask, grad_ref[cols, window], 0)
+        weighed = grads.astype(jnp.float32) * exact_ref[cols, window]
+        ones = jnp.ones((8, 256), jnp.float32)
+        centre = lax.dot_general(ones, weighed, NT, precision=lax.Precision.HIGHEST, preferred_element_type=jnp.float32)[:1]
+        logs = log_ref[pl.ds(head, 1), cols]
+        turned = 0.0
+        for k, v, rows, dk, dv, base in key_parts:
+            keys = k[rows, window]
+            probs = jnp.exp(mat(keys, queries, NT) * factor - logs)
+            d_probs = mat(v[rows, window], grads, NT)
+            d_scores = (probs * (d_probs - centre)).astype(jnp.bfloat16)
+            spot = pl.ds(base + first, 256) if base else window
+            dk[rows, window] += mat(d_scores, queries, NN) * factor
+            dv[rows, spot] += mat(probs.astype(jnp.bfloat16), grads, NN)
+            turned = turned + mat(jnp.where(mask, keys, 0), d_scores, TN)
+        sums[window, cols] += turned * factor
+
+    everything = pl.ds(0, count)
+
+    @pl.when(long_ref[0] == 1)
+    def _():
+        @pl.loop(0, HEADS, unroll=2)
+        def _(head):
+            back(head, [(k_ref, v_ref, everything, dk_ref, dv_ref, 0), (kp_ref, vp_ref, everything, peer_ref, peer_ref, width)], everything)
+
+    @pl.when(long_ref[0] == 0)
+    def _():
+        @pl.loop(0, HEADS, unroll=2)
+        def _(head):
+            for top in range(0, count, SHORT):
+                back(head, [(k_ref, v_ref, pl.ds(top, SHORT), dk_ref, dv_ref, 0)], pl.ds(top, SHORT))
+
+    dq_ref[...] = sums[...].T.astype(jnp.bfloat16)
+
+
+def attend_back(long, qkv, peer, grad, exact, logs, factor):
+    count, width = grad.shape
+    flops = 10 * HEADS * count * 2 * count * 256
+    full = part_spec(count, width, 0)
+    return pl.pallas_call(
+        partial(attend_back_kernel, factor),
+        out_shape=[
+            jax.ShapeDtypeStruct((count, width), jnp.bfloat16),
+            jax.ShapeDtypeStruct((count, width), jnp.float32),
+            jax.ShapeDtypeStruct((count, width), jnp.float32),
+            jax.ShapeDtypeStruct((count, 2 * width), jnp.float32),
+        ],
+        grid=(1,),
+        in_specs=[pl.BlockSpec(memory_space=pltpu.SMEM)]
+        + [part_spec(count, width, j) for j in (0, 1, 2, 0, 1)]
+        + [full, full, part_spec(HEADS, count, 0)],
+        out_specs=[full, full, full, part_spec(count, 2 * width, 0)],
+        scratch_shapes=[pltpu.VMEM((width, count), jnp.float32)],
+        compiler_params=pltpu.CompilerParams(vmem_limit_bytes=48 << 20),
+        cost_estimate=pl.CostEstimate(flops=flops, transcendentals=HEADS * count * 2 * count, bytes_accessed=40 * count * width),
+    )(long, qkv, qkv, qkv, peer, peer, grad, exact, logs)
 
 
 def swapped(block, axis, apart):
@@ -25,15 +178,34 @@
     return lax.ppermute(block, "bins", [(0, 1), (1, 0)])
 
 
+def ring_route(chips):
+    route = [2 * chip for chip in range(chips // 2)]
+    return route + [chip + 1 for chip in reversed(route)]
+
+
 def hop(block, apart):
     chips = lax.axis_size("fsdp") // 2
-    route = [2 * chip for chip in range(chips // 2)]
-    route = route + [chip + 1 for chip in reversed(route)]
+    route = ring_route(chips)
     pairs = []
     for spot, chip in enumerate(route):
         onward = route[(spot + apart) % chips]
         pairs += [(2 * chip, 2 * onward), (2 * chip + 1, 2 * onward + 1)]
     return lax.ppermute(block, "fsdp", pairs)
+
+
+def parted_hop(block, apart):
+    count, groups = lax.axis_size("fsdp"), lax.axis_size("bins")
+    chips = count // 2
+    route = ring_route(chips)
+    pairs = []
+    for group in range(groups):
+        for spot, chip in enumerate(route):
+            for core in range(2):
+                way = apart if (group + core) % 2 == 0 else -apart
+                onward = route[(spot + way) % chips]
+                base = group * count + core
+                pairs.append((base + 2 * chip, base + 2 * onward))
+    return lax.ppermute(block, ("bins", "fsdp"), pairs)
 
 
 def chip_at(apart):
@@ -44,11 +216,115 @@
     return jnp.where(spot < chips // 2, 2 * spot, 2 * (chips - 1 - spot) + 1)
 
 
+def gathered(block):
+    core = lax.axis_index("fsdp") % 2
+    parity = (lax.axis_index("bins") + core) % 2
+    far = lax.axis_size("fsdp") // 4
+    near = max(1, round(far / 3))
+    half = block.shape[0] // 2
+    ahead, behind, peers = [block], [block], {}
+    fresh = [(0, block)]
+    step = 0
+    while fresh:
+        step += 1
+        flights = [(place, swapped(piece, "fsdp", 0), True) for place, piece in fresh]
+        if step < far:
+            flights.append((step, parted_hop(ahead[-1], 1), False))
+        if step == far:
+            part = lax.dynamic_slice_in_dim(ahead[-1], parity * half, half)
+            flights.append((far, parted_hop(part, 1), False))
+        if step <= near:
+            flights.append((-step, parted_hop(behind[-1], -1), False))
+        if near < step - 1 < far:
+            flights.append((1 - step, bins_peer(ahead[step - 1]), False))
+        if step == far + 1:
+            flights.append((far, bins_peer(arm), False))
+        arrived = yield [flight for _, flight, _ in flights]
+        fresh = []
+        for (place, _, swap), piece in zip(flights, arrived):
+            if swap:
+                peers[place] = piece
+                continue
+            if place == far and step == far:
+                arm = piece
+                continue
+            if place == far:
+                first = jnp.where(parity == 0, arm, piece)
+                piece = jnp.concatenate([first, jnp.where(parity == 0, piece, arm)])
+            (behind if place < 0 else ahead).append(piece)
+            fresh.append((place, piece))
+    way = 1 - 2 * parity
+    places = [*range(far + 1), *(-place for place in range(1, far))]
+    origins = [2 * chip_at(-way * place) + core for place in places]
+    origins += [2 * chip_at(way * place) + 1 - core for place in places]
+    pieces = ahead + behind[1:] + [peers[place] for place in places]
+    return pieces, jnp.stack(origins).astype(jnp.int32)
+
+
+def slabs(block):
+    return block.reshape(-1, 8, block.shape[-1])
+
+
+def assemble(pieces, origins, layout, shapes):
+    width = pieces[0].shape[-1]
+    copies = len(pieces) * len(layout)
+
+    def kernel(origins_ref, *refs):
+        blocks, wholes, sems = refs[: len(pieces)], refs[len(pieces) : -1], refs[-1]
+        moves = []
+        for number, block in enumerate(blocks):
+            top = 0
+            for weight, height, column in layout:
+                spot = origins_ref[number] * height
+                moves.append(
+                    pltpu.make_async_copy(
+                        block.at[pl.ds(top, height)],
+                        wholes[weight].at[pl.ds(spot, height), :, pl.ds(column, width)],
+                        sems.at[len(moves)],
+                    )
+                )
+                top += height
+        for move in moves:
+            move.start()
+        for move in moves:
+            move.wait()
+
+    size = 2 * sum(rows * columns for rows, columns in shapes)
+    wholes = pl.pallas_call(
+        kernel,
+        out_shape=[jax.ShapeDtypeStruct((rows // 8, 8, columns), jnp.bfloat16) for rows, columns in shapes],
+        in_specs=[pl.BlockSpec(memory_space=pltpu.SMEM)]
+        + [pl.BlockSpec(memory_space=pl.ANY)] * len(pieces),
+        out_specs=[pl.BlockSpec(memory_space=pltpu.VMEM)] * len(shapes),
+        scratch_shapes=[pltpu.SemaphoreType.DMA((copies,))],
+        compiler_params=pltpu.CompilerParams(vmem_limit_bytes=2 * size + (4 << 20)),
+        cost_estimate=pl.CostEstimate(flops=0, transcendentals=0, bytes_accessed=2 * size),
+    )(origins, *pieces)
+    return [block.reshape(shape) for block, shape in zip(wholes, shapes)]
+
+
+def whole(shards, width):
+    if any(shard.shape[0] % 8 for shard in shards):
+        return [lax.all_gather(shard, "fsdp", axis=0, tiled=True) for shard in shards]
+    blocks, layout = [], []
+    parts = max(shard.shape[1] // width for shard in shards)
+    for column in range(parts):
+        for weight, shard in enumerate(shards):
+            if column * width < shard.shape[1]:
+                blocks.append(shard[:, column * width : (column + 1) * width])
+                layout.append((weight, shard.shape[0] // 8, column * width))
+    block = jnp.concatenate([slabs(block) for block in blocks])
+    count = lax.axis_size("fsdp")
+    shapes = [(count * shard.shape[0], shard.shape[1]) for shard in shards]
+    pieces, origins = yield from gathered(block)
+    return assemble(pieces, origins, layout, shapes)
+
+
 def doubled(block):
     count, place = lax.axis_size("fsdp"), lax.axis_index("fsdp")
     step = 0
     while 1 << step < count:
-        other = swapped(block, "fsdp", step)
+        other = yield swapped(block, "fsdp", step)
         upper = (place >> step) % 2 == 1
         block = jnp.where(
             upper, jnp.concatenate([other, block]), jnp.concatenate([block, other])
@@ -124,6 +400,131 @@
 def both_groups(block):
     rounded = lax.reduce_precision(block, 8, 7)
     return rounded + bins_peer(rounded.astype(jnp.bfloat16)).astype(jnp.float32)
+
+
+def scattered_grad(left, right):
+    total = jnp.einsum("nd,ne->de", left, right, preferred_element_type=jnp.float32)
+    return lax.psum_scatter(total.astype(jnp.bfloat16), "fsdp", scatter_dimension=0, tiled=True)
+
+
+def parts_kernel(spots_ref, mine_ref, theirs_ref, grad_ref, other_ref, *refs):
+    outs, (turned, left, total) = refs[:-3], refs[-3:]
+    number, half = len(outs), outs[0].shape[0]
+    count, rows = mine_ref.shape[0], 2 * half
+
+    @pl.when(pl.program_id(0) == 0)
+    def _():
+        for part in range(number):
+            lanes = pl.ds(pl.multiple_of(spots_ref[0, part] * 128, 128), turned.shape[0])
+            turned[:, :count] = mine_ref[:, lanes].T
+            turned[:, count:] = theirs_ref[:, lanes].T
+            low = pl.ds(pl.multiple_of(spots_ref[1, part], 16), rows)
+            left[part * rows : (part + 1) * rows] = turned[low]
+
+    total[...] = mat(left[:, :count], grad_ref[...], NN) + mat(left[:, count:], other_ref[...], NN)
+    for part, out in enumerate(outs):
+        first = part * rows
+        if out.shape[0] == half:
+            first = pl.multiple_of(first + spots_ref[2, 0] * half, 8)
+        out[...] = total[pl.ds(first, out.shape[0]), :].astype(out.dtype)
+
+
+def grad_parts(mine, theirs, grad, other, chips):
+    (count, columns), features = grad.shape, mine.shape[1]
+    rows = 2 * features // lax.axis_size("fsdp")
+    reach = (rows + 128 - gcd(rows, 128) + 127) // 128 * 128
+    starts = jnp.stack([jnp.asarray(chip, jnp.int32) * rows for chip in chips])
+    windows = jnp.minimum(starts // 128, (features - reach) // 128)
+    core = jnp.broadcast_to(lax.axis_index("fsdp") % 2, starts.shape)
+    spots = jnp.stack([windows, starts - windows * 128, core.astype(jnp.int32)])
+    tile, number = 1152 if columns > 2304 else 384, len(chips)
+    if columns % tile:
+        tile = 256
+    tall = pl.BlockSpec((count, features), lambda i: (0, 0), pipeline_mode=pl.Buffered(1))
+    wide = pl.BlockSpec((count, tile), lambda i: (0, i))
+    kept = [rows // 2] + [rows] * (number - 2) + [rows // 2]
+    kinds = [jnp.bfloat16] + [jnp.float32] * (number - 1)
+    return pl.pallas_call(
+        parts_kernel,
+        out_shape=[jax.ShapeDtypeStruct((k, columns), kind) for k, kind in zip(kept, kinds)],
+        grid=(columns // tile,),
+        in_specs=[pl.BlockSpec(memory_space=pltpu.SMEM), tall, tall, wide, wide],
+        out_specs=[pl.BlockSpec((k, tile), lambda i: (0, i)) for k in kept],
+        scratch_shapes=[
+            pltpu.VMEM((reach, 2 * count), jnp.bfloat16),
+            pltpu.VMEM((number * rows, 2 * count), jnp.bfloat16),
+            pltpu.VMEM((number * rows, tile), jnp.float32),
+        ],
+        compiler_params=pltpu.CompilerParams(vmem_limit_bytes=48 << 20),
+        cost_estimate=pl.CostEstimate(
+            flops=4 * number * rows * count * columns,
+            transcendentals=0,
+            bytes_accessed=4 * count * (columns + features) + 4 * (number - 1) * rows * columns,
+        ),
+    )(spots, mine, theirs, grad, other)
+
+
+def core_hop(block):
+    chips = lax.axis_size("fsdp") // 2
+    route = ring_route(chips)
+    pairs = []
+    for spot, chip in enumerate(route):
+        for core, way in ((0, 1), (1, -1)):
+            pairs.append((2 * chip + core, 2 * route[(spot + way) % chips] + core))
+    return lax.ppermute(block, "fsdp", pairs)
+
+
+def grad_chain(left, right, theirs=None):
+    rows = left.shape[1] // lax.axis_size("fsdp")
+    if rows % 8:
+        return full_grad(left, right)
+    core = lax.axis_index("fsdp") % 2
+    way = 1 - 2 * core
+    far = lax.axis_size("fsdp") // 4
+    if theirs is None:
+        theirs = swapped(left, "fsdp", 0)
+    other = yield swapped(right, "fsdp", 0)
+    steps = list(range(far, 0, -1))
+    chips = [chip_at(far)] + [chip_at(way * apart) for apart in steps[1:]] + [chip_at(0)]
+    parts = grad_parts(left, theirs, right, other, chips)
+    arrived = yield core_hop(parts[0])
+    for number in range(1, far):
+        if number == 1:
+            first = jnp.where(core == 0, arrived, 0)
+            arrived = jnp.concatenate([first, jnp.where(core == 0, 0, arrived)])
+        arrived = yield core_hop((parts[number] + arrived).astype(jnp.bfloat16))
+    kept = lax.dynamic_slice_in_dim(arrived, core * rows, rows)
+    sent = lax.dynamic_slice_in_dim(arrived, (1 - core) * rows, rows)
+    back = yield swapped(sent, "fsdp", 0)
+    total = parts[far] + kept + back
+    rounded = lax.reduce_precision(total, 8, 7)
+    across = yield bins_peer(rounded.astype(jnp.bfloat16))
+    return rounded + across.astype(jnp.float32)
+
+
+class Chain:
+    def __init__(self, steps):
+        self.steps, self.flight, self.result = steps, (), None
+        self.push(None)
+
+    def push(self, arrived):
+        if self.flight is None:
+            return
+        try:
+            self.flight = self.steps.send(arrived)
+        except StopIteration as stop:
+            self.flight, self.result = None, stop.value
+
+    def beat(self, *values):
+        if self.flight is not None:
+            values, arrived = lax.optimization_barrier((values, self.flight))
+            self.push(arrived)
+        return values if len(values) > 1 else values[0]
+
+    def finish(self):
+        while self.flight is not None:
+            self.push(self.flight)
+        return self.result
 
 
 def full_grad(left, right):
@@ -175,109 +576,108 @@
     silu_cond, silu_back = jax.vjp(jax.nn.silu, condition)
     cond_low = silu_cond.astype(jnp.bfloat16)
     mod_cols = product(cond_low, w_ada)
-    modulation = doubled(mod_cols.reshape(-1)).reshape(6, width)
-    block_set = (
-        lax.all_gather(w_qkv, "fsdp", axis=0, tiled=True),
-        lax.all_gather(w_out, "fsdp", axis=0, tiled=True),
-        lax.all_gather(w_fc1, "fsdp", axis=0, tiled=True),
-        lax.all_gather(w_fc2, "fsdp", axis=0, tiled=True),
-    )
-    head_set = (
-        lax.all_gather(w_proj1, "fsdp", axis=0, tiled=True),
-        lax.all_gather(w_proj2, "fsdp", axis=0, tiled=True),
-        lax.all_gather(w_proj3, "fsdp", axis=0, tiled=True),
-    )
-    full_qkv, full_out, full_fc1, full_fc2 = block_set
-    head_first, head_second, head_third = head_set
+    first_set = Chain(whole([w_qkv, w_out], width))
+    mod_chain = Chain(doubled(mod_cols.reshape(-1)))
+    for _ in range(2):
+        mod_chain.push(mod_chain.flight)
+        first_set.push(first_set.flight)
+    w_fc1, w_fc2, w_proj3 = first_set.beat(w_fc1, w_fc2, w_proj3)
+    second_set = Chain(whole([w_fc1, w_fc2], width))
+    head_third = lax.all_gather(w_proj3, "fsdp", axis=0, tiled=True)
+    modulation = mod_chain.finish().reshape(6, width)
+    full_qkv, full_out = first_set.finish()
+    full_qkv, full_out = second_set.beat(full_qkv, full_out)
     h_one, norm_one_back = jax.vjp(modulate, tokens_f, modulation[0], modulation[1])
     in_one = h_one.astype(jnp.bfloat16)
-    qkv_low = product(in_one, full_qkv).astype(jnp.bfloat16).reshape(count, 3, HEADS, head_size)
-    queries = qkv_low[:, 0]
-    pair_own = jnp.stack([qkv_low[:, 1], qkv_low[:, 2]])
-    pair_peer = swapped(pair_own, "fsdp", 0)
-    keys_all = jnp.concatenate([pair_own[0], pair_peer[0]], axis=0)
-    values_all = jnp.concatenate([pair_own[1], pair_peer[1]], axis=0)
+    qkv_low = product(in_one, full_qkv).astype(jnp.bfloat16)
+    peer_low = swapped(qkv_low[:, width:], "fsdp", 0)
+    qkv_low, peer_low, w_proj1, w_proj2 = second_set.beat(qkv_low, peer_low, w_proj1, w_proj2)
+    third_set = Chain(whole([w_proj1, w_proj2], w_proj1.shape[1] // 2))
     place = lax.axis_index("fsdp")
     own_ids = lax.dynamic_slice_in_dim(segments, place * count, count)
-    peer_ids = lax.dynamic_slice_in_dim(segments, jnp.bitwise_xor(place, 1) * count, count)
-    same = own_ids[:, None] == jnp.concatenate([own_ids, peer_ids])[None, :]
-    raw = jnp.einsum("qhd,khd->hqk", queries, keys_all, preferred_element_type=jnp.float32) * factor
-    masked = jnp.where(same[None], raw, -1e30)
-    highest = jnp.max(masked, axis=-1, keepdims=True)
-    expo = jnp.exp(masked - highest)
-    totals = jnp.sum(expo, axis=-1, keepdims=True)
-    log_total = highest + jnp.log(totals)
-    probs_low = (expo / totals).astype(jnp.bfloat16)
-    attended = jnp.einsum("hqk,khd->qhd", probs_low, values_all, preferred_element_type=jnp.float32)
-    attended = attended.astype(jnp.bfloat16).reshape(count, width)
+    long = (own_ids[:1] == own_ids[count - 1 :]).astype(jnp.int32)
+    attended, exact, _, logs = attend(long, qkv_low, peer_low, factor)
+    attended, exact, logs = second_set.beat(attended, exact, logs)
+    attended, exact, logs = third_set.beat(attended, exact, logs)
     branch_one = product(attended, full_out)
     resid_one = tokens_f + modulation[2] * branch_one
+    resid_one = second_set.beat(resid_one)
+    resid_one = third_set.beat(resid_one)
+    full_fc1, full_fc2 = second_set.finish()
+    full_fc1, full_fc2 = third_set.beat(full_fc1, full_fc2)
     h_two, norm_two_back = jax.vjp(modulate, resid_one, modulation[3], modulation[4])
     in_two = h_two.astype(jnp.bfloat16)
     hidden_pre = product(in_two, full_fc1)
     hidden_act, gelu_back = jax.vjp(partial(jax.nn.gelu, approximate=True), hidden_pre)
     hidden_low = hidden_act.astype(jnp.bfloat16)
+    hidden_low = third_set.beat(hidden_low)
     branch_two = product(hidden_low, full_fc2)
     result = resid_one + modulation[5] * branch_two
     result_low = result.astype(jnp.bfloat16)
+    head_first, head_second = third_set.finish()
     first_act, first_back = jax.vjp(jax.nn.silu, product(result_low, head_first))
     first_low = first_act.astype(jnp.bfloat16)
     second_act, second_back = jax.vjp(jax.nn.silu, product(first_low, head_second))
     second_low = second_act.astype(jnp.bfloat16)
     predicted = product(second_low, head_third)
     cos_total, cos_back = jax.vjp(partial(cosine_sum, target_f), predicted)
+    in_one_peer, in_two_peer, attended_peer, hidden_peer = (
+        swapped(block, "fsdp", 0) for block in (in_one, in_two, attended, hidden_low)
+    )
     (grad_pred,) = cos_back(jnp.float32(-1.0))
     grad_pred_low = grad_pred.astype(jnp.bfloat16)
-    grad_third = full_grad(second_low, grad_pred_low)
+    grad_third = scattered_grad(second_low, grad_pred_low)
     (grad_second_pre,) = second_back(input_grad(grad_pred_low, head_third))
     grad_second_low = grad_second_pre.astype(jnp.bfloat16)
-    grad_second = full_grad(first_low, grad_second_low)
+    grad_second = scattered_grad(first_low, grad_second_low)
     (grad_first_pre,) = first_back(input_grad(grad_second_low, head_second))
     grad_first_low = grad_first_pre.astype(jnp.bfloat16)
-    grad_first = full_grad(result_low, grad_first_low)
+    grad_first = scattered_grad(result_low, grad_first_low)
     d_result = cotangent.astype(jnp.float32) + input_grad(grad_first_low, head_first)
     grad_gate_two = jnp.sum(d_result * branch_two, axis=0)
     d_branch_two = (d_result * modulation[5]).astype(jnp.bfloat16)
-    grad_fc2 = full_grad(hidden_low, d_branch_two)
+    chain_fc2 = Chain(grad_chain(hidden_low, d_branch_two, hidden_peer))
+    d_branch_two = chain_fc2.beat(d_branch_two)
     (d_pre,) = gelu_back(input_grad(d_branch_two, full_fc2))
     d_pre_low = d_pre.astype(jnp.bfloat16)
-    grad_fc1 = full_grad(in_two, d_pre_low)
+    d_pre_low = chain_fc2.beat(d_pre_low)
+    chain_fc1 = Chain(grad_chain(in_two, d_pre_low, in_two_peer))
     d_resid_part, grad_shift_two, grad_scale_two = norm_two_back(input_grad(d_pre_low, full_fc1))
+    d_resid_part = chain_fc1.beat(chain_fc2.beat(d_resid_part))
     d_resid = d_result + d_resid_part
     grad_gate_one = jnp.sum(d_resid * branch_one, axis=0)
     d_branch_one = (d_resid * modulation[2]).astype(jnp.bfloat16)
-    grad_out = full_grad(attended, d_branch_one)
-    d_attended = (
-        input_grad(d_branch_one, full_out).astype(jnp.bfloat16).reshape(count, HEADS, head_size)
+    chain_out = Chain(grad_chain(attended, d_branch_one, attended_peer))
+    d_branch_one = chain_fc1.beat(d_branch_one)
+    d_attended = input_grad(d_branch_one, full_out).astype(jnp.bfloat16)
+    d_attended = chain_out.beat(chain_fc2.beat(d_attended))
+    d_queries, d_keys, d_values, d_peer = attend_back(
+        long, qkv_low, peer_low, d_attended, exact, logs, factor
     )
-    again_raw = (
-        jnp.einsum("qhd,khd->hqk", queries, keys_all, preferred_element_type=jnp.float32) * factor
+    from_peer = swapped(d_peer, "fsdp", 0)
+    d_queries = chain_out.beat(chain_fc1.beat(d_queries))
+    from_peer = chain_fc2.beat(from_peer)
+    d_qkv = jnp.concatenate(
+        [
+            d_queries,
+            (d_keys + from_peer[:, :width]).astype(jnp.bfloat16),
+            (d_values + from_peer[:, width:]).astype(jnp.bfloat16),
+        ],
+        axis=1,
     )
-    probs = jnp.exp(jnp.where(same[None], again_raw, -1e30) - log_total)
-    probs_again = probs.astype(jnp.bfloat16)
-    d_probs = jnp.einsum("qhd,khd->hqk", d_attended, values_all, preferred_element_type=jnp.float32)
-    centre = jnp.sum(d_probs * probs, axis=-1, keepdims=True)
-    d_scores = (probs * (d_probs - centre)).astype(jnp.bfloat16)
-    d_queries = (
-        jnp.einsum("hqk,khd->qhd", d_scores, keys_all, preferred_element_type=jnp.float32) * factor
+    chain_qkv = Chain(grad_chain(in_one, d_qkv, in_one_peer))
+    d_qkv = chain_out.beat(chain_fc1.beat(d_qkv))
+    d_tok_part, grad_shift_one, grad_scale_one = norm_one_back(input_grad(d_qkv, full_qkv))
+    d_tok_part = chain_qkv.beat(chain_fc1.beat(d_tok_part))
+    d_tok_part, head_parts = lax.optimization_barrier(
+        (d_tok_part, (grad_first, grad_second, grad_third))
     )
-    d_keys = (
-        jnp.einsum("hqk,qhd->khd", d_scores, queries, preferred_element_type=jnp.float32) * factor
+    grad_first, grad_second, grad_third = (
+        both_groups(part.astype(jnp.float32)) for part in head_parts
     )
-    d_values = jnp.einsum(
-        "hqk,qhd->khd", probs_again, d_attended, preferred_element_type=jnp.float32
-    )
-    from_peer = swapped(jnp.stack([d_keys[count:], d_values[count:]]), "fsdp", 0)
-    keys_grad = d_keys[:count] + from_peer[0]
-    values_grad = d_values[:count] + from_peer[1]
-    d_qkv = (
-        jnp.stack([d_queries, keys_grad, values_grad], axis=1)
-        .reshape(count, 3 * width)
-        .astype(jnp.bfloat16)
-    )
-    grad_qkv = full_grad(in_one, d_qkv)
-    d_tok_part, grad_shift_one, grad_scale_one = norm_one_back(input_grad(d_qkv, full_qkv))
     grad_tokens = d_resid + d_tok_part
+    grad_fc2, grad_out = chain_fc2.finish(), chain_out.finish()
+    grad_fc1, grad_qkv = chain_fc1.finish(), chain_qkv.finish()
     d_modulation = jnp.stack(
         [
             grad_shift_one,

time: 1130 us -> 758 us (0.67)
  waiting for transfers between devices: 565 us -> 278 us
  Pallas kernels: 0 us -> 141 us
  matrix products: 266 us -> 134 us
  local copies, waits for them, and re-layouts: 92.7 us -> 30.5 us
  other arithmetic: 92.5 us -> 54.2 us
    all_gather x7 -> x1, waiting for transfers between devices: 323 us -> 0.02 us  [shards(): head_third = lax.all_gather(w_proj3, 'fsdp', axis=0, tiled=True)]
    pallas_call x0 -> x9, Pallas kernels: none -> 141 us  [the longest x4 48.5 us: grad_parts(): pl.pallas_call(parts_kernel, out_shape=[jax.ShapeDtypeStruct((k, columns)...]
    dot_general x13 -> x3, matrix products: 134 us -> 19.8 us  [scattered_grad(): jnp.einsum('nd,ne->de', left, right, preferred_element_type=jnp.float32)]
    ppermute x9 -> x18, waiting for transfers between devices: 20.8 us -> 64 us  [bins_peer(): return lax.ppermute(block, 'bins', [(0, 1), (1, 0)])]
    ppermute x56 -> x31, waiting for transfers between devices: 197 us -> 164 us  [the longest x16 105 us: core_hop(): return lax.ppermute(block, 'fsdp', pairs)]
    ppermute x28 -> x50, waiting for transfers between devices: 20.7 us -> 50.1 us  [swapped(): return lax.ppermute(block, axis, route)]
    dynamic_slice x5 -> x7, local copies, waits for them, and re-layouts: 20.5 us -> 2.1 us  [the longest x3 1.11 us: gathered(): part = lax.dynamic_slice_in_dim(ahead[-1], parity * half, half)]
    dot_general x8, matrix products: 72 us -> 55.6 us  [product(): return jnp.dot(left, right, preferred_element_type=jnp.float32)]
  transfers between devices with their start and end apart: 100 -> 103, of which waited for: 57 -> 41; matrix products, arithmetic and copies ran while one was open for 39% -> 25% of each run, Pallas kernels for 0% -> 19%
where the time goes in v2:
time: 758 us; the launch traced here: 747 us
  waiting for transfers between devices  278 us (37%)
  Pallas kernels  141 us (19%)
  matrix products  134 us (18%)
  starting transfers between devices  91.5 us (12%)
  other arithmetic  54.2 us (7%)
  local copies, waits for them, and re-layouts  30.5 us (4%)
  between operations  17.3 us (2%)
    ppermute x16, waiting for transfers between devices, core_hop(): return lax.ppermute(block, 'fsdp', pairs)  105 us
    ppermute x18, waiting for transfers between devices, bins_peer(): return lax.ppermute(block, 'bins', [(0, 1), (1, 0)])  64 us
    ppermute x15, waiting for transfers between devices, parted_hop(): return lax.ppermute(block, ('bins', 'fsdp'), pairs)  59.3 us
    dot_general x7, matrix products, input_grad(): jnp.einsum('ne,de->nd', grad, weight, preferred_element_type=jnp.float32)  57.9 us
    dot_general x8, matrix products, product(): return jnp.dot(left, right, preferred_element_type=jnp.float32)  55.6 us
    ppermute x50, waiting for transfers between devices, swapped(): return lax.ppermute(block, axis, route)  50.1 us
    pallas_call x4, Pallas kernels, grad_parts(): pl.pallas_call(parts_kernel, out_shape=[jax.ShapeDtypeStruct((k, columns)...  48.5 us
    pallas_call x1, Pallas kernels, attend_back(): pl.pallas_call(partial(attend_back_kernel, factor), out_shape=[jax.ShapeD...  39.8 us
  transfers between devices with their start and end apart: 103, of which 41 were waited for; matrix products, arithmetic and copies ran while one was open for 25% of the time, Pallas kernels for 19%

profile of v2, /device:TPU:0, one launch (start us, length us, event | category | flops | bytes accessed | tf_op | source)
XLA Modules:
  0.0 746.8 jit_solution(12881588335320196842)
XLA Ops:
  13.3 14.4 %collective-permute-done.4.refs_1_ = bf16[36,8,1152]{2,1,0:T(8,128)(2,1)S(1)} collective-permute-done((bf16[36,8,1152]{2,1,0:T(8,128)(2,1)S(1)}, bf16[36,8,1152]{2,1,0:T(8,128)(2,1)S(1)}, u32[]{:S(2)}, u32[]{:S(2)}) %collective-permute-start.4) | collective-permute-done | bytes 663584 | tf_op jit(solution)/shard_map/ppermute | solution.py:208
  70.2 13.2 %collective-permute-done.10 = bf16[18,8,1152]{2,1,0:T(8,128)(2,1)S(1)} collective-permute-done((bf16[18,8,1152]{2,1,0:T(8,128)(2,1)S(1)}, bf16[18,8,1152]{2,1,0:T(8,128)(2,1)S(1)}, u32[]{:S(2)}, u32[]{:S(2)}) %collective-permute-start.10) | collective-permute-done | bytes 331808 | tf_op jit(solution)/shard_map/ppermute | solution.py:178
  119.7 9.9 %collective-permute-done.26.refs_2_ = bf16[72,8,1152]{2,1,0:T(8,128)(2,1)} collective-permute-done((bf16[72,8,1152]{2,1,0:T(8,128)(2,1)}, bf16[72,8,1152]{2,1,0:T(8,128)(2,1)}, u32[]{:S(2)}, u32[]{:S(2)}) %collective-permute-start.26) | collective-permute-done | bytes 1327136 | tf_op jit(solution)/shard_map/ppermute | solution.py:208
  137.6 24.7 %shard_map.213 = (bf16[512,1152]{1,0:T(8,128)(2,1)}, f32[512,1152]{1,0:T(8,128)S(1)}, bf16[1152,512]{1,0:T(8,128)(2,1)}, f32[16,512]{1,0:T(8,128)S(1)}) custom-call(s32[1]{0:T(128)S(6)} %convert_element_type.241.long_ref, bf16[512,3456]{1,0:T(8,128)(2,1)S(1)} %copy-done.10, bf16[512,3456]{1,0:T(8,128)(2,1)S(1)} %copy-done.10, ...), custom_call_target="tpu_custom_call" | custom-call | flops 8589934592 | bytes 9437184 | tf_op jit(solution)/shard_map/pallas_call | solution.py:81
  168.1 17.4 %collective-permute-done.32.refs_5_ = bf16[50,8,1024]{2,1,0:T(8,128)(2,1)} collective-permute-done((bf16[50,8,1024]{2,1,0:T(8,128)(2,1)S(1)}, bf16[50,8,1024]{2,1,0:T(8,128)(2,1)}, u32[]{:S(2)}, u32[]{:S(2)}) %collective-permute-start.32) | collective-permute-done | bytes 819232 | tf_op jit(solution)/shard_map/ppermute | solution.py:208
  198.7 12.9 %collective-permute-done.40 = bf16[36,8,1152]{2,1,0:T(8,128)(2,1)S(1)} collective-permute-done((bf16[36,8,1152]{2,1,0:T(8,128)(2,1)S(1)}, bf16[36,8,1152]{2,1,0:T(8,128)(2,1)S(1)}, u32[]{:S(2)}, u32[]{:S(2)}) %collective-permute-start.40) | collective-permute-done | bytes 663584 | tf_op jit(solution)/shard_map/ppermute | solution.py:178
  221.1 14.9 %shard_map.214 = (bf16[144,8,4608]{2,1,0:T(8,128)(2,1)}, bf16[576,8,1152]{2,1,0:T(8,128)(2,1)}) custom-call(s32[16]{0:T(128)S(1)} %stack.84.origins_ref, bf16[72,8,1152]{2,1,0:T(8,128)(2,1)S(1)} %copy-done.8, bf16[72,8,1152]{2,1,0:T(8,128)(2,1)} %collective-permute-done.21.refs_1_, bf16[72,8,1152]{2,1,0:T(8,128)(2,1)} %collective-permute-done.26.refs_2_, ...), custom_call_target="tpu_custom_call" | custom-call | bytes 42467328 | tf_op jit(solution)/shard_map/pallas_call | solution.py:293
  240.0 14.6 %multiply_convert_fusion = (bf16[512,4608]{1,0:T(8,128)(2,1)}, f32[512,4608]{1,0:T(8,128)}) fusion(bf16[512,1152]{1,0:T(8,128)(2,1)S(1)} %add_convert_fusion.9.mine_ref, bf16[1152,4608]{1,0:T(8,128)(2,1)} %bitcast.129), kind=kOutput, calls=%fused_computation.9 | convolution fusion | flops 5457051648 | bytes 25952256 | tf_op jit(solution)/shard_map/dot_general | solution.py:548
  268.5 12.3 %add_convert_fusion.8 = (bf16[512,1152]{1,0:T(8,128)(2,1)S(1)}, f32[512,1152]{1,0:T(8,128)}) fusion(f32[512,1152]{1,0:T(8,128)S(1)} %copy-done.28, f32[1152]{0:T(1024)S(1)} %get-tuple-element.284, bf16[512,4608]{1,0:T(8,128)(2,1)} %get-tuple-element.168.mine_ref, bf16[4608,1152]{1,0:T(8,128)(2,1)} %bitcast.131), kind=kOutput, calls=%fused_computation.70 | convolution fusion | flops 5437587456 | bytes 21238272 | tf_op jit(solution)/shard_map/dot_general | solution.py:548
  319.5 9.5 %fusion.20 = bf16[512,2048]{1,0:T(8,128)(2,1)S(1)} fusion(f32[512,2048]{1,0:T(8,128)S(1)} %copy-done.88, bf16[512,2048]{1,0:T(8,128)(2,1)S(1)} %fusion.17, bf16[256,8,2048]{2,1,0:T(8,128)(2,1)} %get-tuple-element.179), kind=kOutput, calls=%fused_computation.28 | convolution fusion | flops 4305453056 | bytes 16777216 | tf_op jit(solution)/shard_map/ne,de->nd/dot_general | solution.py:552
  347.1 18.1 %shard_map.216 = (bf16[288,1152]{1,0:T(8,128)(2,1)S(1)}, f32[576,1152]{1,0:T(8,128)}, f32[576,1152]{1,0:T(8,128)}, f32[576,1152]{1,0:T(8,128)}, f32[288,1152]{1,0:T(8,128)S(1)}) custom-call(s32[3,5]{1,0:T(4,128)S(1)} %get-tuple-element.297.spots_ref, bf16[512,4608]{1,0:T(8,128)(2,1)} %get-tuple-element.168.mine_ref, ...), custom_call_target="tpu_custom_call" | custom-call | flops 6794772480 | bytes 22413312 | tf_op jit(solution)/shard_map/pallas_call | solution.py:447
  365.3 16.3 %fusion.6.grad_ref = bf16[512,4608]{1,0:T(8,128)(2,1)} fusion(f32[512,4608]{1,0:T(8,128)} %get-tuple-element.301, bf16[512,1152]{1,0:T(8,128)(2,1)S(1)} %copy-done.26, bf16[4608,1152]{1,0:T(8,128)(2,1)} %bitcast.132), kind=kOutput, calls=%fused_computation.8 | convolution fusion | flops 5483003904 | bytes 25952256 | tf_op jit(solution)/shard_map/ne,de->nd/dot_general | solution.py:552
  385.7 12.8 %multiply_reduce_fusion.1 = (f32[1152]{0:T(1024)}, f32[512]{0:T(512)S(1)}, f32[1152]{0:T(1024)}, f32[512,1152]{1,0:T(8,128)S(1)}) fusion(f32[512,1152]{1,0:T(8,128)S(1)} %copy-done.29, f32[512]{0:T(512)S(1)} %copy-done.75, f32[512]{0:T(512)S(1)} %copy-done.70, f32[1152]{0:T(1024)S(1)} %copy-done.61, bf16[512,4608]{1,0:T(8,128)(2,1)} %fusion.6.grad_ref, ...), kind=kOutput, calls=%fused_computation.63 | convolution fusion | flops 5440534016 | bytes 20073984 | tf_op jit(solution)/shard_map/ne,de->nd/dot_general | solution.py:552
  406.6 13.4 %shard_map.217 = (bf16[72,4608]{1,0:T(8,128)(2,1)S(1)}, f32[144,4608]{1,0:T(8,128)}, f32[144,4608]{1,0:T(8,128)}, f32[144,4608]{1,0:T(8,128)}, f32[72,4608]{1,0:T(8,128)S(1)}) custom-call(s32[3,5]{1,0:T(4,128)S(1)} %get-tuple-element.296.spots_ref, bf16[512,1152]{1,0:T(8,128)(2,1)S(1)} %copy-done.16, bf16[512,1152]{1,0:T(8,128)(2,1)} %collective-permute-done.58.theirs_ref, ...), custom_call_target="tpu_custom_call" | custom-call | flops 6794772480 | bytes 22413312 | tf_op jit(solution)/shard_map/pallas_call | solution.py:447
  425.6 22.6 %collective-permute-done.59 = bf16[72,4608]{1,0:T(8,128)(2,1)S(1)} collective-permute-done((bf16[72,4608]{1,0:T(8,128)(2,1)S(1)}, bf16[72,4608]{1,0:T(8,128)(2,1)S(1)}, u32[]{:S(2)}, u32[]{:S(2)}) %collective-permute-start.59) | collective-permute-done | bytes 663584 | tf_op jit(solution)/shard_map/ppermute | solution.py:474
  454.1 39.8 %shard_map.218 = (bf16[512,1152]{1,0:T(8,128)(2,1)S(1)}, f32[512,1152]{1,0:T(8,128)S(1)}, f32[512,1152]{1,0:T(8,128)}, f32[512,2304]{1,0:T(8,128)}) custom-call(s32[1]{0:T(128)S(6)} %convert_element_type.241.long_ref, bf16[512,3456]{1,0:T(8,128)(2,1)} %copy-done.9, bf16[512,3456]{1,0:T(8,128)(2,1)} %copy-done.9, bf16[512,3456]{1,0:T(8,128)(2,1)} %copy-done.9, ...), custom_call_target="tpu_custom_call" | custom-call | flops 21474836480 | bytes 23592960 | tf_op jit(solution)/shard_map/pallas_call | solution.py:148
  496.3 9.2 %convolution_convert_fusion = bf16[2048,2048]{1,0:T(8,128)(2,1)} fusion(bf16[512,2048]{1,0:T(8,128)(2,1)S(1)} %copy-done.91, f32[512,2048]{1,0:T(8,128)} %copy-done.87), kind=kOutput, calls=%fused_computation.14 | convolution fusion | flops 4304404480 | bytes 14680064 | tf_op jit(solution)/shard_map/nd,ne->de/dot_general | solution.py:406
  519.1 9.1 %collective-permute-done.64 = bf16[72,1152]{1,0:T(8,128)(2,1)S(1)} collective-permute-done((bf16[72,1152]{1,0:T(8,128)(2,1)S(1)}, bf16[72,1152]{1,0:T(8,128)(2,1)S(1)}, u32[]{:S(2)}, u32[]{:S(2)}) %collective-permute-start.64) | collective-permute-done | bytes 165920 | tf_op jit(solution)/shard_map/ppermute | solution.py:474
  536.7 26.1 %collective-permute-done.67 = bf16[144,4608]{1,0:T(8,128)(2,1)S(1)} collective-permute-done((bf16[144,4608]{1,0:T(8,128)(2,1)S(1)}, bf16[144,4608]{1,0:T(8,128)(2,1)S(1)}, u32[]{:S(2)}, u32[]{:S(2)}) %collective-permute-start.67) | collective-permute-done | bytes 1327136 | tf_op jit(solution)/shard_map/ppermute | solution.py:474
  562.8 10.7 %collective-permute-done.68 = bf16[144,1152]{1,0:T(8,128)(2,1)} collective-permute-done((bf16[144,1152]{1,0:T(8,128)(2,1)S(1)}, bf16[144,1152]{1,0:T(8,128)(2,1)}, u32[]{:S(2)}, u32[]{:S(2)}) %collective-permute-start.68) | collective-permute-done | bytes 331808 | tf_op jit(solution)/shard_map/ppermute | solution.py:474
  582.3 11.8 %collective-permute-start.71 = (f32[3456]{0:T(1024)S(1)}, f32[3456]{0:T(1024)S(1)}, u32[]{:S(2)}, u32[]{:S(2)}) collective-permute-start(f32[3456]{0:T(1024)S(1)} %dynamic_slice.65), channel_id=1, source_target_pairs={{0,8},{8,0},{1,9},{9,1},{2,10},{10,2},{3,11},{11,3},{4,12},{12,4},... | collective-permute-start | bytes 41480 | tf_op jit(solution)/shard_map/ppermute | solution.py:174
  617.0 15.1 %collective-permute-done.76 = f32[1,1152]{1,0:T(1,128)S(1)} collective-permute-done((f32[1,1152]{1,0:T(1,128)S(1)}, f32[1,1152]{1,0:T(1,128)S(1)}, u32[]{:S(2)}, u32[]{:S(2)}) %collective-permute-start.76) | collective-permute-done | bytes 4640 | tf_op jit(solution)/shard_map/ppermute | solution.py:174
  654.2 11.0 %shard_map.220 = (bf16[72,3456]{1,0:T(8,128)(2,1)S(1)}, f32[144,3456]{1,0:T(8,128)S(1)}, f32[144,3456]{1,0:T(8,128)}, f32[144,3456]{1,0:T(8,128)}, f32[72,3456]{1,0:T(8,128)S(1)}) custom-call(s32[3,5]{1,0:T(4,128)S(1)} %get-tuple-element.296.spots_ref, bf16[512,1152]{1,0:T(8,128)(2,1)} %fusion.33.mine_ref, ...), custom_call_target="tpu_custom_call" | custom-call | flops 5096079360 | bytes 17399808 | tf_op jit(solution)/shard_map/pallas_call | solution.py:447
  678.3 10.6 %collective-permute-done.83 = bf16[144,3456]{1,0:T(8,128)(2,1)S(1)} collective-permute-done((bf16[144,3456]{1,0:T(8,128)(2,1)S(1)}, bf16[144,3456]{1,0:T(8,128)(2,1)S(1)}, u32[]{:S(2)}, u32[]{:S(2)}) %collective-permute-start.83) | collective-permute-done | bytes 995360 | tf_op jit(solution)/shard_map/ppermute | solution.py:474
  (524 shorter events, 358.8 us)
Async XLA Ops:
  7.2 295.2 %all-gather.2.cloned.1.call-start = ((), (), s32[]{:S(2)}) async-start(), calls=%async_computation.3 | async-start | bytes 3342336 | tf_op jit(solution)/shard_map/all_gather | solution.py:586
  12.6 45.8 %collective-permute-start.11 = (bf16[36,8,1152]{2,1,0:T(8,128)(2,1)S(1)}, bf16[36,8,1152]{2,1,0:T(8,128)(2,1)}, u32[]{:S(2)}, u32[]{:S(2)}) collective-permute-start(bf16[36,8,1152]{2,1,0:T(8,128)(2,1)S(1)} %pad_maximum_fusion.4.refs_0_), channel_id=1, source_target_pairs={{0,2},{1,5},{4,0},{5,9},{8,4},{9,13},{12,8},{13,15},{14,12},{15,11... | collective-permute-start | bytes 1990664 | tf_op jit(solution)/shard_map/ppermute | solution.py:208
  129.7 34.1 %collective-permute-start.27 = (bf16[72,8,1152]{2,1,0:T(8,128)(2,1)}, bf16[72,8,1152]{2,1,0:T(8,128)(2,1)S(1)}, u32[]{:S(2)}, u32[]{:S(2)}) collective-permute-start(bf16[72,8,1152]{2,1,0:T(8,128)(2,1)} %collective-permute-done.26.refs_2_), channel_id=1, source_target_pairs={{0,1},{1,0},{2,3},{3,2},{4,5},{5,4},{6,7},{7,6},{8,9},{9,8},{10,11... | collective-permute-start | bytes 3981320 | tf_op jit(solution)/shard_map/ppermute | solution.py:174
  129.7 34.1 %collective-permute-start.28 = (bf16[72,8,1152]{2,1,0:T(8,128)(2,1)}, bf16[72,8,1152]{2,1,0:T(8,128)(2,1)S(1)}, u32[]{:S(2)}, u32[]{:S(2)}) collective-permute-start(bf16[72,8,1152]{2,1,0:T(8,128)(2,1)} %collective-permute-done.26.refs_2_), channel_id=1, source_target_pairs={{0,4},{1,3},{4,8},{5,1},{8,12},{9,5},{12,14},{13,9},{14,10},{15,13... | collective-permute-start | bytes 3981320 | tf_op jit(solution)/shard_map/ppermute | solution.py:208
  131.2 32.5 %collective-permute-start.29 = (bf16[72,8,1152]{2,1,0:T(8,128)(2,1)}, bf16[72,8,1152]{2,1,0:T(8,128)(2,1)}, u32[]{:S(2)}, u32[]{:S(2)}) collective-permute-start(bf16[72,8,1152]{2,1,0:T(8,128)(2,1)} %collective-permute-done.26.refs_2_), channel_id=1, source_target_pairs={{0,16},{16,0},{1,17},{17,1},{2,18},{18,2},{3,19},{19,3},{4,20},{20... | collective-permute-start | bytes 3981320 | tf_op jit(solution)/shard_map/ppermute | solution.py:178
  133.7 31.3 %collective-permute-start.30 = (bf16[50,8,1024]{2,1,0:T(8,128)(2,1)S(1)}, bf16[50,8,1024]{2,1,0:T(8,128)(2,1)S(1)}, u32[]{:S(2)}, u32[]{:S(2)}) collective-permute-start(bf16[50,8,1024]{2,1,0:T(8,128)(2,1)S(1)} %pad_maximum_fusion.2.refs_0_), channel_id=1, source_target_pairs={{0,1},{1,0},{2,3},{3,2},{4,5},{5,4},{6,7},{7,6},{8,9},{9,8},{10,11... | collective-permute-start | bytes 2457608 | tf_op jit(solution)/shard_map/ppermute | solution.py:174
  134.2 31.8 %collective-permute-start.31 = (bf16[50,8,1024]{2,1,0:T(8,128)(2,1)S(1)}, bf16[50,8,1024]{2,1,0:T(8,128)(2,1)}, u32[]{:S(2)}, u32[]{:S(2)}) collective-permute-start(bf16[50,8,1024]{2,1,0:T(8,128)(2,1)S(1)} %pad_maximum_fusion.2.refs_0_), channel_id=1, source_target_pairs={{0,4},{1,3},{4,8},{5,1},{8,12},{9,5},{12,14},{13,9},{14,10},{15,13... | collective-permute-start | bytes 2457608 | tf_op jit(solution)/shard_map/ppermute | solution.py:208
  164.4 31.2 %collective-permute-start.36 = (bf16[72,8,1152]{2,1,0:T(8,128)(2,1)S(1)}, bf16[72,8,1152]{2,1,0:T(8,128)(2,1)}, u32[]{:S(2)}, u32[]{:S(2)}) collective-permute-start(bf16[72,8,1152]{2,1,0:T(8,128)(2,1)S(1)} %collective-permute-done.28.refs_3_), channel_id=1, source_target_pairs={{0,16},{16,0},{1,17},{17,1},{2,18},{18,2},{3,19},{19,3},{4,20},{20... | collective-permute-start | bytes 3981320 | tf_op jit(solution)/shard_map/ppermute | solution.py:178
  212.0 481.9 %reduce-scatter.8.cloned.1.call-start = ((), (), s32[]{:S(2)}) async-start(), calls=%async_computation.6 | async-start | bytes 3342336 | tf_op jit(solution)/shard_map/reduce_scatter | solution.py:407
  258.9 86.9 %collective-permute-start.54 = (bf16[512,4608]{1,0:T(8,128)(2,1)}, bf16[512,4608]{1,0:T(8,128)(2,1)}, u32[]{:S(2)}, u32[]{:S(2)}) collective-permute-start(bf16[512,4608]{1,0:T(8,128)(2,1)} %get-tuple-element.168.mine_ref), channel_id=1, source_target_pairs={{0,1},{1,0},{2,3},{3,2},{4,5},{5,4},{6,7},{7,6},{8,9},{9,8},{10,11... | collective-permute-start | bytes 14155784 | tf_op jit(solution)/shard_map/ppermute | solution.py:174
  312.2 381.7 %reduce-scatter.4.cloned.1.call-start = ((), (), s32[]{:S(2)}) async-start(), calls=%async_computation.4 | async-start | bytes 5013504 | tf_op jit(solution)/shard_map/reduce_scatter | solution.py:407
  338.1 316.0 %collective-permute-start.81 = (bf16[512,1152]{1,0:T(8,128)(2,1)}, bf16[512,1152]{1,0:T(8,128)(2,1)}, u32[]{:S(2)}, u32[]{:S(2)}) collective-permute-start(bf16[512,1152]{1,0:T(8,128)(2,1)} %fusion.33.mine_ref), channel_id=1, source_target_pairs={{0,1},{1,0},{2,3},{3,2},{4,5},{5,4},{6,7},{7,6},{8,9},{9,8},{10,11... | collective-permute-start | bytes 3538952 | tf_op jit(solution)/shard_map/ppermute | solution.py:174
  338.1 171.4 %collective-permute-start.63 = (bf16[512,1152]{1,0:T(8,128)(2,1)}, bf16[512,1152]{1,0:T(8,128)(2,1)}, u32[]{:S(2)}, u32[]{:S(2)}) collective-permute-start(bf16[512,1152]{1,0:T(8,128)(2,1)} %get-tuple-element.146.mine_ref), channel_id=1, source_target_pairs={{0,1},{1,0},{2,3},{3,2},{4,5},{5,4},{6,7},{7,6},{8,9},{9,8},{10,11... | collective-permute-start | bytes 3538952 | tf_op jit(solution)/shard_map/ppermute | solution.py:174
  338.6 67.9 %collective-permute-start.58 = (bf16[512,1152]{1,0:T(8,128)(2,1)S(1)}, bf16[512,1152]{1,0:T(8,128)(2,1)}, u32[]{:S(2)}, u32[]{:S(2)}) collective-permute-start(bf16[512,1152]{1,0:T(8,128)(2,1)S(1)} %copy-done.16), channel_id=1, source_target_pairs={{0,1},{1,0},{2,3},{3,2},{4,5},{5,4},{6,7},{7,6},{8,9},{9,8},{10,11... | collective-permute-start | bytes 3538952 | tf_op jit(solution)/shard_map/ppermute | solution.py:174
  345.8 348.1 %reduce-scatter.6.cloned.1.call-start = ((), (), s32[]{:S(2)}) async-start(), calls=%async_computation.5 | async-start | bytes 8912896 | tf_op jit(solution)/shard_map/reduce_scatter | solution.py:407
  405.0 45.0 %collective-permute-start.60 = (bf16[576,1152]{1,0:T(8,128)(2,1)}, bf16[576,1152]{1,0:T(8,128)(2,1)S(1)}, u32[]{:S(2)}, u32[]{:S(2)}) collective-permute-start(bf16[576,1152]{1,0:T(8,128)(2,1)} %add_convert_fusion.4), channel_id=1, source_target_pairs={{0,4},{1,3},{4,8},{5,1},{8,12},{9,5},{12,14},{13,9},{14,10},{15,13... | collective-permute-start | bytes 3981320 | tf_op jit(solution)/shard_map/ppermute | solution.py:474
  424.4 29.7 %collective-permute-start.61 = (bf16[512,1152]{1,0:T(8,128)(2,1)S(1)}, bf16[512,1152]{1,0:T(8,128)(2,1)S(1)}, u32[]{:S(2)}, u32[]{:S(2)}) collective-permute-start(bf16[512,1152]{1,0:T(8,128)(2,1)S(1)} %multiply_convert_fusion.3.grad_ref), channel_id=1, source_target_pairs={{0,1},{1,0},{2,3},{3,2},{4,5},{5,4},{6,7},{7,6},{8,9},{9,8},{10,11... | collective-permute-start | bytes 3538952 | tf_op jit(solution)/shard_map/ppermute | solution.py:174
  451.6 65.6 %collective-permute-start.62 = (bf16[144,4608]{1,0:T(8,128)(2,1)}, bf16[144,4608]{1,0:T(8,128)(2,1)}, u32[]{:S(2)}, u32[]{:S(2)}) collective-permute-start(bf16[144,4608]{1,0:T(8,128)(2,1)} %add_convert_fusion.3), channel_id=1, source_target_pairs={{0,4},{1,3},{4,8},{5,1},{8,12},{9,5},{12,14},{13,9},{14,10},{15,13... | collective-permute-start | bytes 3981320 | tf_op jit(solution)/shard_map/ppermute | solution.py:474
  496.3 34.8 %collective-permute-start.65 = (f32[512,2304]{1,0:T(8,128)}, f32[512,2304]{1,0:T(8,128)}, u32[]{:S(2)}, u32[]{:S(2)}) collective-permute-start(f32[512,2304]{1,0:T(8,128)} %get-tuple-element.206), channel_id=1, source_target_pairs={{0,1},{1,0},{2,3},{3,2},{4,5},{5,4},{6,7},{7,6},{8,9},{9,8},{10,11... | collective-permute-start | bytes 14155784 | tf_op jit(solution)/shard_map/ppermute | solution.py:174
  528.3 34.5 %collective-permute-start.67 = (bf16[144,4608]{1,0:T(8,128)(2,1)S(1)}, bf16[144,4608]{1,0:T(8,128)(2,1)S(1)}, u32[]{:S(2)}, u32[]{:S(2)}) collective-permute-start(bf16[144,4608]{1,0:T(8,128)(2,1)S(1)} %add_convert_fusion.1), channel_id=1, source_target_pairs={{0,4},{1,3},{4,8},{5,1},{8,12},{9,5},{12,14},{13,9},{14,10},{15,13... | collective-permute-start | bytes 3981320 | tf_op jit(solution)/shard_map/ppermute | solution.py:474
  529.2 44.2 %collective-permute-start.68 = (bf16[144,1152]{1,0:T(8,128)(2,1)S(1)}, bf16[144,1152]{1,0:T(8,128)(2,1)}, u32[]{:S(2)}, u32[]{:S(2)}) collective-permute-start(bf16[144,1152]{1,0:T(8,128)(2,1)S(1)} %add_convert_fusion.15), channel_id=1, source_target_pairs={{0,4},{1,3},{4,8},{5,1},{8,12},{9,5},{12,14},{13,9},{14,10},{15,13... | collective-permute-start | bytes 995336 | tf_op jit(solution)/shard_map/ppermute | solution.py:474
  536.6 117.5 %collective-permute-start.70 = (bf16[512,3456]{1,0:T(8,128)(2,1)}, bf16[512,3456]{1,0:T(8,128)(2,1)}, u32[]{:S(2)}, u32[]{:S(2)}) collective-permute-start(bf16[512,3456]{1,0:T(8,128)(2,1)} %pad_maximum_fusion.grad_ref), channel_id=1, source_target_pairs={{0,1},{1,0},{2,3},{3,2},{4,5},{5,4},{6,7},{7,6},{8,9},{9,8},{10,11... | collective-permute-start | bytes 10616840 | tf_op jit(solution)/shard_map/ppermute | solution.py:174
  595.3 36.8 %collective-permute-start.88 = (bf16[144,1152]{1,0:T(8,128)(2,1)S(1)}, bf16[144,1152]{1,0:T(8,128)(2,1)S(1)}, u32[]{:S(2)}, u32[]{:S(2)}) collective-permute-start(bf16[144,1152]{1,0:T(8,128)(2,1)S(1)} %add_convert_fusion.14), channel_id=1, source_target_pairs={{0,4},{1,3},{4,8},{5,1},{8,12},{9,5},{12,14},{13,9},{14,10},{15,13... | collective-permute-start | bytes 995336 | tf_op jit(solution)/shard_map/ppermute | solution.py:474
  614.2 39.1 %collective-permute-start.69 = (bf16[144,4608]{1,0:T(8,128)(2,1)S(1)}, bf16[144,4608]{1,0:T(8,128)(2,1)S(1)}, u32[]{:S(2)}, u32[]{:S(2)}) collective-permute-start(bf16[144,4608]{1,0:T(8,128)(2,1)S(1)} %add_convert_fusion), channel_id=1, source_target_pairs={{0,4},{1,3},{4,8},{5,1},{8,12},{9,5},{12,14},{13,9},{14,10},{15,13... | collective-permute-start | bytes 3981320 | tf_op jit(solution)/shard_map/ppermute | solution.py:474
  (175 other events, 2662.8 us)
Sparse Core Ops, SparseCore 0:
  212.1 49.3 all-gather.1
  312.3 67.0 reduce-scatter.7
  383.3 88.1 reduce-scatter.3
  505.6 112.4 reduce-scatter.5

commit v3 on v2

--- a/solution.py
+++ b/solution.py
@@ -216,6 +216,22 @@
     return jnp.where(spot < chips // 2, 2 * spot, 2 * (chips - 1 - spot) + 1)
 
 
+def onward(block):
+    return parted_hop(block, 1)
+
+
+def backward(block):
+    return parted_hop(block, -1)
+
+
+def core_swap(block):
+    return swapped(block, "fsdp", 0)
+
+
+def each(sends):
+    return lambda blocks: [send(block) for send, block in zip(sends, blocks)]
+
+
 def gathered(block):
     core = lax.axis_index("fsdp") % 2
     parity = (lax.axis_index("bins") + core) % 2
@@ -227,21 +243,23 @@
     step = 0
     while fresh:
         step += 1
-        flights = [(place, swapped(piece, "fsdp", 0), True) for place, piece in fresh]
+        flights = []
         if step < far:
-            flights.append((step, parted_hop(ahead[-1], 1), False))
+            flights.append((step, onward, ahead[-1], False))
         if step == far:
             part = lax.dynamic_slice_in_dim(ahead[-1], parity * half, half)
-            flights.append((far, parted_hop(part, 1), False))
+            flights.append((far, onward, part, False))
         if step <= near:
-            flights.append((-step, parted_hop(behind[-1], -1), False))
+            flights.append((-step, backward, behind[-1], False))
         if near < step - 1 < far:
-            flights.append((1 - step, bins_peer(ahead[step - 1]), False))
+            flights.append((1 - step, bins_peer, ahead[step - 1], False))
         if step == far + 1:
-            flights.append((far, bins_peer(arm), False))
-        arrived = yield [flight for _, flight, _ in flights]
+            flights.append((far, bins_peer, arm, False))
+        flights += [(place, core_swap, piece, True) for place, piece in fresh]
+        sends = [send for _, send, _, _ in flights]
+        arrived = yield each(sends), [piece for _, _, piece, _ in flights]
         fresh = []
-        for (place, _, swap), piece in zip(flights, arrived):
+        for (place, _, _, swap), piece in zip(flights, arrived):
             if swap:
                 peers[place] = piece
                 continue
@@ -324,7 +342,7 @@
     count, place = lax.axis_size("fsdp"), lax.axis_index("fsdp")
     step = 0
     while 1 << step < count:
-        other = yield swapped(block, "fsdp", step)
+        other = yield partial(swapped, axis="fsdp", apart=step), block
         upper = (place >> step) % 2 == 1
         block = jnp.where(
             upper, jnp.concatenate([other, block]), jnp.concatenate([block, other])
@@ -333,7 +351,7 @@
     return block
 
 
-def halved(block):
+def column_sums(block, columns_weight):
     count, place = lax.axis_size("fsdp"), lax.axis_index("fsdp")
     step = count.bit_length() - 1
     while step:
@@ -342,16 +360,14 @@
         length = block.shape[0] // 2
         sent = lax.dynamic_slice_in_dim(block, (1 - upper) * length, length)
         kept = lax.dynamic_slice_in_dim(block, upper * length, length)
-        block = kept + swapped(sent, "fsdp", step)
-    return block
-
-
-def group_sum(block):
-    step = 0
-    while 1 << step < lax.axis_size("fsdp"):
-        block = block + swapped(block, "fsdp", step)
+        block = kept + (yield partial(swapped, axis="fsdp", apart=step), sent)
+    columns = block.reshape(1, -1)
+    total = jnp.dot(columns, columns_weight.astype(jnp.float32).T, precision=HIGH)
+    across = yield bins_peer, columns
+    while 1 << step < count:
+        total = total + (yield partial(swapped, axis="fsdp", apart=step), total)
         step += 1
-    return block
+    return columns, across, total
 
 
 def core_rows(turned, core):
@@ -402,9 +418,13 @@
     return rounded + bins_peer(rounded.astype(jnp.bfloat16)).astype(jnp.float32)
 
 
-def scattered_grad(left, right):
+def scattered(block):
+    return lax.psum_scatter(block, "fsdp", scatter_dimension=0, tiled=True)
+
+
+def low_grad(left, right):
     total = jnp.einsum("nd,ne->de", left, right, preferred_element_type=jnp.float32)
-    return lax.psum_scatter(total.astype(jnp.bfloat16), "fsdp", scatter_dimension=0, tiled=True)
+    return total.astype(jnp.bfloat16)
 
 
 def parts_kernel(spots_ref, mine_ref, theirs_ref, grad_ref, other_ref, *refs):
@@ -474,57 +494,103 @@
     return lax.ppermute(block, "fsdp", pairs)
 
 
-def grad_chain(left, right, theirs=None):
-    rows = left.shape[1] // lax.axis_size("fsdp")
-    if rows % 8:
-        return full_grad(left, right)
+def bins_sum(part):
+    across = yield bins_peer, part
+    return part.astype(jnp.float32) + across.astype(jnp.float32)
+
+
+def grad_chain(pairs, theirs):
+    heights = [left.shape[1] // lax.axis_size("fsdp") for left, _ in pairs]
+    if any(rows % 8 for rows in heights):
+        return [full_grad(left, right) for left, right in pairs]
     core = lax.axis_index("fsdp") % 2
     way = 1 - 2 * core
     far = lax.axis_size("fsdp") // 4
-    if theirs is None:
-        theirs = swapped(left, "fsdp", 0)
-    other = yield swapped(right, "fsdp", 0)
+    others = yield each([core_swap] * len(pairs)), [right for _, right in pairs]
     steps = list(range(far, 0, -1))
     chips = [chip_at(far)] + [chip_at(way * apart) for apart in steps[1:]] + [chip_at(0)]
-    parts = grad_parts(left, theirs, right, other, chips)
-    arrived = yield core_hop(parts[0])
+    parts = [
+        grad_parts(left, peer, right, other, chips)
+        for (left, right), peer, other in zip(pairs, theirs, others)
+    ]
+
+    def joined(blocks):
+        return blocks[0] if len(blocks) == 1 else jnp.concatenate(blocks)
+
+    def split(block, times):
+        out, top = [], 0
+        for rows in heights:
+            out.append(block[top : top + times * rows])
+            top += times * rows
+        return out
+
+    arrived = yield core_hop, joined([part[0] for part in parts])
     for number in range(1, far):
         if number == 1:
-            first = jnp.where(core == 0, arrived, 0)
-            arrived = jnp.concatenate([first, jnp.where(core == 0, 0, arrived)])
-        arrived = yield core_hop((parts[number] + arrived).astype(jnp.bfloat16))
-    kept = lax.dynamic_slice_in_dim(arrived, core * rows, rows)
-    sent = lax.dynamic_slice_in_dim(arrived, (1 - core) * rows, rows)
-    back = yield swapped(sent, "fsdp", 0)
-    total = parts[far] + kept + back
-    rounded = lax.reduce_precision(total, 8, 7)
-    across = yield bins_peer(rounded.astype(jnp.bfloat16))
-    return rounded + across.astype(jnp.float32)
+            spread = []
+            for half in split(arrived, 1):
+                spread += [jnp.where(core == 0, half, 0), jnp.where(core == 0, 0, half)]
+            arrived = jnp.concatenate(spread)
+        sums = [part[number] + block for part, block in zip(parts, split(arrived, 2))]
+        arrived = yield core_hop, joined([block.astype(jnp.bfloat16) for block in sums])
+    kept = [lax.dynamic_slice_in_dim(block, core * rows, rows) for block, rows in zip(split(arrived, 2), heights)]
+    sent = [lax.dynamic_slice_in_dim(block, (1 - core) * rows, rows) for block, rows in zip(split(arrived, 2), heights)]
+    back = yield core_swap, joined(sent)
+    rounded = [
+        lax.reduce_precision(part[far] + mine + more, 8, 7)
+        for part, mine, more in zip(parts, kept, split(back, 1))
+    ]
+    across = yield bins_peer, joined([block.astype(jnp.bfloat16) for block in rounded])
+    return [block + more.astype(jnp.float32) for block, more in zip(rounded, split(across, 1))]
 
 
 class Chain:
     def __init__(self, steps):
         self.steps, self.flight, self.result = steps, (), None
-        self.push(None)
-
-    def push(self, arrived):
-        if self.flight is None:
-            return
+        self.take(None)
+        self.launch()
+
+    def take(self, arrived):
         try:
-            self.flight = self.steps.send(arrived)
+            self.send, self.block = self.steps.send(arrived)
         except StopIteration as stop:
-            self.flight, self.result = None, stop.value
-
-    def beat(self, *values):
+            self.send, self.block, self.result = None, None, stop.value
+
+    def launch(self):
+        self.flight = None if self.send is None else self.send(self.block)
+
+    def push(self):
         if self.flight is not None:
-            values, arrived = lax.optimization_barrier((values, self.flight))
-            self.push(arrived)
-        return values if len(values) > 1 else values[0]
+            self.take(self.flight)
+            self.launch()
 
     def finish(self):
         while self.flight is not None:
-            self.push(self.flight)
+            self.push()
         return self.result
+
+
+def arrive(values, *chains):
+    chains = [chain for chain in chains if chain.flight is not None]
+    if not chains:
+        return values
+    values, flights = lax.optimization_barrier((values, [chain.flight for chain in chains]))
+    for chain, flight in zip(chains, flights):
+        chain.take(flight)
+    return values
+
+
+def depart(values, *chains):
+    ready = [(chain.block, chain.result) for chain in chains]
+    values, ready = lax.optimization_barrier((values, ready))
+    for chain, (chain.block, chain.result) in zip(chains, ready):
+        chain.launch()
+    return values
+
+
+def beats(values, *chains):
+    chains = [chain for chain in chains if chain.flight is not None]
+    return depart(arrive(values, *chains), *chains) if chains else values
 
 
 def full_grad(left, right):
@@ -579,38 +645,40 @@
     first_set = Chain(whole([w_qkv, w_out], width))
     mod_chain = Chain(doubled(mod_cols.reshape(-1)))
     for _ in range(2):
-        mod_chain.push(mod_chain.flight)
-        first_set.push(first_set.flight)
-    w_fc1, w_fc2, w_proj3 = first_set.beat(w_fc1, w_fc2, w_proj3)
+        first_set.push()
+        mod_chain.push()
+    w_fc1, w_fc2, w_proj3 = beats((w_fc1, w_fc2, w_proj3), first_set)
     second_set = Chain(whole([w_fc1, w_fc2], width))
     head_third = lax.all_gather(w_proj3, "fsdp", axis=0, tiled=True)
     modulation = mod_chain.finish().reshape(6, width)
     full_qkv, full_out = first_set.finish()
-    full_qkv, full_out = second_set.beat(full_qkv, full_out)
+    full_qkv, full_out = beats((full_qkv, full_out), second_set)
     h_one, norm_one_back = jax.vjp(modulate, tokens_f, modulation[0], modulation[1])
     in_one = h_one.astype(jnp.bfloat16)
     qkv_low = product(in_one, full_qkv).astype(jnp.bfloat16)
     peer_low = swapped(qkv_low[:, width:], "fsdp", 0)
-    qkv_low, peer_low, w_proj1, w_proj2 = second_set.beat(qkv_low, peer_low, w_proj1, w_proj2)
+    qkv_low, peer_low, w_proj1, w_proj2 = beats(
+        (qkv_low, peer_low, w_proj1, w_proj2), second_set
+    )
     third_set = Chain(whole([w_proj1, w_proj2], w_proj1.shape[1] // 2))
     place = lax.axis_index("fsdp")
     own_ids = lax.dynamic_slice_in_dim(segments, place * count, count)
     long = (own_ids[:1] == own_ids[count - 1 :]).astype(jnp.int32)
     attended, exact, _, logs = attend(long, qkv_low, peer_low, factor)
-    attended, exact, logs = second_set.beat(attended, exact, logs)
-    attended, exact, logs = third_set.beat(attended, exact, logs)
+    attended, exact, logs = beats((attended, exact, logs), second_set)
+    attended, exact, logs = beats((attended, exact, logs), third_set)
     branch_one = product(attended, full_out)
     resid_one = tokens_f + modulation[2] * branch_one
-    resid_one = second_set.beat(resid_one)
-    resid_one = third_set.beat(resid_one)
+    resid_one = beats(resid_one, second_set)
+    resid_one = beats(resid_one, third_set)
     full_fc1, full_fc2 = second_set.finish()
-    full_fc1, full_fc2 = third_set.beat(full_fc1, full_fc2)
+    full_fc1, full_fc2 = beats((full_fc1, full_fc2), third_set)
     h_two, norm_two_back = jax.vjp(modulate, resid_one, modulation[3], modulation[4])
     in_two = h_two.astype(jnp.bfloat16)
     hidden_pre = product(in_two, full_fc1)
     hidden_act, gelu_back = jax.vjp(partial(jax.nn.gelu, approximate=True), hidden_pre)
     hidden_low = hidden_act.astype(jnp.bfloat16)
-    hidden_low = third_set.beat(hidden_low)
+    hidden_low = beats(hidden_low, third_set)
     branch_two = product(hidden_low, full_fc2)
     result = resid_one + modulation[5] * branch_two
     result_low = result.astype(jnp.bfloat16)
@@ -626,37 +694,46 @@
     )
     (grad_pred,) = cos_back(jnp.float32(-1.0))
     grad_pred_low = grad_pred.astype(jnp.bfloat16)
-    grad_third = scattered_grad(second_low, grad_pred_low)
+    total_third = low_grad(second_low, grad_pred_low)
+    grad_pred_low, total_third = lax.optimization_barrier((grad_pred_low, total_third))
+    part_third = scattered(total_third)
     (grad_second_pre,) = second_back(input_grad(grad_pred_low, head_third))
     grad_second_low = grad_second_pre.astype(jnp.bfloat16)
-    grad_second = scattered_grad(first_low, grad_second_low)
+    total_second = low_grad(first_low, grad_second_low)
+    grad_second_low, total_second = lax.optimization_barrier((grad_second_low, total_second))
+    part_second = scattered(total_second)
     (grad_first_pre,) = first_back(input_grad(grad_second_low, head_second))
     grad_first_low = grad_first_pre.astype(jnp.bfloat16)
-    grad_first = scattered_grad(result_low, grad_first_low)
     d_result = cotangent.astype(jnp.float32) + input_grad(grad_first_low, head_first)
+    total_first = low_grad(result_low, grad_first_low)
+    d_result, total_first = lax.optimization_barrier((d_result, total_first))
+    part_first = scattered(total_first)
     grad_gate_two = jnp.sum(d_result * branch_two, axis=0)
     d_branch_two = (d_result * modulation[5]).astype(jnp.bfloat16)
-    chain_fc2 = Chain(grad_chain(hidden_low, d_branch_two, hidden_peer))
-    d_branch_two = chain_fc2.beat(d_branch_two)
+    chain_fc2 = Chain(grad_chain([(hidden_low, d_branch_two)], [hidden_peer]))
     (d_pre,) = gelu_back(input_grad(d_branch_two, full_fc2))
     d_pre_low = d_pre.astype(jnp.bfloat16)
-    d_pre_low = chain_fc2.beat(d_pre_low)
-    chain_fc1 = Chain(grad_chain(in_two, d_pre_low, in_two_peer))
-    d_resid_part, grad_shift_two, grad_scale_two = norm_two_back(input_grad(d_pre_low, full_fc1))
-    d_resid_part = chain_fc1.beat(chain_fc2.beat(d_resid_part))
+    d_pre_low = beats(d_pre_low, chain_fc2)
+    d_pre_low, part_third = lax.optimization_barrier((d_pre_low, part_third))
+    chain_third = Chain(bins_sum(part_third))
+    chain_fc1 = Chain(grad_chain([(in_two, d_pre_low)], [in_two_peer]))
+    d_in_two = input_grad(d_pre_low, full_fc1)
+    d_resid_part, grad_shift_two, grad_scale_two = norm_two_back(d_in_two)
     d_resid = d_result + d_resid_part
     grad_gate_one = jnp.sum(d_resid * branch_one, axis=0)
     d_branch_one = (d_resid * modulation[2]).astype(jnp.bfloat16)
-    chain_out = Chain(grad_chain(attended, d_branch_one, attended_peer))
-    d_branch_one = chain_fc1.beat(d_branch_one)
+    d_branch_one, d_resid = beats((d_branch_one, d_resid), chain_fc2)
+    chain_out = Chain(grad_chain([(attended, d_branch_one)], [attended_peer]))
+    d_branch_one = beats(d_branch_one, chain_fc1)
     d_attended = input_grad(d_branch_one, full_out).astype(jnp.bfloat16)
-    d_attended = chain_out.beat(chain_fc2.beat(d_attended))
-    d_queries, d_keys, d_values, d_peer = attend_back(
-        long, qkv_low, peer_low, d_attended, exact, logs, factor
+    d_attended = beats(d_attended, chain_out)
+    d_attended = beats(d_attended, chain_fc2, chain_third)
+    busy = [chain for chain in (chain_fc2, chain_fc1) if chain.flight is not None]
+    d_queries, d_keys, d_values, d_peer = arrive(
+        attend_back(long, qkv_low, peer_low, d_attended, exact, logs, factor), *busy
     )
     from_peer = swapped(d_peer, "fsdp", 0)
-    d_queries = chain_out.beat(chain_fc1.beat(d_queries))
-    from_peer = chain_fc2.beat(from_peer)
+    d_queries = depart(d_queries, *busy)
     d_qkv = jnp.concatenate(
         [
             d_queries,
@@ -665,19 +742,12 @@
         ],
         axis=1,
     )
-    chain_qkv = Chain(grad_chain(in_one, d_qkv, in_one_peer))
-    d_qkv = chain_out.beat(chain_fc1.beat(d_qkv))
-    d_tok_part, grad_shift_one, grad_scale_one = norm_one_back(input_grad(d_qkv, full_qkv))
-    d_tok_part = chain_qkv.beat(chain_fc1.beat(d_tok_part))
-    d_tok_part, head_parts = lax.optimization_barrier(
-        (d_tok_part, (grad_first, grad_second, grad_third))
-    )
-    grad_first, grad_second, grad_third = (
-        both_groups(part.astype(jnp.float32)) for part in head_parts
-    )
-    grad_tokens = d_resid + d_tok_part
-    grad_fc2, grad_out = chain_fc2.finish(), chain_out.finish()
-    grad_fc1, grad_qkv = chain_fc1.finish(), chain_qkv.finish()
+    chain_qkv = Chain(grad_chain([(in_one, d_qkv)], [in_one_peer]))
+    d_in_one = input_grad(d_qkv, full_qkv)
+    d_in_one = beats(d_in_one, chain_qkv)
+    d_in_one, part_second = lax.optimization_barrier((d_in_one, part_second))
+    chain_second = Chain(bins_sum(part_second))
+    d_tok_part, grad_shift_one, grad_scale_one = norm_one_back(d_in_one)
     d_modulation = jnp.stack(
         [
             grad_shift_one,
@@ -688,12 +758,34 @@
             grad_gate_two,
         ]
     ).reshape(6 * width)
-    mod_grad_cols = halved(d_modulation).reshape(1, -1)
-    cond_part = jnp.dot(mod_grad_cols, w_ada.astype(jnp.float32).T, precision=HIGH)
-    (grad_condition,) = silu_back(group_sum(cond_part))
+    grad_tokens = d_resid + d_tok_part
+    chain_mod = Chain(column_sums(d_modulation, w_ada))
+    rounds = (
+        (chain_fc2, chain_fc1, chain_out, chain_mod),
+        (chain_qkv, chain_fc2, chain_mod, chain_second),
+        (chain_fc1, chain_out, chain_mod),
+        (chain_qkv, chain_mod),
+        (chain_fc1, chain_out, chain_fc2, chain_mod),
+        (chain_qkv, chain_fc1, chain_out, chain_mod),
+    )
+    for number, chains in enumerate(rounds):
+        grad_tokens = beats(grad_tokens, *chains)
+        if number == 2:
+            grad_tokens, part_first = lax.optimization_barrier((grad_tokens, part_first))
+            chain_first = Chain(bins_sum(part_first))
+    grad_tokens = beats(grad_tokens, chain_qkv, chain_first, chain_mod)
+    grad_tokens = beats(grad_tokens, chain_qkv, chain_fc1, chain_out, chain_mod)
+    grad_first, grad_second, grad_third = (
+        chain.finish() for chain in (chain_first, chain_second, chain_third)
+    )
+    mod_grad_cols, other_cols, cond_total = chain_mod.finish()
+    (grad_qkv,), (grad_fc1,), (grad_out,), (grad_fc2,) = (
+        chain.finish() for chain in (chain_qkv, chain_fc1, chain_out, chain_fc2)
+    )
+    (grad_condition,) = silu_back(cond_total)
     group = lax.axis_index("bins")
     cond_low_f = cond_low.astype(jnp.float32)
-    other_cond, other_cols = bins_peer(cond_low_f), bins_peer(mod_grad_cols)
+    other_cond = bins_peer(cond_low_f)
     first_cond = jnp.where(group == 0, cond_low_f, other_cond)
     last_cond = jnp.where(group == 0, other_cond, cond_low_f)
     first_cols = jnp.where(group == 0, mod_grad_cols, other_cols)

time: 758 us -> 727 us (0.959)
  waiting for transfers between devices: 278 us -> 214 us
  other arithmetic: 54.2 us -> 76.8 us
  local copies, waits for them, and re-layouts: 30.5 us -> 40.2 us
  starting transfers between devices: 91.5 us -> 100 us
    ppermute x16, waiting for transfers between devices: 105 us -> 41.8 us  [core_hop(): return lax.ppermute(block, 'fsdp', pairs)]
    ppermute x18, waiting for transfers between devices: 64 us -> 91.9 us  [bins_peer(): return lax.ppermute(block, 'bins', [(0, 1), (1, 0)])]
    ppermute x15, waiting for transfers between devices: 59.3 us -> 44.5 us  [parted_hop(): return lax.ppermute(block, ('bins', 'fsdp'), pairs)]
    ppermute x50, waiting for transfers between devices: 50.1 us -> 35.4 us  [swapped(): return lax.ppermute(block, axis, route)]
    convert_element_type x19 -> x17, other arithmetic: 16.3 us -> 30.4 us  [the longest x16 30.3 us: grad_chain(): block.astype(jnp.bfloat16)]
    ppermute x16, starting transfers between devices: 25.1 us -> 38.6 us  [core_hop(): return lax.ppermute(block, 'fsdp', pairs)]
    dot_general x7, matrix products: 57.9 us -> 66.5 us  [input_grad(): jnp.einsum('ne,de->nd', grad, weight, preferred_element_type=jnp.float32)]
    dot_general x8, matrix products: 55.6 us -> 47.5 us  [product(): return jnp.dot(left, right, preferred_element_type=jnp.float32)]
  transfers between devices with their start and end apart: 103 -> 103, of which waited for: 41 -> 38; matrix products, arithmetic and copies ran while one was open for 25% -> 28% of each run, Pallas kernels for 19% -> 19%
where the time goes in v3:
time: 727 us; the launch traced here: 717 us
  waiting for transfers between devices  214 us (29%)
  Pallas kernels  139 us (19%)
  matrix products  129 us (18%)
  starting transfers between devices  100 us (14%)
  other arithmetic  76.8 us (11%)
  local copies, waits for them, and re-layouts  40.2 us (6%)
  between operations  17.4 us (2%)
    ppermute x18, waiting for transfers between devices, bins_peer(): return lax.ppermute(block, 'bins', [(0, 1), (1, 0)])  91.9 us
    dot_general x7, matrix products, input_grad(): jnp.einsum('ne,de->nd', grad, weight, preferred_element_type=jnp.float32)  66.5 us
    pallas_call x4, Pallas kernels, grad_parts(): pl.pallas_call(parts_kernel, out_shape=[jax.ShapeDtypeStruct((k, columns)...  47.8 us
    dot_general x8, matrix products, product(): return jnp.dot(left, right, preferred_element_type=jnp.float32)  47.5 us
    ppermute x15, waiting for transfers between devices, parted_hop(): return lax.ppermute(block, ('bins', 'fsdp'), pairs)  44.5 us
    ppermute x16, waiting for transfers between devices, core_hop(): return lax.ppermute(block, 'fsdp', pairs)  41.8 us
    pallas_call x1, Pallas kernels, attend_back(): pl.pallas_call(partial(attend_back_kernel, factor), out_shape=[jax.ShapeD...  39.6 us
    ppermute x16, starting transfers between devices, core_hop(): return lax.ppermute(block, 'fsdp', pairs)  38.6 us
  transfers between devices with their start and end apart: 103, of which 38 were waited for; matrix products, arithmetic and copies ran while one was open for 28% of the time, Pallas kernels for 19%

profile of v3, /device:TPU:0, one launch (start us, length us, event | category | flops | bytes accessed | tf_op | source)
XLA Modules:
  0.0 717.2 jit_solution(14058730269463802388)
XLA Ops:
  13.9 13.8 %collective-permute-done.4.refs_1_ = bf16[36,8,1152]{2,1,0:T(8,128)(2,1)S(1)} collective-permute-done((bf16[36,8,1152]{2,1,0:T(8,128)(2,1)S(1)}, bf16[36,8,1152]{2,1,0:T(8,128)(2,1)S(1)}, u32[]{:S(2)}, u32[]{:S(2)}) %collective-permute-start.4) | collective-permute-done | bytes 663584 | tf_op jit(solution)/shard_map/ppermute | solution.py:208
  31.1 7.8 %collective-permute-done.5.refs_2_ = bf16[36,8,1152]{2,1,0:T(8,128)(2,1)} collective-permute-done((bf16[36,8,1152]{2,1,0:T(8,128)(2,1)S(1)}, bf16[36,8,1152]{2,1,0:T(8,128)(2,1)}, u32[]{:S(2)}, u32[]{:S(2)}) %collective-permute-start.5) | collective-permute-done | bytes 663584 | tf_op jit(solution)/shard_map/ppermute | solution.py:208
  69.7 15.0 %collective-permute-done.10 = bf16[18,8,1152]{2,1,0:T(8,128)(2,1)S(1)} collective-permute-done((bf16[18,8,1152]{2,1,0:T(8,128)(2,1)S(1)}, bf16[18,8,1152]{2,1,0:T(8,128)(2,1)S(1)}, u32[]{:S(2)}, u32[]{:S(2)}) %collective-permute-start.10) | collective-permute-done | bytes 331808 | tf_op jit(solution)/shard_map/ppermute | solution.py:178
  113.5 13.8 %collective-permute-done.24.refs_2_ = bf16[72,8,1152]{2,1,0:T(8,128)(2,1)S(1)} collective-permute-done((bf16[72,8,1152]{2,1,0:T(8,128)(2,1)}, bf16[72,8,1152]{2,1,0:T(8,128)(2,1)S(1)}, u32[]{:S(2)}, u32[]{:S(2)}) %collective-permute-start.24) | collective-permute-done | bytes 1327136 | tf_op jit(solution)/shard_map/ppermute | solution.py:208
  133.3 24.5 %shard_map.213 = (bf16[512,1152]{1,0:T(8,128)(2,1)S(1)}, f32[512,1152]{1,0:T(8,128)S(1)}, bf16[1152,512]{1,0:T(8,128)(2,1)}, f32[16,512]{1,0:T(8,128)S(1)}) custom-call(s32[1]{0:T(128)S(6)} %convert_element_type.232.long_ref, bf16[512,3456]{1,0:T(8,128)(2,1)S(1)} %copy-done.10, bf16[512,3456]{1,0:T(8,128)(2,1)S(1)} %copy-done.10, ...), custom_call_target="tpu_custom_call" | custom-call | flops 8589934592 | bytes 9437184 | tf_op jit(solution)/shard_map/pallas_call | solution.py:81
  173.5 16.2 %collective-permute-done.34.refs_7_ = bf16[72,8,1152]{2,1,0:T(8,128)(2,1)} collective-permute-done((bf16[72,8,1152]{2,1,0:T(8,128)(2,1)S(1)}, bf16[72,8,1152]{2,1,0:T(8,128)(2,1)}, u32[]{:S(2)}, u32[]{:S(2)}) %collective-permute-start.34) | collective-permute-done | bytes 1327136 | tf_op jit(solution)/shard_map/ppermute | solution.py:178
  192.9 12.6 %collective-permute-done.40 = bf16[36,8,1152]{2,1,0:T(8,128)(2,1)S(1)} collective-permute-done((bf16[36,8,1152]{2,1,0:T(8,128)(2,1)S(1)}, bf16[36,8,1152]{2,1,0:T(8,128)(2,1)S(1)}, u32[]{:S(2)}, u32[]{:S(2)}) %collective-permute-start.40) | collective-permute-done | bytes 663584 | tf_op jit(solution)/shard_map/ppermute | solution.py:178
  216.1 14.5 %shard_map.214 = (bf16[144,8,4608]{2,1,0:T(8,128)(2,1)}, bf16[576,8,1152]{2,1,0:T(8,128)(2,1)}) custom-call(s32[16]{0:T(128)S(1)} %stack.84.origins_ref, bf16[72,8,1152]{2,1,0:T(8,128)(2,1)S(1)} %copy-done.8, bf16[72,8,1152]{2,1,0:T(8,128)(2,1)} %collective-permute-done.20.refs_1_, bf16[72,8,1152]{2,1,0:T(8,128)(2,1)S(1)} %copy-done.14, ...), custom_call_target="tpu_custom_call" | custom-call | bytes 42467328 | tf_op jit(solution)/shard_map/pallas_call | solution.py:311
  234.7 13.4 %multiply_convert_fusion = (bf16[512,4608]{1,0:T(8,128)(2,1)}, f32[512,4608]{1,0:T(8,128)}) fusion(bf16[512,1152]{1,0:T(8,128)(2,1)} %add_convert_fusion.7.mine_ref, bf16[1152,4608]{1,0:T(8,128)(2,1)} %bitcast.122), kind=kOutput, calls=%fused_computation.9 | convolution fusion | flops 5457051648 | bytes 25952256 | tf_op jit(solution)/shard_map/dot_general | solution.py:614
  255.4 8.5 %collective-permute-done.50 = bf16[25,8,1024]{2,1,0:T(8,128)(2,1)S(1)} collective-permute-done((bf16[25,8,1024]{2,1,0:T(8,128)(2,1)S(1)}, bf16[25,8,1024]{2,1,0:T(8,128)(2,1)S(1)}, u32[]{:S(2)}, u32[]{:S(2)}) %collective-permute-start.50) | collective-permute-done | bytes 409632 | tf_op jit(solution)/shard_map/ppermute | solution.py:178
  264.1 9.2 %add_convert_fusion.6 = (bf16[512,1152]{1,0:T(8,128)(2,1)S(1)}, f32[512,1152]{1,0:T(8,128)}) fusion(f32[512,1152]{1,0:T(8,128)S(1)} %copy-done.39, f32[1152]{0:T(1024)S(1)} %get-tuple-element.558, bf16[512,4608]{1,0:T(8,128)(2,1)} %get-tuple-element.353.mine_ref, bf16[4608,1152]{1,0:T(8,128)(2,1)S(1)} %bitcast.127), kind=kOutput, calls=%fused_computation.74 | convolution fusion | flops 5437587456 | bytes 21238272 | tf_op jit(solution)/shard_map/dot_general | solution.py:614
  318.7 11.1 %fusion.20 = bf16[512,2048]{1,0:T(8,128)(2,1)S(1)} fusion(f32[512,2048]{1,0:T(8,128)} %copy-done.99, bf16[512,2048]{1,0:T(8,128)(2,1)} %copy-done.102, bf16[256,8,2048]{2,1,0:T(8,128)(2,1)} %get-tuple-element.364), kind=kOutput, calls=%fused_computation.28 | convolution fusion | flops 4305453056 | bytes 16777216 | tf_op jit(solution)/shard_map/ne,de->nd/dot_general | solution.py:618
  343.9 16.8 %fusion.6.grad_ref = bf16[512,4608]{1,0:T(8,128)(2,1)} fusion(f32[512,4608]{1,0:T(8,128)} %get-tuple-element.575, bf16[512,1152]{1,0:T(8,128)(2,1)S(1)} %multiply_convert_fusion.4.grad_ref, bf16[4608,1152]{1,0:T(8,128)(2,1)} %bitcast.124), kind=kOutput, calls=%fused_computation.8 | convolution fusion | flops 5483003904 | bytes 25952256 | tf_op jit(solution)/shard_map/ne,de->nd/dot_general | solution.py:618
  360.7 17.8 %shard_map.216 = (bf16[288,1152]{1,0:T(8,128)(2,1)S(1)}, f32[576,1152]{1,0:T(8,128)}, f32[576,1152]{1,0:T(8,128)}, f32[576,1152]{1,0:T(8,128)}, f32[288,1152]{1,0:T(8,128)S(1)}) custom-call(s32[3,5]{1,0:T(4,128)S(1)} %get-tuple-element.571.spots_ref, bf16[512,4608]{1,0:T(8,128)(2,1)} %get-tuple-element.353.mine_ref, ...), custom_call_target="tpu_custom_call" | custom-call | flops 6794772480 | bytes 22413312 | tf_op jit(solution)/shard_map/pallas_call | solution.py:467
  383.2 14.5 %multiply_reduce_fusion.1 = (f32[1152]{0:T(1024)}, f32[512]{0:T(512)S(1)}, f32[1152]{0:T(1024)}, f32[512,1152]{1,0:T(8,128)}) fusion(f32[512,1152]{1,0:T(8,128)} %get-tuple-element.327, f32[512]{0:T(512)S(1)} %copy-done.86, f32[512]{0:T(512)S(1)} %copy-done.80, f32[1152]{0:T(1024)S(1)} %copy-done.73, bf16[512,4608]{1,0:T(8,128)(2,1)} %fusion.6.grad_ref, ...), kind=kOutput, calls=%fused_computation.67 | convolution fusion | flops 5440534016 | bytes 20073984 | tf_op jit(solution)/shard_map/ne,de->nd/dot_general | solution.py:618
  408.8 13.6 %shard_map.217 = (bf16[72,4608]{1,0:T(8,128)(2,1)S(1)}, f32[144,4608]{1,0:T(8,128)}, f32[144,4608]{1,0:T(8,128)}, f32[144,4608]{1,0:T(8,128)}, f32[72,4608]{1,0:T(8,128)S(1)}) custom-call(s32[3,5]{1,0:T(4,128)S(1)} %get-tuple-element.570.spots_ref, bf16[512,1152]{1,0:T(8,128)(2,1)} %add_convert_fusion.7.mine_ref, ...), custom_call_target="tpu_custom_call" | custom-call | flops 6794772480 | bytes 22413312 | tf_op jit(solution)/shard_map/pallas_call | solution.py:467
  429.5 13.8 %collective-permute-done.60 = bf16[576,1152]{1,0:T(8,128)(2,1)} collective-permute-done((bf16[576,1152]{1,0:T(8,128)(2,1)S(1)}, bf16[576,1152]{1,0:T(8,128)(2,1)}, u32[]{:S(2)}, u32[]{:S(2)}) %collective-permute-start.60) | collective-permute-done | bytes 1327136 | tf_op jit(solution)/shard_map/ppermute | solution.py:494
  446.9 15.0 %collective-permute-start.62 = (bf16[576,1152]{1,0:T(8,128)(2,1)}, bf16[576,1152]{1,0:T(8,128)(2,1)S(1)}, u32[]{:S(2)}, u32[]{:S(2)}) collective-permute-start(bf16[576,1152]{1,0:T(8,128)(2,1)} %add_convert_fusion.4), channel_id=1, source_target_pairs={{0,4},{1,3},{4,8},{5,1},{8,12},{9,5},{12,14},{13,9},{14,10},{15,13... | collective-permute-start | bytes 3981320 | tf_op jit(solution)/shard_map/ppermute | solution.py:494
  464.5 39.6 %shard_map.219 = (bf16[512,1152]{1,0:T(8,128)(2,1)S(1)}, f32[512,1152]{1,0:T(8,128)S(1)}, f32[512,1152]{1,0:T(8,128)}, f32[512,2304]{1,0:T(8,128)}) custom-call(s32[1]{0:T(128)S(6)} %convert_element_type.232.long_ref, bf16[512,3456]{1,0:T(8,128)(2,1)} %copy-done.9, bf16[512,3456]{1,0:T(8,128)(2,1)} %copy-done.9, bf16[512,3456]{1,0:T(8,128)(2,1)} %copy-done.9, ...), custom_call_target="tpu_custom_call" | custom-call | flops 21474836480 | bytes 23592960 | tf_op jit(solution)/shard_map/pallas_call | solution.py:148
  520.7 10.5 %fusion.62 = f32[512,1152]{1,0:T(8,128)} fusion(bf16[1152,3456]{1,0:T(8,128)(2,1)} %bitcast.111, bf16[512,1152]{1,0:T(8,128)(2,1)} %copy-done.46, bf16[512,1152]{1,0:T(8,128)(2,1)} %copy-done.45, bf16[512,1152]{1,0:T(8,128)(2,1)S(1)} %get-tuple-element.410), kind=kOutput, calls=%fused_computation.197 | convolution fusion | flops 4087480320 | bytes 13860864 | tf_op jit(solution)/shard_map/ne,de->nd/dot_general | solution.py:618
  531.3 11.3 %shard_map.220 = (bf16[72,3456]{1,0:T(8,128)(2,1)}, f32[144,3456]{1,0:T(8,128)S(1)}, f32[144,3456]{1,0:T(8,128)}, f32[144,3456]{1,0:T(8,128)}, f32[72,3456]{1,0:T(8,128)S(1)}) custom-call(s32[3,5]{1,0:T(4,128)S(1)} %get-tuple-element.570.spots_ref, bf16[512,1152]{1,0:T(8,128)(2,1)S(1)} %copy-done.18, bf16[512,1152]{1,0:T(8,128)(2,1)} %collective-permute-done.66.theirs_ref, ...), custom_call_target="tpu_custom_call" | custom-call | flops 5096079360 | bytes 17399808 | tf_op jit(solution)/shard_map/pallas_call | solution.py:467
  592.5 13.3 %collective-permute-done.76 = bf16[144,1152]{1,0:T(8,128)(2,1)} collective-permute-done((bf16[144,1152]{1,0:T(8,128)(2,1)}, bf16[144,1152]{1,0:T(8,128)(2,1)}, u32[]{:S(2)}, u32[]{:S(2)}) %collective-permute-start.76) | collective-permute-done | bytes 331808 | tf_op jit(solution)/shard_map/ppermute | solution.py:494
  658.2 7.9 %collective-permute-done.89 = bf16[72,2048]{1,0:T(8,128)(2,1)S(1)} collective-permute-done((bf16[72,2048]{1,0:T(8,128)(2,1)S(1)}, bf16[72,2048]{1,0:T(8,128)(2,1)S(1)}, u32[]{:S(2)}, u32[]{:S(2)}) %collective-permute-start.89) | collective-permute-done | bytes 294944 | tf_op jit(solution)/shard_map/ppermute | solution.py:178
  693.0 13.2 %collective-permute-done.98 = bf16[72,1152]{1,0:T(8,128)(2,1)S(1)} collective-permute-done((bf16[72,1152]{1,0:T(8,128)(2,1)S(1)}, bf16[72,1152]{1,0:T(8,128)(2,1)S(1)}, u32[]{:S(2)}, u32[]{:S(2)}) %collective-permute-start.98) | collective-permute-done | bytes 165920 | tf_op jit(solution)/shard_map/ppermute | solution.py:178
  (540 shorter events, 352.1 us)
Async XLA Ops:
  7.2 287.6 %all-gather.2.cloned.1.call-start = ((), (), s32[]{:S(2)}) async-start(), calls=%async_computation.3 | async-start | bytes 3342336 | tf_op jit(solution)/shard_map/all_gather | solution.py:652
  12.6 45.8 %collective-permute-start.11 = (bf16[36,8,1152]{2,1,0:T(8,128)(2,1)S(1)}, bf16[36,8,1152]{2,1,0:T(8,128)(2,1)}, u32[]{:S(2)}, u32[]{:S(2)}) collective-permute-start(bf16[36,8,1152]{2,1,0:T(8,128)(2,1)S(1)} %pad_maximum_fusion.4.refs_0_), channel_id=1, source_target_pairs={{0,2},{1,5},{4,0},{5,9},{8,4},{9,13},{12,8},{13,15},{14,12},{15,11... | collective-permute-start | bytes 1990664 | tf_op jit(solution)/shard_map/ppermute | solution.py:208
  67.6 31.7 %collective-permute-start.20 = (bf16[72,8,1152]{2,1,0:T(8,128)(2,1)S(1)}, bf16[72,8,1152]{2,1,0:T(8,128)(2,1)}, u32[]{:S(2)}, u32[]{:S(2)}) collective-permute-start(bf16[72,8,1152]{2,1,0:T(8,128)(2,1)S(1)} %bitcast_dynamic-update-slice_fusion.1.refs_0_), channel_id=1, source_target_pairs={{0,4},{1,3},{4,8},{5,1},{8,12},{9,5},{12,14},{13,9},{14,10},{15,13... | collective-permute-start | bytes 3981320 | tf_op jit(solution)/shard_map/ppermute | solution.py:208
  69.7 29.6 %collective-permute-start.21 = (bf16[72,8,1152]{2,1,0:T(8,128)(2,1)S(1)}, bf16[72,8,1152]{2,1,0:T(8,128)(2,1)}, u32[]{:S(2)}, u32[]{:S(2)}) collective-permute-start(bf16[72,8,1152]{2,1,0:T(8,128)(2,1)S(1)} %bitcast_dynamic-update-slice_fusion.1.refs_0_), channel_id=1, source_target_pairs={{0,2},{1,5},{4,0},{5,9},{8,4},{9,13},{12,8},{13,15},{14,12},{15,11... | collective-permute-start | bytes 3981320 | tf_op jit(solution)/shard_map/ppermute | solution.py:208
  69.7 29.6 %collective-permute-start.22 = (bf16[72,8,1152]{2,1,0:T(8,128)(2,1)S(1)}, bf16[72,8,1152]{2,1,0:T(8,128)(2,1)S(1)}, u32[]{:S(2)}, u32[]{:S(2)}) collective-permute-start(bf16[72,8,1152]{2,1,0:T(8,128)(2,1)S(1)} %bitcast_dynamic-update-slice_fusion.1.refs_0_), channel_id=1, source_target_pairs={{0,1},{1,0},{2,3},{3,2},{4,5},{5,4},{6,7},{7,6},{8,9},{9,8},{10,11... | collective-permute-start | bytes 3981320 | tf_op jit(solution)/shard_map/ppermute | solution.py:174
  127.3 30.5 %collective-permute-start.27 = (bf16[72,8,1152]{2,1,0:T(8,128)(2,1)S(1)}, bf16[72,8,1152]{2,1,0:T(8,128)(2,1)S(1)}, u32[]{:S(2)}, u32[]{:S(2)}) collective-permute-start(bf16[72,8,1152]{2,1,0:T(8,128)(2,1)S(1)} %collective-permute-done.24.refs_2_), channel_id=1, source_target_pairs={{0,4},{1,3},{4,8},{5,1},{8,12},{9,5},{12,14},{13,9},{14,10},{15,13... | collective-permute-start | bytes 3981320 | tf_op jit(solution)/shard_map/ppermute | solution.py:208
  128.4 30.2 %collective-permute-start.28 = (bf16[72,8,1152]{2,1,0:T(8,128)(2,1)S(1)}, bf16[72,8,1152]{2,1,0:T(8,128)(2,1)S(1)}, u32[]{:S(2)}, u32[]{:S(2)}) collective-permute-start(bf16[72,8,1152]{2,1,0:T(8,128)(2,1)S(1)} %collective-permute-done.24.refs_2_), channel_id=1, source_target_pairs={{0,16},{16,0},{1,17},{17,1},{2,18},{18,2},{3,19},{19,3},{4,20},{20... | collective-permute-start | bytes 3981320 | tf_op jit(solution)/shard_map/ppermute | solution.py:178
  128.8 29.8 %collective-permute-start.29 = (bf16[72,8,1152]{2,1,0:T(8,128)(2,1)S(1)}, bf16[72,8,1152]{2,1,0:T(8,128)(2,1)S(1)}, u32[]{:S(2)}, u32[]{:S(2)}) collective-permute-start(bf16[72,8,1152]{2,1,0:T(8,128)(2,1)S(1)} %collective-permute-done.24.refs_2_), channel_id=1, source_target_pairs={{0,1},{1,0},{2,3},{3,2},{4,5},{5,4},{6,7},{7,6},{8,9},{9,8},{10,11... | collective-permute-start | bytes 3981320 | tf_op jit(solution)/shard_map/ppermute | solution.py:174
  129.2 33.6 %collective-permute-start.30 = (bf16[50,8,1024]{2,1,0:T(8,128)(2,1)S(1)}, bf16[50,8,1024]{2,1,0:T(8,128)(2,1)}, u32[]{:S(2)}, u32[]{:S(2)}) collective-permute-start(bf16[50,8,1024]{2,1,0:T(8,128)(2,1)S(1)} %pad_maximum_fusion.2.refs_0_), channel_id=1, source_target_pairs={{0,4},{1,3},{4,8},{5,1},{8,12},{9,5},{12,14},{13,9},{14,10},{15,13... | collective-permute-start | bytes 2457608 | tf_op jit(solution)/shard_map/ppermute | solution.py:208
  130.4 32.4 %collective-permute-start.31 = (bf16[50,8,1024]{2,1,0:T(8,128)(2,1)S(1)}, bf16[50,8,1024]{2,1,0:T(8,128)(2,1)}, u32[]{:S(2)}, u32[]{:S(2)}) collective-permute-start(bf16[50,8,1024]{2,1,0:T(8,128)(2,1)S(1)} %pad_maximum_fusion.2.refs_0_), channel_id=1, source_target_pairs={{0,2},{1,5},{4,0},{5,9},{8,4},{9,13},{12,8},{13,15},{14,12},{15,11... | collective-permute-start | bytes 2457608 | tf_op jit(solution)/shard_map/ppermute | solution.py:208
  158.6 31.0 %collective-permute-start.34 = (bf16[72,8,1152]{2,1,0:T(8,128)(2,1)S(1)}, bf16[72,8,1152]{2,1,0:T(8,128)(2,1)}, u32[]{:S(2)}, u32[]{:S(2)}) collective-permute-start(bf16[72,8,1152]{2,1,0:T(8,128)(2,1)S(1)} %collective-permute-done.27.refs_3_), channel_id=1, source_target_pairs={{0,16},{16,0},{1,17},{17,1},{2,18},{18,2},{3,19},{19,3},{4,20},{20... | collective-permute-start | bytes 3981320 | tf_op jit(solution)/shard_map/ppermute | solution.py:178
  160.4 29.2 %collective-permute-start.36 = (bf16[72,8,1152]{2,1,0:T(8,128)(2,1)S(1)}, bf16[72,8,1152]{2,1,0:T(8,128)(2,1)S(1)}, u32[]{:S(2)}, u32[]{:S(2)}) collective-permute-start(bf16[72,8,1152]{2,1,0:T(8,128)(2,1)S(1)} %collective-permute-done.28.refs_6_), channel_id=1, source_target_pairs={{0,1},{1,0},{2,3},{3,2},{4,5},{5,4},{6,7},{7,6},{8,9},{9,8},{10,11... | collective-permute-start | bytes 3981320 | tf_op jit(solution)/shard_map/ppermute | solution.py:174
  206.3 175.1 %reduce-scatter.4.cloned.1.call-start = ((), (), s32[]{:S(2)}) async-start(), calls=%async_computation.4 | async-start | bytes 3342336 | tf_op jit(solution)/shard_map/reduce_scatter | solution.py:422
  254.8 154.0 %collective-permute-start.57 = (bf16[512,1152]{1,0:T(8,128)(2,1)}, bf16[512,1152]{1,0:T(8,128)(2,1)}, u32[]{:S(2)}, u32[]{:S(2)}) collective-permute-start(bf16[512,1152]{1,0:T(8,128)(2,1)} %add_convert_fusion.7.mine_ref), channel_id=1, source_target_pairs={{0,1},{1,0},{2,3},{3,2},{4,5},{5,4},{6,7},{7,6},{8,9},{9,8},{10,11... | collective-permute-start | bytes 3538952 | tf_op jit(solution)/shard_map/ppermute | solution.py:174
  255.3 105.4 %collective-permute-start.54 = (bf16[512,4608]{1,0:T(8,128)(2,1)}, bf16[512,4608]{1,0:T(8,128)(2,1)}, u32[]{:S(2)}, u32[]{:S(2)}) collective-permute-start(bf16[512,4608]{1,0:T(8,128)(2,1)} %get-tuple-element.353.mine_ref), channel_id=1, source_target_pairs={{0,1},{1,0},{2,3},{3,2},{4,5},{5,4},{6,7},{7,6},{8,9},{9,8},{10,11... | collective-permute-start | bytes 14155784 | tf_op jit(solution)/shard_map/ppermute | solution.py:174
  304.5 239.4 %reduce-scatter.6.cloned.1.call-start = ((), (), s32[]{:S(2)}) async-start(), calls=%async_computation.5 | async-start | bytes 8912896 | tf_op jit(solution)/shard_map/reduce_scatter | solution.py:422
  343.8 268.5 %reduce-scatter.8.cloned.1.call-start = ((), (), s32[]{:S(2)}) async-start(), calls=%async_computation.6 | async-start | bytes 5013504 | tf_op jit(solution)/shard_map/reduce_scatter | solution.py:422
  406.9 36.4 %collective-permute-start.60 = (bf16[576,1152]{1,0:T(8,128)(2,1)S(1)}, bf16[576,1152]{1,0:T(8,128)(2,1)}, u32[]{:S(2)}, u32[]{:S(2)}) collective-permute-start(bf16[576,1152]{1,0:T(8,128)(2,1)S(1)} %add_convert_fusion.5), channel_id=1, source_target_pairs={{0,4},{1,3},{4,8},{5,1},{8,12},{9,5},{12,14},{13,9},{14,10},{15,13... | collective-permute-start | bytes 3981320 | tf_op jit(solution)/shard_map/ppermute | solution.py:494
  446.9 57.1 %collective-permute-start.62 = (bf16[576,1152]{1,0:T(8,128)(2,1)}, bf16[576,1152]{1,0:T(8,128)(2,1)S(1)}, u32[]{:S(2)}, u32[]{:S(2)}) collective-permute-start(bf16[576,1152]{1,0:T(8,128)(2,1)} %add_convert_fusion.4), channel_id=1, source_target_pairs={{0,4},{1,3},{4,8},{5,1},{8,12},{9,5},{12,14},{13,9},{14,10},{15,13... | collective-permute-start | bytes 3981320 | tf_op jit(solution)/shard_map/ppermute | solution.py:494
  461.9 42.2 %collective-permute-start.63 = (bf16[72,4608]{1,0:T(8,128)(2,1)S(1)}, bf16[72,4608]{1,0:T(8,128)(2,1)S(1)}, u32[]{:S(2)}, u32[]{:S(2)}) collective-permute-start(bf16[72,4608]{1,0:T(8,128)(2,1)S(1)} %get-tuple-element.404), channel_id=1, source_target_pairs={{0,4},{1,3},{4,8},{5,1},{8,12},{9,5},{12,14},{13,9},{14,10},{15,13... | collective-permute-start | bytes 1990664 | tf_op jit(solution)/shard_map/ppermute | solution.py:494
  517.3 37.3 %collective-permute-start.69 = (bf16[72,1152]{1,0:T(8,128)(2,1)}, bf16[72,1152]{1,0:T(8,128)(2,1)}, u32[]{:S(2)}, u32[]{:S(2)}) collective-permute-start(bf16[72,1152]{1,0:T(8,128)(2,1)} %copy-done.33), channel_id=1, source_target_pairs={{0,4},{1,3},{4,8},{5,1},{8,12},{9,5},{12,14},{13,9},{14,10},{15,13... | collective-permute-start | bytes 497672 | tf_op jit(solution)/shard_map/ppermute | solution.py:494
  518.2 36.5 %collective-permute-start.67 = (bf16[576,1152]{1,0:T(8,128)(2,1)}, bf16[576,1152]{1,0:T(8,128)(2,1)}, u32[]{:S(2)}, u32[]{:S(2)}) collective-permute-start(bf16[576,1152]{1,0:T(8,128)(2,1)} %add_convert_fusion.3), channel_id=1, source_target_pairs={{0,4},{1,3},{4,8},{5,1},{8,12},{9,5},{12,14},{13,9},{14,10},{15,13... | collective-permute-start | bytes 3981320 | tf_op jit(solution)/shard_map/ppermute | solution.py:494
  519.8 37.6 %collective-permute-start.68 = (bf16[144,4608]{1,0:T(8,128)(2,1)}, bf16[144,4608]{1,0:T(8,128)(2,1)}, u32[]{:S(2)}, u32[]{:S(2)}) collective-permute-start(bf16[144,4608]{1,0:T(8,128)(2,1)} %add_convert_fusion.2), channel_id=1, source_target_pairs={{0,4},{1,3},{4,8},{5,1},{8,12},{9,5},{12,14},{13,9},{14,10},{15,13... | collective-permute-start | bytes 3981320 | tf_op jit(solution)/shard_map/ppermute | solution.py:494
  571.5 34.3 %collective-permute-start.75 = (bf16[144,4608]{1,0:T(8,128)(2,1)}, bf16[144,4608]{1,0:T(8,128)(2,1)}, u32[]{:S(2)}, u32[]{:S(2)}) collective-permute-start(bf16[144,4608]{1,0:T(8,128)(2,1)} %add_convert_fusion.1), channel_id=1, source_target_pairs={{0,4},{1,3},{4,8},{5,1},{8,12},{9,5},{12,14},{13,9},{14,10},{15,13... | collective-permute-start | bytes 3981320 | tf_op jit(solution)/shard_map/ppermute | solution.py:494
  (185 other events, 2590.0 us)
Sparse Core Ops, SparseCore 0:
  206.4 48.8 all-gather.1
  304.6 67.8 reduce-scatter.3
  376.6 122.6 reduce-scatter.5
  517.1 81.2 reduce-scatter.7

commit v4 on v3

--- a/solution.py
+++ b/solution.py
@@ -718,11 +718,11 @@
     chain_third = Chain(bins_sum(part_third))
     chain_fc1 = Chain(grad_chain([(in_two, d_pre_low)], [in_two_peer]))
     d_in_two = input_grad(d_pre_low, full_fc1)
+    d_in_two = beats(d_in_two, chain_fc2)
     d_resid_part, grad_shift_two, grad_scale_two = norm_two_back(d_in_two)
     d_resid = d_result + d_resid_part
     grad_gate_one = jnp.sum(d_resid * branch_one, axis=0)
     d_branch_one = (d_resid * modulation[2]).astype(jnp.bfloat16)
-    d_branch_one, d_resid = beats((d_branch_one, d_resid), chain_fc2)
     chain_out = Chain(grad_chain([(attended, d_branch_one)], [attended_peer]))
     d_branch_one = beats(d_branch_one, chain_fc1)
     d_attended = input_grad(d_branch_one, full_out).astype(jnp.bfloat16)

time: 727 us -> 715 us (0.983)
  starting transfers between devices: 100 us -> 89.7 us
    ppermute x16, starting transfers between devices: 38.6 us -> 28.4 us  [core_hop(): return lax.ppermute(block, 'fsdp', pairs)]
  transfers between devices with their start and end apart: 103 -> 103, of which waited for: 38 -> 40; matrix products, arithmetic and copies ran while one was open for 28% -> 27% of each run, Pallas kernels for 19% -> 20%
where the time goes in v4:
time: 715 us; the launch traced here: 707 us
  waiting for transfers between devices  219 us (31%)
  Pallas kernels  140 us (20%)
  matrix products  125 us (17%)
  starting transfers between devices  89.7 us (13%)
  other arithmetic  75.9 us (11%)
  local copies, waits for them, and re-layouts  39.8 us (6%)
  between operations  17.5 us (2%)
    ppermute x18, waiting for transfers between devices, bins_peer(): return lax.ppermute(block, 'bins', [(0, 1), (1, 0)])  92.8 us
    dot_general x7, matrix products, input_grad(): jnp.einsum('ne,de->nd', grad, weight, preferred_element_type=jnp.float32)  62.5 us
    pallas_call x4, Pallas kernels, grad_parts(): pl.pallas_call(parts_kernel, out_shape=[jax.ShapeDtypeStruct((k, columns)...  47.9 us
    dot_general x8, matrix products, product(): return jnp.dot(left, right, preferred_element_type=jnp.float32)  47.5 us
    ppermute x15, waiting for transfers between devices, parted_hop(): return lax.ppermute(block, ('bins', 'fsdp'), pairs)  44 us
    ppermute x16, waiting for transfers between devices, core_hop(): return lax.ppermute(block, 'fsdp', pairs)  43.9 us
    pallas_call x1, Pallas kernels, attend_back(): pl.pallas_call(partial(attend_back_kernel, factor), out_shape=[jax.ShapeD...  39.5 us
    ppermute x50, waiting for transfers between devices, swapped(): return lax.ppermute(block, axis, route)  38 us
  transfers between devices with their start and end apart: 103, of which 40 were waited for; matrix products, arithmetic and copies ran while one was open for 27% of the time, Pallas kernels for 20%

profile of v4, /device:TPU:0, one launch (start us, length us, event | category | flops | bytes accessed | tf_op | source)
XLA Modules:
  0.0 706.6 jit_solution(5079290240981546002)
XLA Ops:
  13.9 13.8 %collective-permute-done.4.refs_1_ = bf16[36,8,1152]{2,1,0:T(8,128)(2,1)S(1)} collective-permute-done((bf16[36,8,1152]{2,1,0:T(8,128)(2,1)S(1)}, bf16[36,8,1152]{2,1,0:T(8,128)(2,1)S(1)}, u32[]{:S(2)}, u32[]{:S(2)}) %collective-permute-start.4) | collective-permute-done | bytes 663584 | tf_op jit(solution)/shard_map/ppermute | solution.py:208
  31.1 7.8 %collective-permute-done.5.refs_2_ = bf16[36,8,1152]{2,1,0:T(8,128)(2,1)} collective-permute-done((bf16[36,8,1152]{2,1,0:T(8,128)(2,1)S(1)}, bf16[36,8,1152]{2,1,0:T(8,128)(2,1)}, u32[]{:S(2)}, u32[]{:S(2)}) %collective-permute-start.5) | collective-permute-done | bytes 663584 | tf_op jit(solution)/shard_map/ppermute | solution.py:208
  69.7 15.0 %collective-permute-done.10 = bf16[18,8,1152]{2,1,0:T(8,128)(2,1)S(1)} collective-permute-done((bf16[18,8,1152]{2,1,0:T(8,128)(2,1)S(1)}, bf16[18,8,1152]{2,1,0:T(8,128)(2,1)S(1)}, u32[]{:S(2)}, u32[]{:S(2)}) %collective-permute-start.10) | collective-permute-done | bytes 331808 | tf_op jit(solution)/shard_map/ppermute | solution.py:178
  113.4 13.7 %collective-permute-done.24.refs_2_ = bf16[72,8,1152]{2,1,0:T(8,128)(2,1)S(1)} collective-permute-done((bf16[72,8,1152]{2,1,0:T(8,128)(2,1)}, bf16[72,8,1152]{2,1,0:T(8,128)(2,1)S(1)}, u32[]{:S(2)}, u32[]{:S(2)}) %collective-permute-start.24) | collective-permute-done | bytes 1327136 | tf_op jit(solution)/shard_map/ppermute | solution.py:208
  133.2 24.4 %shard_map.213 = (bf16[512,1152]{1,0:T(8,128)(2,1)S(1)}, f32[512,1152]{1,0:T(8,128)S(1)}, bf16[1152,512]{1,0:T(8,128)(2,1)}, f32[16,512]{1,0:T(8,128)S(1)}) custom-call(s32[1]{0:T(128)S(6)} %convert_element_type.232.long_ref, bf16[512,3456]{1,0:T(8,128)(2,1)S(1)} %copy-done.10, bf16[512,3456]{1,0:T(8,128)(2,1)S(1)} %copy-done.10, ...), custom_call_target="tpu_custom_call" | custom-call | flops 8589934592 | bytes 9437184 | tf_op jit(solution)/shard_map/pallas_call | solution.py:81
  173.3 16.3 %collective-permute-done.34.refs_7_ = bf16[72,8,1152]{2,1,0:T(8,128)(2,1)} collective-permute-done((bf16[72,8,1152]{2,1,0:T(8,128)(2,1)S(1)}, bf16[72,8,1152]{2,1,0:T(8,128)(2,1)}, u32[]{:S(2)}, u32[]{:S(2)}) %collective-permute-start.34) | collective-permute-done | bytes 1327136 | tf_op jit(solution)/shard_map/ppermute | solution.py:178
  192.7 12.9 %collective-permute-done.40 = bf16[36,8,1152]{2,1,0:T(8,128)(2,1)S(1)} collective-permute-done((bf16[36,8,1152]{2,1,0:T(8,128)(2,1)S(1)}, bf16[36,8,1152]{2,1,0:T(8,128)(2,1)S(1)}, u32[]{:S(2)}, u32[]{:S(2)}) %collective-permute-start.40) | collective-permute-done | bytes 663584 | tf_op jit(solution)/shard_map/ppermute | solution.py:178
  215.9 14.6 %shard_map.214 = (bf16[144,8,4608]{2,1,0:T(8,128)(2,1)}, bf16[576,8,1152]{2,1,0:T(8,128)(2,1)}) custom-call(s32[16]{0:T(128)S(1)} %stack.84.origins_ref, bf16[72,8,1152]{2,1,0:T(8,128)(2,1)S(1)} %copy-done.8, bf16[72,8,1152]{2,1,0:T(8,128)(2,1)} %collective-permute-done.20.refs_1_, bf16[72,8,1152]{2,1,0:T(8,128)(2,1)S(1)} %copy-done.14, ...), custom_call_target="tpu_custom_call" | custom-call | bytes 42467328 | tf_op jit(solution)/shard_map/pallas_call | solution.py:311
  234.9 13.5 %multiply_convert_fusion = (bf16[512,4608]{1,0:T(8,128)(2,1)}, f32[512,4608]{1,0:T(8,128)}) fusion(bf16[512,1152]{1,0:T(8,128)(2,1)} %add_convert_fusion.7.mine_ref, bf16[1152,4608]{1,0:T(8,128)(2,1)} %bitcast.122), kind=kOutput, calls=%fused_computation.9 | convolution fusion | flops 5457051648 | bytes 25952256 | tf_op jit(solution)/shard_map/dot_general | solution.py:614
  255.4 8.6 %collective-permute-done.50 = bf16[25,8,1024]{2,1,0:T(8,128)(2,1)S(1)} collective-permute-done((bf16[25,8,1024]{2,1,0:T(8,128)(2,1)S(1)}, bf16[25,8,1024]{2,1,0:T(8,128)(2,1)S(1)}, u32[]{:S(2)}, u32[]{:S(2)}) %collective-permute-start.50) | collective-permute-done | bytes 409632 | tf_op jit(solution)/shard_map/ppermute | solution.py:178
  264.3 9.2 %add_convert_fusion.6 = (bf16[512,1152]{1,0:T(8,128)(2,1)S(1)}, f32[512,1152]{1,0:T(8,128)}) fusion(f32[512,1152]{1,0:T(8,128)S(1)} %copy-done.35, f32[1152]{0:T(1024)S(1)} %get-tuple-element.554, bf16[512,4608]{1,0:T(8,128)(2,1)} %get-tuple-element.351.mine_ref, bf16[4608,1152]{1,0:T(8,128)(2,1)S(1)} %bitcast.127), kind=kOutput, calls=%fused_computation.74 | convolution fusion | flops 5437587456 | bytes 21238272 | tf_op jit(solution)/shard_map/dot_general | solution.py:614
  318.8 11.1 %fusion.20 = bf16[512,2048]{1,0:T(8,128)(2,1)S(1)} fusion(f32[512,2048]{1,0:T(8,128)} %copy-done.99, bf16[512,2048]{1,0:T(8,128)(2,1)} %copy-done.102, bf16[256,8,2048]{2,1,0:T(8,128)(2,1)} %get-tuple-element.362), kind=kOutput, calls=%fused_computation.28 | convolution fusion | flops 4305453056 | bytes 16777216 | tf_op jit(solution)/shard_map/ne,de->nd/dot_general | solution.py:618
  343.7 16.7 %fusion.6.grad_ref = bf16[512,4608]{1,0:T(8,128)(2,1)} fusion(f32[512,4608]{1,0:T(8,128)} %get-tuple-element.571, bf16[512,1152]{1,0:T(8,128)(2,1)S(1)} %multiply_convert_fusion.4.grad_ref, bf16[4608,1152]{1,0:T(8,128)(2,1)} %bitcast.124), kind=kOutput, calls=%fused_computation.8 | convolution fusion | flops 5483003904 | bytes 25952256 | tf_op jit(solution)/shard_map/ne,de->nd/dot_general | solution.py:618
  360.5 17.8 %shard_map.216 = (bf16[288,1152]{1,0:T(8,128)(2,1)S(1)}, f32[576,1152]{1,0:T(8,128)}, f32[576,1152]{1,0:T(8,128)}, f32[576,1152]{1,0:T(8,128)}, f32[288,1152]{1,0:T(8,128)S(1)}) custom-call(s32[3,5]{1,0:T(4,128)S(1)} %get-tuple-element.567.spots_ref, bf16[512,4608]{1,0:T(8,128)(2,1)} %get-tuple-element.351.mine_ref, ...), custom_call_target="tpu_custom_call" | custom-call | flops 6794772480 | bytes 22413312 | tf_op jit(solution)/shard_map/pallas_call | solution.py:467
  382.7 10.5 %fusion.68 = f32[512,1152]{1,0:T(8,128)S(1)} fusion(bf16[512,4608]{1,0:T(8,128)(2,1)} %fusion.6.grad_ref, bf16[1152,4608]{1,0:T(8,128)(2,1)} %bitcast.123), kind=kOutput, calls=%fused_computation.201 | convolution fusion | flops 5435817984 | bytes 17694720 | tf_op jit(solution)/shard_map/ne,de->nd/dot_general | solution.py:618
  406.1 13.6 %shard_map.217 = (bf16[72,4608]{1,0:T(8,128)(2,1)S(1)}, f32[144,4608]{1,0:T(8,128)}, f32[144,4608]{1,0:T(8,128)}, f32[144,4608]{1,0:T(8,128)}, f32[72,4608]{1,0:T(8,128)S(1)}) custom-call(s32[3,5]{1,0:T(4,128)S(1)} %get-tuple-element.566.spots_ref, bf16[512,1152]{1,0:T(8,128)(2,1)} %add_convert_fusion.7.mine_ref, ...), custom_call_target="tpu_custom_call" | custom-call | flops 6794772480 | bytes 22413312 | tf_op jit(solution)/shard_map/pallas_call | solution.py:467
  435.1 13.5 %collective-permute-start.62 = (bf16[576,1152]{1,0:T(8,128)(2,1)}, bf16[576,1152]{1,0:T(8,128)(2,1)S(1)}, u32[]{:S(2)}, u32[]{:S(2)}) collective-permute-start(bf16[576,1152]{1,0:T(8,128)(2,1)} %add_convert_fusion.4), channel_id=1, source_target_pairs={{0,4},{1,3},{4,8},{5,1},{8,12},{9,5},{12,14},{13,9},{14,10},{15,13... | collective-permute-start | bytes 3981320 | tf_op jit(solution)/shard_map/ppermute | solution.py:494
  451.3 39.5 %shard_map.219 = (bf16[512,1152]{1,0:T(8,128)(2,1)S(1)}, f32[512,1152]{1,0:T(8,128)S(1)}, f32[512,1152]{1,0:T(8,128)}, f32[512,2304]{1,0:T(8,128)}) custom-call(s32[1]{0:T(128)S(6)} %convert_element_type.232.long_ref, bf16[512,3456]{1,0:T(8,128)(2,1)} %copy-done.9, bf16[512,3456]{1,0:T(8,128)(2,1)} %copy-done.9, bf16[512,3456]{1,0:T(8,128)(2,1)} %copy-done.9, ...), custom_call_target="tpu_custom_call" | custom-call | flops 21474836480 | bytes 23592960 | tf_op jit(solution)/shard_map/pallas_call | solution.py:148
  504.6 10.6 %fusion.62 = f32[512,1152]{1,0:T(8,128)} fusion(bf16[1152,3456]{1,0:T(8,128)(2,1)} %bitcast.111, bf16[512,1152]{1,0:T(8,128)(2,1)} %copy-done.46, bf16[512,1152]{1,0:T(8,128)(2,1)} %copy-done.45, bf16[512,1152]{1,0:T(8,128)(2,1)S(1)} %get-tuple-element.406), kind=kOutput, calls=%fused_computation.197 | convolution fusion | flops 4087480320 | bytes 13860864 | tf_op jit(solution)/shard_map/ne,de->nd/dot_general | solution.py:618
  515.2 11.3 %shard_map.220 = (bf16[72,3456]{1,0:T(8,128)(2,1)}, f32[144,3456]{1,0:T(8,128)S(1)}, f32[144,3456]{1,0:T(8,128)}, f32[144,3456]{1,0:T(8,128)}, f32[72,3456]{1,0:T(8,128)S(1)}) custom-call(s32[3,5]{1,0:T(4,128)S(1)} %get-tuple-element.566.spots_ref, bf16[512,1152]{1,0:T(8,128)(2,1)S(1)} %copy-done.18, bf16[512,1152]{1,0:T(8,128)(2,1)} %collective-permute-done.66.theirs_ref, ...), custom_call_target="tpu_custom_call" | custom-call | flops 5096079360 | bytes 17399808 | tf_op jit(solution)/shard_map/pallas_call | solution.py:467
  537.6 11.5 %collective-permute-done.68 = bf16[144,4608]{1,0:T(8,128)(2,1)} collective-permute-done((bf16[144,4608]{1,0:T(8,128)(2,1)}, bf16[144,4608]{1,0:T(8,128)(2,1)}, u32[]{:S(2)}, u32[]{:S(2)}) %collective-permute-start.68) | collective-permute-done | bytes 1327136 | tf_op jit(solution)/shard_map/ppermute | solution.py:494
  583.8 8.7 %collective-permute-done.76 = bf16[144,1152]{1,0:T(8,128)(2,1)} collective-permute-done((bf16[144,1152]{1,0:T(8,128)(2,1)}, bf16[144,1152]{1,0:T(8,128)(2,1)}, u32[]{:S(2)}, u32[]{:S(2)}) %collective-permute-start.76) | collective-permute-done | bytes 331808 | tf_op jit(solution)/shard_map/ppermute | solution.py:494
  616.4 8.8 %collective-permute-done.81 = bf16[144,1152]{1,0:T(8,128)(2,1)S(1)} collective-permute-done((bf16[144,1152]{1,0:T(8,128)(2,1)}, bf16[144,1152]{1,0:T(8,128)(2,1)S(1)}, u32[]{:S(2)}, u32[]{:S(2)}) %collective-permute-start.81) | collective-permute-done | bytes 331808 | tf_op jit(solution)/shard_map/ppermute | solution.py:494
  683.0 12.5 %collective-permute-done.98 = bf16[72,1152]{1,0:T(8,128)(2,1)S(1)} collective-permute-done((bf16[72,1152]{1,0:T(8,128)(2,1)S(1)}, bf16[72,1152]{1,0:T(8,128)(2,1)S(1)}, u32[]{:S(2)}, u32[]{:S(2)}) %collective-permute-start.98) | collective-permute-done | bytes 165920 | tf_op jit(solution)/shard_map/ppermute | solution.py:178
  (541 shorter events, 353.2 us)
Async XLA Ops:
  7.2 287.8 %all-gather.2.cloned.1.call-start = ((), (), s32[]{:S(2)}) async-start(), calls=%async_computation.3 | async-start | bytes 3342336 | tf_op jit(solution)/shard_map/all_gather | solution.py:652
  12.6 45.8 %collective-permute-start.11 = (bf16[36,8,1152]{2,1,0:T(8,128)(2,1)S(1)}, bf16[36,8,1152]{2,1,0:T(8,128)(2,1)}, u32[]{:S(2)}, u32[]{:S(2)}) collective-permute-start(bf16[36,8,1152]{2,1,0:T(8,128)(2,1)S(1)} %pad_maximum_fusion.4.refs_0_), channel_id=1, source_target_pairs={{0,2},{1,5},{4,0},{5,9},{8,4},{9,13},{12,8},{13,15},{14,12},{15,11... | collective-permute-start | bytes 1990664 | tf_op jit(solution)/shard_map/ppermute | solution.py:208
  67.6 31.7 %collective-permute-start.20 = (bf16[72,8,1152]{2,1,0:T(8,128)(2,1)S(1)}, bf16[72,8,1152]{2,1,0:T(8,128)(2,1)}, u32[]{:S(2)}, u32[]{:S(2)}) collective-permute-start(bf16[72,8,1152]{2,1,0:T(8,128)(2,1)S(1)} %bitcast_dynamic-update-slice_fusion.1.refs_0_), channel_id=1, source_target_pairs={{0,4},{1,3},{4,8},{5,1},{8,12},{9,5},{12,14},{13,9},{14,10},{15,13... | collective-permute-start | bytes 3981320 | tf_op jit(solution)/shard_map/ppermute | solution.py:208
  69.7 29.6 %collective-permute-start.21 = (bf16[72,8,1152]{2,1,0:T(8,128)(2,1)S(1)}, bf16[72,8,1152]{2,1,0:T(8,128)(2,1)}, u32[]{:S(2)}, u32[]{:S(2)}) collective-permute-start(bf16[72,8,1152]{2,1,0:T(8,128)(2,1)S(1)} %bitcast_dynamic-update-slice_fusion.1.refs_0_), channel_id=1, source_target_pairs={{0,2},{1,5},{4,0},{5,9},{8,4},{9,13},{12,8},{13,15},{14,12},{15,11... | collective-permute-start | bytes 3981320 | tf_op jit(solution)/shard_map/ppermute | solution.py:208
  69.7 29.6 %collective-permute-start.22 = (bf16[72,8,1152]{2,1,0:T(8,128)(2,1)S(1)}, bf16[72,8,1152]{2,1,0:T(8,128)(2,1)S(1)}, u32[]{:S(2)}, u32[]{:S(2)}) collective-permute-start(bf16[72,8,1152]{2,1,0:T(8,128)(2,1)S(1)} %bitcast_dynamic-update-slice_fusion.1.refs_0_), channel_id=1, source_target_pairs={{0,1},{1,0},{2,3},{3,2},{4,5},{5,4},{6,7},{7,6},{8,9},{9,8},{10,11... | collective-permute-start | bytes 3981320 | tf_op jit(solution)/shard_map/ppermute | solution.py:174
  127.1 30.5 %collective-permute-start.27 = (bf16[72,8,1152]{2,1,0:T(8,128)(2,1)S(1)}, bf16[72,8,1152]{2,1,0:T(8,128)(2,1)S(1)}, u32[]{:S(2)}, u32[]{:S(2)}) collective-permute-start(bf16[72,8,1152]{2,1,0:T(8,128)(2,1)S(1)} %collective-permute-done.24.refs_2_), channel_id=1, source_target_pairs={{0,4},{1,3},{4,8},{5,1},{8,12},{9,5},{12,14},{13,9},{14,10},{15,13... | collective-permute-start | bytes 3981320 | tf_op jit(solution)/shard_map/ppermute | solution.py:208
  128.3 30.1 %collective-permute-start.28 = (bf16[72,8,1152]{2,1,0:T(8,128)(2,1)S(1)}, bf16[72,8,1152]{2,1,0:T(8,128)(2,1)S(1)}, u32[]{:S(2)}, u32[]{:S(2)}) collective-permute-start(bf16[72,8,1152]{2,1,0:T(8,128)(2,1)S(1)} %collective-permute-done.24.refs_2_), channel_id=1, source_target_pairs={{0,16},{16,0},{1,17},{17,1},{2,18},{18,2},{3,19},{19,3},{4,20},{20... | collective-permute-start | bytes 3981320 | tf_op jit(solution)/shard_map/ppermute | solution.py:178
  128.7 29.8 %collective-permute-start.29 = (bf16[72,8,1152]{2,1,0:T(8,128)(2,1)S(1)}, bf16[72,8,1152]{2,1,0:T(8,128)(2,1)S(1)}, u32[]{:S(2)}, u32[]{:S(2)}) collective-permute-start(bf16[72,8,1152]{2,1,0:T(8,128)(2,1)S(1)} %collective-permute-done.24.refs_2_), channel_id=1, source_target_pairs={{0,1},{1,0},{2,3},{3,2},{4,5},{5,4},{6,7},{7,6},{8,9},{9,8},{10,11... | collective-permute-start | bytes 3981320 | tf_op jit(solution)/shard_map/ppermute | solution.py:174
  129.1 33.5 %collective-permute-start.30 = (bf16[50,8,1024]{2,1,0:T(8,128)(2,1)S(1)}, bf16[50,8,1024]{2,1,0:T(8,128)(2,1)}, u32[]{:S(2)}, u32[]{:S(2)}) collective-permute-start(bf16[50,8,1024]{2,1,0:T(8,128)(2,1)S(1)} %pad_maximum_fusion.2.refs_0_), channel_id=1, source_target_pairs={{0,4},{1,3},{4,8},{5,1},{8,12},{9,5},{12,14},{13,9},{14,10},{15,13... | collective-permute-start | bytes 2457608 | tf_op jit(solution)/shard_map/ppermute | solution.py:208
  130.4 32.3 %collective-permute-start.31 = (bf16[50,8,1024]{2,1,0:T(8,128)(2,1)S(1)}, bf16[50,8,1024]{2,1,0:T(8,128)(2,1)}, u32[]{:S(2)}, u32[]{:S(2)}) collective-permute-start(bf16[50,8,1024]{2,1,0:T(8,128)(2,1)S(1)} %pad_maximum_fusion.2.refs_0_), channel_id=1, source_target_pairs={{0,2},{1,5},{4,0},{5,9},{8,4},{9,13},{12,8},{13,15},{14,12},{15,11... | collective-permute-start | bytes 2457608 | tf_op jit(solution)/shard_map/ppermute | solution.py:208
  158.6 31.1 %collective-permute-start.34 = (bf16[72,8,1152]{2,1,0:T(8,128)(2,1)S(1)}, bf16[72,8,1152]{2,1,0:T(8,128)(2,1)}, u32[]{:S(2)}, u32[]{:S(2)}) collective-permute-start(bf16[72,8,1152]{2,1,0:T(8,128)(2,1)S(1)} %collective-permute-done.27.refs_3_), channel_id=1, source_target_pairs={{0,16},{16,0},{1,17},{17,1},{2,18},{18,2},{3,19},{19,3},{4,20},{20... | collective-permute-start | bytes 3981320 | tf_op jit(solution)/shard_map/ppermute | solution.py:178
  160.4 29.3 %collective-permute-start.36 = (bf16[72,8,1152]{2,1,0:T(8,128)(2,1)S(1)}, bf16[72,8,1152]{2,1,0:T(8,128)(2,1)S(1)}, u32[]{:S(2)}, u32[]{:S(2)}) collective-permute-start(bf16[72,8,1152]{2,1,0:T(8,128)(2,1)S(1)} %collective-permute-done.28.refs_6_), channel_id=1, source_target_pairs={{0,1},{1,0},{2,3},{3,2},{4,5},{5,4},{6,7},{7,6},{8,9},{9,8},{10,11... | collective-permute-start | bytes 3981320 | tf_op jit(solution)/shard_map/ppermute | solution.py:174
  206.3 175.2 %reduce-scatter.4.cloned.1.call-start = ((), (), s32[]{:S(2)}) async-start(), calls=%async_computation.4 | async-start | bytes 3342336 | tf_op jit(solution)/shard_map/reduce_scatter | solution.py:422
  254.8 151.3 %collective-permute-start.57 = (bf16[512,1152]{1,0:T(8,128)(2,1)}, bf16[512,1152]{1,0:T(8,128)(2,1)}, u32[]{:S(2)}, u32[]{:S(2)}) collective-permute-start(bf16[512,1152]{1,0:T(8,128)(2,1)} %add_convert_fusion.7.mine_ref), channel_id=1, source_target_pairs={{0,1},{1,0},{2,3},{3,2},{4,5},{5,4},{6,7},{7,6},{8,9},{9,8},{10,11... | collective-permute-start | bytes 3538952 | tf_op jit(solution)/shard_map/ppermute | solution.py:174
  255.3 105.2 %collective-permute-start.54 = (bf16[512,4608]{1,0:T(8,128)(2,1)}, bf16[512,4608]{1,0:T(8,128)(2,1)}, u32[]{:S(2)}, u32[]{:S(2)}) collective-permute-start(bf16[512,4608]{1,0:T(8,128)(2,1)} %get-tuple-element.351.mine_ref), channel_id=1, source_target_pairs={{0,1},{1,0},{2,3},{3,2},{4,5},{5,4},{6,7},{7,6},{8,9},{9,8},{10,11... | collective-permute-start | bytes 14155784 | tf_op jit(solution)/shard_map/ppermute | solution.py:174
  304.7 223.1 %reduce-scatter.6.cloned.1.call-start = ((), (), s32[]{:S(2)}) async-start(), calls=%async_computation.5 | async-start | bytes 8912896 | tf_op jit(solution)/shard_map/reduce_scatter | solution.py:422
  343.7 257.3 %reduce-scatter.8.cloned.1.call-start = ((), (), s32[]{:S(2)}) async-start(), calls=%async_computation.6 | async-start | bytes 5013504 | tf_op jit(solution)/shard_map/reduce_scatter | solution.py:422
  403.7 29.3 %collective-permute-start.60 = (bf16[576,1152]{1,0:T(8,128)(2,1)}, bf16[576,1152]{1,0:T(8,128)(2,1)S(1)}, u32[]{:S(2)}, u32[]{:S(2)}) collective-permute-start(bf16[576,1152]{1,0:T(8,128)(2,1)} %add_convert_fusion.5), channel_id=1, source_target_pairs={{0,4},{1,3},{4,8},{5,1},{8,12},{9,5},{12,14},{13,9},{14,10},{15,13... | collective-permute-start | bytes 3981320 | tf_op jit(solution)/shard_map/ppermute | solution.py:494
  435.1 55.7 %collective-permute-start.62 = (bf16[576,1152]{1,0:T(8,128)(2,1)}, bf16[576,1152]{1,0:T(8,128)(2,1)S(1)}, u32[]{:S(2)}, u32[]{:S(2)}) collective-permute-start(bf16[576,1152]{1,0:T(8,128)(2,1)} %add_convert_fusion.4), channel_id=1, source_target_pairs={{0,4},{1,3},{4,8},{5,1},{8,12},{9,5},{12,14},{13,9},{14,10},{15,13... | collective-permute-start | bytes 3981320 | tf_op jit(solution)/shard_map/ppermute | solution.py:494
  448.6 42.2 %collective-permute-start.63 = (bf16[72,4608]{1,0:T(8,128)(2,1)S(1)}, bf16[72,4608]{1,0:T(8,128)(2,1)S(1)}, u32[]{:S(2)}, u32[]{:S(2)}) collective-permute-start(bf16[72,4608]{1,0:T(8,128)(2,1)S(1)} %get-tuple-element.400), channel_id=1, source_target_pairs={{0,4},{1,3},{4,8},{5,1},{8,12},{9,5},{12,14},{13,9},{14,10},{15,13... | collective-permute-start | bytes 1990664 | tf_op jit(solution)/shard_map/ppermute | solution.py:494
  504.1 33.5 %collective-permute-start.69 = (bf16[72,1152]{1,0:T(8,128)(2,1)}, bf16[72,1152]{1,0:T(8,128)(2,1)}, u32[]{:S(2)}, u32[]{:S(2)}) collective-permute-start(bf16[72,1152]{1,0:T(8,128)(2,1)} %copy-done.33), channel_id=1, source_target_pairs={{0,4},{1,3},{4,8},{5,1},{8,12},{9,5},{12,14},{13,9},{14,10},{15,13... | collective-permute-start | bytes 497672 | tf_op jit(solution)/shard_map/ppermute | solution.py:494
  504.2 33.4 %collective-permute-start.67 = (bf16[576,1152]{1,0:T(8,128)(2,1)}, bf16[576,1152]{1,0:T(8,128)(2,1)}, u32[]{:S(2)}, u32[]{:S(2)}) collective-permute-start(bf16[576,1152]{1,0:T(8,128)(2,1)} %add_convert_fusion.3), channel_id=1, source_target_pairs={{0,4},{1,3},{4,8},{5,1},{8,12},{9,5},{12,14},{13,9},{14,10},{15,13... | collective-permute-start | bytes 3981320 | tf_op jit(solution)/shard_map/ppermute | solution.py:494
  504.3 44.9 %collective-permute-start.68 = (bf16[144,4608]{1,0:T(8,128)(2,1)}, bf16[144,4608]{1,0:T(8,128)(2,1)}, u32[]{:S(2)}, u32[]{:S(2)}) collective-permute-start(bf16[144,4608]{1,0:T(8,128)(2,1)} %add_convert_fusion.2), channel_id=1, source_target_pairs={{0,4},{1,3},{4,8},{5,1},{8,12},{9,5},{12,14},{13,9},{14,10},{15,13... | collective-permute-start | bytes 3981320 | tf_op jit(solution)/shard_map/ppermute | solution.py:494
  558.0 34.5 %collective-permute-start.75 = (bf16[144,4608]{1,0:T(8,128)(2,1)}, bf16[144,4608]{1,0:T(8,128)(2,1)}, u32[]{:S(2)}, u32[]{:S(2)}) collective-permute-start(bf16[144,4608]{1,0:T(8,128)(2,1)} %add_convert_fusion.1), channel_id=1, source_target_pairs={{0,4},{1,3},{4,8},{5,1},{8,12},{9,5},{12,14},{13,9},{14,10},{15,13... | collective-permute-start | bytes 3981320 | tf_op jit(solution)/shard_map/ppermute | solution.py:494
  (185 other events, 2469.7 us)
Sparse Core Ops, SparseCore 0:
  206.4 48.5 all-gather.1
  304.8 67.3 reduce-scatter.3
  376.3 120.4 reduce-scatter.5
  503.9 81.0 reduce-scatter.7
